TPU v7x, 256 devices: a whole 4x4x8 slice. The times are simulated.
256 devices in a mesh: tile: 16 (over z, core), blk: 16 (over y, x).
Axes of the slice: x: 4, y: 4, z: 8, core: 2. Of those that a mesh axis runs over, the one named last changes fastest.
Arguments:
- spectra: float32 [4096, 3, 2, 2048], P(('tile', 'blk')), may hold values from -200 to 200
- send_rows: int32 [256, 16, 2], P(('tile', 'blk')), may hold values from 0 to 15
- send_counts: int32 [256, 16], P(('tile', 'blk')), may hold values from 1 to 2, as said below
- pair_rows: int32 [2, 65536], P(None, ('tile', 'blk')), may hold values from 0 to 511, as said below
- pair_counts: int32 [256], P(('tile', 'blk')), may hold values from 32 to 256, as said below
Outputs:
- stacks: bfloat16 [129, 9, 65536], P(None, None, ('tile', 'blk'))
Inputs may be any that keep to these rules, and one draw needn't show every extreme that they name: `send_counts`: each entry counts the live slots of one list; some entry equals 2 in every draw. `pair_rows`: every entry of pair p, owned by device d = p // 256, is d2 * 2 + s with s < send_counts[d2, d mod 16], a live row of the panel of its owner's column. `pair_counts`: some device has all 256 pairs live in every draw.
All inputs are finite; a program needn't handle non-finite values.
Results may differ from a plain program's by a relative error of at most 0.0067.
Values may be sent and summed in bfloat16 or wider, within the bound.
A program may use at most 128 MiB of HBM per device.

v0:
```python
import math

import jax
import jax.numpy as jnp
from jax import lax
from jax.sharding import PartitionSpec as P

LAGS = 129


def whiten(spectra):
    station_count = spectra.shape[0]
    bin_count = spectra.shape[-1]
    ramp_bins = bin_count // 32
    bin_index = jnp.arange(bin_count, dtype=jnp.int32)
    edge_dist = jnp.minimum(bin_index, bin_count - 1 - bin_index).astype(jnp.float32) + 0.5
    ramp_vals = 0.5 - 0.5 * jnp.cos(jnp.pi * edge_dist / ramp_bins)
    taper = jnp.where(edge_dist < ramp_bins, ramp_vals, jnp.ones_like(ramp_vals))
    blocked = spectra.reshape(station_count, 3, 2, bin_count // 64, 64)
    power = jnp.mean(blocked * blocked, axis=(1, 2, 4))
    inverse = 1.0 / jnp.sqrt(power + 1e-05)
    spread_scale = jnp.repeat(inverse, 64, axis=1)
    return (spectra * taper * spread_scale[:, None, None, :]).astype(jnp.bfloat16)


def lag_halves(lag_count, bin_count):
    lag_index = jnp.arange(lag_count, dtype=jnp.int32) - lag_count // 2
    bin_index = jnp.arange(bin_count, dtype=jnp.int32)
    phase_steps = lag_index[:, None] * bin_index[None, :] % (2 * bin_count)
    angle = phase_steps.astype(jnp.float32) * (jnp.pi / bin_count)
    return (jnp.cos(angle).astype(jnp.bfloat16), (-jnp.sin(angle)).astype(jnp.bfloat16))


def cross_parts(first_rows, second_rows):
    pair_total = first_rows.shape[0]
    bin_count = first_rows.shape[-1]
    left_re = first_rows[:, :, 0, :].astype(jnp.float32)[:, :, None, :]
    left_im = first_rows[:, :, 1, :].astype(jnp.float32)[:, :, None, :]
    right_re = second_rows[:, :, 0, :].astype(jnp.float32)[:, None, :, :]
    right_im = second_rows[:, :, 1, :].astype(jnp.float32)[:, None, :, :]
    real_part = (left_re * right_re + left_im * right_im).astype(jnp.bfloat16)
    imag_part = (left_im * right_re - left_re * right_im).astype(jnp.bfloat16)
    return (
        real_part.reshape(pair_total, 9, bin_count),
        imag_part.reshape(pair_total, 9, bin_count),
    )


def shards(spectra, send_rows, send_counts, pair_rows, pair_counts):
    whitened = whiten(spectra)
    bin_count = spectra.shape[-1]
    station_count = spectra.shape[0]
    slot_count = send_rows.shape[2]
    blk_count = lax.axis_size("blk")
    tile_count = lax.axis_size("tile")
    slot_index = jnp.arange(slot_count, dtype=jnp.int32)
    pool, lists, counts = (
        lax.all_gather(whitened, "tile", axis=0, tiled=True),
        lax.all_gather(send_rows, "tile", axis=0, tiled=True),
        lax.all_gather(send_counts, "tile", axis=0, tiled=True),
    )
    tile_offsets = jnp.arange(tile_count, dtype=jnp.int32) * station_count
    station_ids = jnp.transpose(tile_offsets[:, None, None] + lists, (1, 0, 2))
    alive_slot = jnp.transpose(slot_index[None, None, :] < counts[:, :, None], (1, 0, 2))
    flat_pool = pool.reshape(-1, 6 * bin_count)
    picked = jnp.take(flat_pool, station_ids, axis=0)
    picked = jnp.where(alive_slot[:, :, :, None], picked, jnp.zeros_like(picked))
    received = lax.all_to_all(picked, "blk", split_axis=0, concat_axis=0, tiled=True)
    row_panel = received.reshape(-1, 6 * bin_count)

    def remap(canonical):
        source = canonical // slot_count
        slot_id = canonical % slot_count
        tile_id = source // blk_count
        blk_id = source % blk_count
        return (blk_id * tile_count + tile_id) * slot_count + slot_id

    left_index = remap(pair_rows[0])
    right_index = remap(pair_rows[1])
    pair_total = pair_rows.shape[1]
    block_rows = min(512, pair_total)
    cos_rows, sin_rows = lag_halves(LAGS, bin_count)
    live_pairs = pair_counts[0]
    block_count = (live_pairs + block_rows - 1) // block_rows
    scale_factor = 1.0 / math.sqrt(bin_count)

    def step(block_id, stacks):
        offset = block_id * block_rows
        first_rows = jnp.take(row_panel, left_index, axis=0)
        second_rows = jnp.take(row_panel, right_index, axis=0)
        first_rows = first_rows.reshape(block_rows, 3, 2, bin_count)
        second_rows = second_rows.reshape(block_rows, 3, 2, bin_count)
        real_part, imag_part = cross_parts(first_rows, second_rows)
        lag_sums = jnp.einsum(
            "lf,pcf->lcp", cos_rows, real_part, preferred_element_type=jnp.float32
        )
        lag_sums = lag_sums + jnp.einsum(
            "lf,pcf->lcp", sin_rows, imag_part, preferred_element_type=jnp.float32
        )
        lag_sums = lag_sums * scale_factor
        pair_ids = offset + jnp.arange(block_rows, dtype=jnp.int32)
        lag_sums = jnp.where((pair_ids < live_pairs)[None, None, :], lag_sums, 0.0).astype(
            jnp.bfloat16
        )
        return lag_sums

    initial = jnp.zeros((LAGS, 9, pair_total), jnp.bfloat16)
    return lax.fori_loop(0, block_count, step, initial)


def solution(mesh):
    return jax.shard_map(
        shards,
        mesh=mesh,
        in_specs=(
            P(("tile", "blk"), None, None, None),
            P(("tile", "blk"), None, None),
            P(("tile", "blk"), None),
            P(None, ("tile", "blk")),
            P(("tile", "blk")),
        ),
        out_specs=P(None, None, ("tile", "blk")),
        check_vma=False,
    )
```

profile of v0, /device:TPU:1, one launch (start us, length us, event | category | flops | bytes accessed | tf_op | source)
XLA Modules:
  0.0 543.8 jit_solution(12361057580870116507)
XLA Ops:
  6.5 0.0 all-gather.3.cloned.1.call-start
  6.5 0.1 subtract_select_fusion
  6.6 1.7 multiply_reduce_fusion
  8.3 0.1 reduce_sum.14
  8.4 0.1 reduce_sum.18
  8.6 0.1 broadcast_in_dim.82
  8.7 0.1 mul.189
  8.8 2.2 multiply_convert_fusion
  11.1 0.0 all-gather.3.cloned.1.call-update
  11.1 21.6 %all_gather.10 = s32[16,16,2]{1,2,0:T(2,128)S(1)} all-gather(s32[1,16,2]{1,2,0:T(2,128)} %param.10), channel_id=1, replica_groups=mesh['tile'=16,'blk'=16] {'tile'}, dimensions={0}, use_global_device_ids=true | all-gather | bytes 2176 | tf_op jit(solution)/shard_map/all_gather | solution.py:59
  32.6 0.1 compare_and_fusion
  32.7 0.2 copy.34
  32.9 0.1 reshape.152
  33.1 0.2 copy.33
  33.3 14.5 %all-gather = s32[16,1,16]{2,1,0:T(1,128)S(1)} all-gather(s32[1,1,16]{2,1,0:T(1,128)} %bitcast.50), channel_id=1, replica_groups=mesh['tile'=16,'blk'=16] {'tile'}, dimensions={0}, use_global_device_ids=true | all-gather | bytes 1088 | tf_op jit(solution)/shard_map/all_gather | solution.py:60
  47.8 0.1 copy.32
  47.8 0.1 iota_compare_fusion
  47.9 13.6 %all-gather.3.cloned.1.call-done = bf16[256,3,2,2048]{3,2,1,0:T(2,128)(2,1)} async-done(((bf16[16,3,2,2048]{3,2,1,0:T(2,128)(2,1)}), bf16[256,3,2,2048]{3,2,1,0:T(2,128)(2,1)}) %all-gather.3.cloned.1.call-update) | async-done | bytes 6291472 | tf_op jit(solution)/shard_map/all_gather | solution.py:58
  61.5 14.4 %reshape.126 = bf16[256,12288]{1,0:T(8,128)(2,1)} reshape(bf16[256,3,2,2048]{3,2,1,0:T(2,128)(2,1)} %all-gather.3.cloned.1.call-done) | data formatting | bytes 12582912 | tf_op jit(solution)/shard_map/reshape | solution.py:65
  76.0 26.5 %gather_fusion = bf16[512,12288]{1,0:T(8,128)(2,1)} fusion(bf16[256,12288]{1,0:T(8,128)(2,1)} %reshape.126, s32[1024]{0:T(1024)S(1)} %pad_clamp_fusion.2), kind=kCustom, calls=%fused_computation.2 | custom fusion | bytes 25167872 | tf_op jit(solution)/shard_map/jit(_take)/gather | solution.py:66
  102.4 24.0 %reshape.151 = bf16[16,16,2,12288]{3,2,1,0:T(2,128)(2,1)} reshape(bf16[512,12288]{1,0:T(8,128)(2,1)} %gather_fusion) | data formatting | bytes 25165824 | tf_op jit(solution)/shard_map/jit(_take)/gather | solution.py:66
  126.5 20.1 %broadcast_select_fusion.1 = bf16[16,16,2,12288]{3,2,1,0:T(2,128)(2,1)} fusion(pred[16,16,2]{2,1,0:T(8,128)(4,1)S(1)} %iota_compare_fusion, bf16[16,16,2,12288]{3,2,1,0:T(2,128)(2,1)} %reshape.151, pred[16,16,2]{2,1,0:T(8,128)(4,1)S(1)} %copy.33), kind=kLoop, calls=%fused_computation.6 | loop fusion | flops 12582912 | bytes 25166848 | tf_op jit(solution)/shard_map/jit(_where)/select_n | solution.py:67
  146.5 6.7 %all-to-all-start = ((bf16[16,16,2,12288]{3,2,1,0:T(2,128)(2,1)}), bf16[16,16,2,12288]{3,2,1,0:T(2,128)(2,1)}, u32[]{:S(2)}, u32[]{:S(2)}) async-start(bf16[16,16,2,12288]{3,2,1,0:T(2,128)(2,1)} %broadcast_select_fusion.1), calls=%async_computation | async-start | bytes 25165824 | tf_op jit(solution)/shard_map/all_to_all | solution.py:68
  153.9 0.0 copy-done.1
  154.0 187.2 %all-to-all-done = bf16[16,16,2,12288]{3,2,1,0:T(2,128)(2,1)} async-done(((bf16[16,16,2,12288]{3,2,1,0:T(2,128)(2,1)}), bf16[16,16,2,12288]{3,2,1,0:T(2,128)(2,1)}, u32[]{:S(2)}, u32[]{:S(2)}) %all-to-all-start) | async-done | bytes 12582944 | tf_op jit(solution)/shard_map/all_to_all | solution.py:68
  341.2 25.1 %reshape.127 = bf16[512,12288]{1,0:T(8,128)(2,1)} reshape(bf16[16,16,2,12288]{3,2,1,0:T(2,128)(2,1)} %all-to-all-done) | data formatting | bytes 25165824 | tf_op jit(solution)/shard_map/reshape | solution.py:69
  366.3 18.9 %gather_fusion.1 = bf16[256,12288]{1,0:T(8,128)(2,1)} fusion(bf16[512,12288]{1,0:T(8,128)(2,1)} %reshape.127, s32[1024]{0:T(1024)S(1)} %pad_clamp_fusion.1), kind=kCustom, calls=%fused_computation.clone | custom fusion | bytes 12583936 | tf_op jit(solution)/shard_map/while/body/jit(_take)/gather | solution.py:89
  385.2 6.4 %broadcast_select_fusion.3 = bf16[256,12288]{1,0:T(8,128)(2,1)} fusion(bf16[256,12288]{1,0:T(8,128)(2,1)} %gather_fusion.1, pred[256]{0:T(512)(128)(4,1)S(1)} %get-tuple-element.226), kind=kLoop, calls=%fused_computation.10 | loop fusion | flops 3145728 | bytes 12583168 | tf_op jit(solution)/shard_map/while/body/jit(_take)/select_n | solution.py:89
  391.7 14.5 %reshape.128 = bf16[256,3,2,2048]{3,2,1,0:T(2,128)(2,1)} reshape(bf16[256,12288]{1,0:T(8,128)(2,1)} %broadcast_select_fusion.3) | data formatting | bytes 12582912 | tf_op jit(solution)/shard_map/while/body/reshape | solution.py:91
  406.2 13.7 %fusion.35 = (bf16[256,3,1,2048]{3,2,1,0:T(2,128)(2,1)}, bf16[256,3,1,2048]{3,2,1,0:T(2,128)(2,1)}) fusion(bf16[256,3,2,2048]{3,2,1,0:T(2,128)(2,1)} %reshape.128), kind=kLoop, calls=%fused_computation.89 | loop fusion | bytes 12582912 | tf_op jit(solution)/shard_map/while/body/slice | solution.py:37
  419.9 19.0 %gather_fusion.2 = bf16[256,12288]{1,0:T(8,128)(2,1)} fusion(bf16[512,12288]{1,0:T(8,128)(2,1)} %reshape.127, s32[1024]{0:T(1024)S(1)} %pad_clamp_fusion), kind=kCustom, calls=%fused_computation.1.clone | custom fusion | bytes 12583936 | tf_op jit(solution)/shard_map/while/body/jit(_take)/gather | solution.py:90
  438.9 6.3 %broadcast_select_fusion.2 = bf16[256,12288]{1,0:T(8,128)(2,1)} fusion(bf16[256,12288]{1,0:T(8,128)(2,1)} %gather_fusion.2, pred[256]{0:T(512)(128)(4,1)S(1)} %get-tuple-element.228), kind=kLoop, calls=%fused_computation.9 | loop fusion | flops 3145728 | bytes 12583168 | tf_op jit(solution)/shard_map/while/body/jit(_take)/select_n | solution.py:90
  445.3 14.7 %reshape.129 = bf16[256,3,2,2048]{3,2,1,0:T(2,128)(2,1)} reshape(bf16[256,12288]{1,0:T(8,128)(2,1)} %broadcast_select_fusion.2) | data formatting | bytes 12582912 | tf_op jit(solution)/shard_map/while/body/reshape | solution.py:92
  459.9 13.8 %fusion.36 = (bf16[256,3,1,2048]{3,2,1,0:T(2,128)(2,1)}, bf16[256,3,1,2048]{3,2,1,0:T(2,128)(2,1)}) fusion(bf16[256,3,2,2048]{3,2,1,0:T(2,128)(2,1)} %reshape.129), kind=kLoop, calls=%fused_computation.90 | loop fusion | bytes 12582912 | tf_op jit(solution)/shard_map/while/body/slice | solution.py:39
  473.8 0.0 slice-done
  473.8 0.0 slice-done.1
  473.8 13.7 %fusion.1 = (f32[256,3,2048]{2,0,1:T(8,128)}, f32[256,3,2048]{2,0,1:T(8,128)}) fusion(bf16[256,3,1,2048]{3,2,1,0:T(2,128)(2,1)} %get-tuple-element.235, bf16[256,3,1,2048]{3,2,1,0:T(2,128)(2,1)S(1)} %bitcast.44), kind=kLoop, calls=%fused_computation.14 | loop fusion | flops 3145728 | bytes 18874368 | tf_op jit(solution)/shard_map/while/body/mul | solution.py:41
  487.5 15.9 %fusion = (f32[256,3,2048]{2,0,1:T(8,128)}, f32[256,3,2048]{2,0,1:T(8,128)}) fusion(bf16[256,3,1,2048]{3,2,1,0:T(2,128)(2,1)} %get-tuple-element.237, bf16[256,3,1,2048]{3,2,1,0:T(2,128)(2,1)} %get-tuple-element.236), kind=kLoop, calls=%fused_computation.12 | loop fusion | flops 3145728 | bytes 18874368 | tf_op jit(solution)/shard_map/while/body/convert_element_type | solution.py:40
  503.4 0.0 copy-done
  503.4 11.8 %subtract_convert_fusion = (bf16[256,3,3,2048]{3,0,2,1:T(8,128)(2,1)S(1)}, bf16[256,3,3,2048]{3,0,2,1:T(8,128)(2,1)}) fusion(f32[256,3,2048]{2,0,1:T(8,128)} %get-tuple-element.240, f32[256,3,2048]{2,0,1:T(8,128)S(1)} %copy-done, f32[256,3,2048]{2,0,1:T(8,128)} %get-tuple-element.241, f32[256,3,2048]{2,0,1:T(8,128)} %get-tuple-element.243), kind=kLoop, calls=%fused_computation.7 | loop fusion | flops 37748736 | bytes 44040192 | tf_op jit(solution)/shard_map/while/body/convert_element_type | solution.py:42
  515.1 9.2 %fusion.12 = f32[256,9,129]{0,2,1:T(8,128)S(1)} fusion(bf16[256,9,2048]{2,0,1:T(8,128)(2,1)} %bitcast.46, s32[129]{0:T(256)S(1)} %iota_add_fusion), kind=kOutput, calls=%fused_computation.35 | convolution fusion | flops 1221359616 | bytes 10626564 | tf_op jit(solution)/shard_map/while/body/lf,pcf->lcp/dot_general | solution.py:94
  524.3 6.7 %fusion.4 = f32[129,9,256]{2,0,1:T(8,128)S(1)} fusion(f32[256,9,129]{0,2,1:T(8,128)S(1)} %fusion.12, bf16[256,9,2048]{2,0,1:T(8,128)(2,1)S(1)} %bitcast.45, s32[129]{0:T(256)S(1)} %iota_add_fusion), kind=kOutput, calls=%fused_computation.23 | convolution fusion | flops 1221921024 | bytes 11815428 | tf_op jit(solution)/shard_map/while/body/lf,pcf->lcp/dot_general | solution.py:97
  531.0 0.5 copy.39
  531.5 1.1 broadcast_in_dim.78
  532.6 1.9 while.16
  532.6 0.7 add_compare_fusion.2
  533.2 1.3 select_convert_fusion.2
  534.5 2.3 copy.40
  (14 shorter events, 0.1 us)
Async XLA Ops:
  6.5 55.0 %all-gather.3.cloned.1.call-start = ((), (), s32[]{:S(2)}) async-start(), calls=%async_computation.1 | async-start | bytes 6684672 | tf_op jit(solution)/shard_map/all_gather | solution.py:58
  146.5 7.4 %copy-start.1 = (s32[2,256]{1,0:T(2,128)S(1)}, s32[2,256]{1,0:T(2,128)}, u32[]{:S(2)}) copy-start(s32[2,256]{1,0:T(2,128)} %param.12) | copy-start | bytes 6148
  146.5 194.7 %all-to-all-start = ((bf16[16,16,2,12288]{3,2,1,0:T(2,128)(2,1)}), bf16[16,16,2,12288]{3,2,1,0:T(2,128)(2,1)}, u32[]{:S(2)}, u32[]{:S(2)}) async-start(bf16[16,16,2,12288]{3,2,1,0:T(2,128)(2,1)} %broadcast_select_fusion.1), calls=%async_computation | async-start | bytes 25165824 | tf_op jit(solution)/shard_map/all_to_all | solution.py:68
  445.3 28.5 %slice-start = ((s8[6291456]{0:T(1024)(128)(4,1)}), s8[2097152]{0:T(1024)(128)(4,1)S(1)}, s32[]{:S(2)}) async-start(s8[6291456]{0:T(1024)(128)(4,1)} %bitcast.43), calls=%async_computation.2 | async-start | bytes 4194304
  459.9 13.8 %slice-start.1 = ((s8[6291456]{0:T(1024)(128)(4,1)}), s8[4194304]{0:T(1024)(128)(4,1)S(1)}, s32[]{:S(2)}) async-start(s8[6291456]{0:T(1024)(128)(4,1)} %bitcast.43), calls=%async_computation.3 | async-start | bytes 8388608
  487.5 15.9 %copy-start = (f32[256,3,2048]{2,0,1:T(8,128)S(1)}, f32[256,3,2048]{2,0,1:T(8,128)}, u32[]{:S(2)}) copy-start(f32[256,3,2048]{2,0,1:T(8,128)} %get-tuple-element.242) | copy-start | bytes 18874372
Sparse Core Ops, SparseCore 0:
  11.2 50.2 all-gather.2
where the time goes:
time: 551 us; the launch traced here: 544 us
  waiting for transfers between devices  201 us (36%)
  local copies, waits for them, and re-layouts  189 us (34%)
  other arithmetic  80.5 us (15%)
  blocking collectives  36.1 us (7%)
  matrix products  15.9 us (3%)
  between operations  14.5 us (3%)
  starting transfers between devices  6.71 us (1%)
    all_to_all x1, waiting for transfers between devices, shards(): lax.all_to_all(picked, 'blk', split_axis=0, concat_axis=0, tiled=True)  187 us
    gather x2, local copies, waits for them, and re-layouts, shards(): picked = jnp.take(flat_pool, station_ids, axis=0)  50.5 us
    reshape x1, local copies, waits for them, and re-layouts, shards(): row_panel = received.reshape(-1, 6 * bin_count)  25.1 us
    all_gather x1, blocking collectives, shards(): lax.all_gather(send_rows, 'tile', axis=0, tiled=True)  21.6 us
    select_n x1, other arithmetic, shards(): jnp.where(alive_slot[:, :, :, None], picked, jnp.zeros_like(picked))  20.1 us
    gather x1, local copies, waits for them, and re-layouts, step(): second_rows = jnp.take(row_panel, right_index, axis=0)  19 us
    gather x1, local copies, waits for them, and re-layouts, step(): first_rows = jnp.take(row_panel, left_index, axis=0)  18.9 us
    convert_element_type x1, other arithmetic, cross_parts(): right_im = second_rows[:, :, 1, :].astype(jnp.float32)[:, None, :, :]  15.9 us
  transfers between devices with their start and end apart: 2, of which 2 were waited for; matrix products, arithmetic and copies ran while one was open for 0% of the time, Pallas kernels for 0%

commit v1 on v0

v1 whole, which is shorter than its diff:
```python
import functools
import math

import jax
import jax.numpy as jnp
from jax import lax
from jax.experimental import pallas as pl
from jax.experimental.pallas import tpu as pltpu
from jax.sharding import Mesh
from jax.sharding import PartitionSpec as P

LAGS = 129
LAG_ROWS = 144
PAIR_BLOCK = 128
BIN_CHUNK = 256
GATHER_CHUNK = 512


def whiten(spectra):
    station_count = spectra.shape[0]
    bin_count = spectra.shape[-1]
    ramp_bins = bin_count // 32
    bin_index = jnp.arange(bin_count, dtype=jnp.int32)
    edge_dist = jnp.minimum(bin_index, bin_count - 1 - bin_index).astype(jnp.float32) + 0.5
    ramp_vals = 0.5 - 0.5 * jnp.cos(jnp.pi * edge_dist / ramp_bins)
    taper = jnp.where(edge_dist < ramp_bins, ramp_vals, jnp.ones_like(ramp_vals))
    blocked = spectra.reshape(station_count, 3, 2, bin_count // 64, 64)
    power = jnp.mean(blocked * blocked, axis=(1, 2, 4))
    inverse = 1.0 / jnp.sqrt(power + 1e-05)
    spread_scale = jnp.repeat(inverse, 64, axis=1)
    return (spectra * taper * spread_scale[:, None, None, :]).astype(jnp.bfloat16)


def lag_part(bin_count, first_bin, part_bins):
    lag_index = jnp.arange(LAGS, dtype=jnp.int32) - LAGS // 2
    bin_index = first_bin + jnp.arange(part_bins, dtype=jnp.int32)
    phase_steps = lag_index[:, None] * bin_index[None, :] % (2 * bin_count)
    angle = phase_steps.astype(jnp.float32) * (jnp.pi / bin_count)
    pad = ((0, LAG_ROWS - LAGS), (0, 0))
    cos_rows = jnp.pad(jnp.cos(angle).astype(jnp.bfloat16), pad)
    sin_rows = jnp.pad((-jnp.sin(angle)).astype(jnp.bfloat16), pad)
    return cos_rows, sin_rows


def pair_kernel(counts_ref, first_ref, second_ref, panel_ref, cos_ref, sin_ref, out_ref,
                f_scr, s_scr, *, blocks_per_owner, part_bins):
    step = pl.program_id(0)
    owner = step // blocks_per_owner
    start = (step % blocks_per_owner) * PAIR_BLOCK
    live = start < counts_ref[owner]

    @pl.when(jnp.logical_not(live))
    def _():
        out_ref[...] = jnp.zeros_like(out_ref)

    @pl.when(live)
    def _():
        rows = panel_ref.shape[0]
        width = panel_ref.shape[1]
        iota = lax.broadcasted_iota(jnp.int32, (PAIR_BLOCK, rows), 1)
        pick_first = (first_ref[...] == iota).astype(jnp.bfloat16)
        pick_second = (second_ref[...] == iota).astype(jnp.bfloat16)

        def gather(c, carry):
            off = pl.multiple_of(c * GATHER_CHUNK, GATHER_CHUNK)
            block = panel_ref[:, pl.ds(off, GATHER_CHUNK)]
            f_scr[:, pl.ds(off, GATHER_CHUNK)] = jnp.dot(
                pick_first, block, preferred_element_type=jnp.float32)
            s_scr[:, pl.ds(off, GATHER_CHUNK)] = jnp.dot(
                pick_second, block, preferred_element_type=jnp.float32)
            return carry

        lax.fori_loop(0, width // GATHER_CHUNK, gather, 0)
        out_ref[...] = jnp.zeros_like(out_ref)
        nt = (((1,), (1,)), ((), ()))

        def chunk(kc, carry):
            off = pl.multiple_of(kc * BIN_CHUNK, BIN_CHUNK)
            cos_blk = cos_ref[:, pl.ds(off, BIN_CHUNK)]
            sin_blk = sin_ref[:, pl.ds(off, BIN_CHUNK)]
            for a in range(3):
                f_re = f_scr[:, pl.ds(2 * a * part_bins + off, BIN_CHUNK)]
                f_im = f_scr[:, pl.ds((2 * a + 1) * part_bins + off, BIN_CHUNK)]
                for b in range(3):
                    s_re = s_scr[:, pl.ds(2 * b * part_bins + off, BIN_CHUNK)]
                    s_im = s_scr[:, pl.ds((2 * b + 1) * part_bins + off, BIN_CHUNK)]
                    real_part = (f_re * s_re + f_im * s_im).astype(jnp.bfloat16)
                    imag_part = (f_im * s_re - f_re * s_im).astype(jnp.bfloat16)
                    acc = lax.dot_general(cos_blk, real_part, nt,
                                          preferred_element_type=jnp.float32)
                    acc = acc + lax.dot_general(sin_blk, imag_part, nt,
                                                preferred_element_type=jnp.float32)
                    out_ref[0, 3 * a + b] += acc
            return carry

        lax.fori_loop(0, part_bins // BIN_CHUNK, chunk, 0)


def pair_sums(counts, first_idx, second_idx, panel, cos_rows, sin_rows, owners):
    rows, width = panel.shape
    part_bins = width // 6
    pairs = first_idx.shape[0]
    per_owner = pairs // owners
    blocks_per_owner = per_owner // PAIR_BLOCK
    grid = (pairs // PAIR_BLOCK,)
    kernel = functools.partial(pair_kernel, blocks_per_owner=blocks_per_owner,
                               part_bins=part_bins)
    flops = 2 * pairs * rows * width * 2 + 2 * LAG_ROWS * 2 * part_bins * 9 * pairs
    cost = pl.CostEstimate(flops=flops, transcendentals=0,
                           bytes_accessed=rows * width * 2 + owners * 9 * LAG_ROWS * per_owner * 4)
    return pl.pallas_call(
        kernel,
        out_shape=jax.ShapeDtypeStruct((owners, 9, LAG_ROWS, per_owner), jnp.float32),
        grid_spec=pltpu.PrefetchScalarGridSpec(
            num_scalar_prefetch=1,
            grid=grid,
            in_specs=[
                pl.BlockSpec((PAIR_BLOCK, 1), lambda i, c: (i, 0)),
                pl.BlockSpec((PAIR_BLOCK, 1), lambda i, c: (i, 0)),
                pl.BlockSpec((rows, width), lambda i, c: (0, 0)),
                pl.BlockSpec((LAG_ROWS, part_bins), lambda i, c: (0, 0)),
                pl.BlockSpec((LAG_ROWS, part_bins), lambda i, c: (0, 0)),
            ],
            out_specs=pl.BlockSpec(
                (1, 9, LAG_ROWS, PAIR_BLOCK),
                lambda i, c: (i // blocks_per_owner, 0, 0, i % blocks_per_owner)),
            scratch_shapes=[
                pltpu.VMEM((PAIR_BLOCK, width), jnp.float32),
                pltpu.VMEM((PAIR_BLOCK, width), jnp.float32),
            ],
        ),
        compiler_params=pltpu.CompilerParams(
            dimension_semantics=("arbitrary",), vmem_limit_bytes=60 * 1024 * 1024),
        cost_estimate=cost,
    )(counts, first_idx, second_idx, panel, cos_rows, sin_rows)


def shards(spectra, send_rows, send_counts, pair_rows, pair_counts):
    whitened = whiten(spectra)
    station_count, comps, parts, bin_count = whitened.shape
    row_width = comps * parts * bin_count
    slot_count = send_rows.shape[2]
    cores = lax.axis_size("core")
    part_bins = bin_count // cores
    core = lax.axis_index("core")

    flat = whitened.reshape(station_count, row_width)
    lists = send_rows[0]
    col_count = lists.shape[0]
    picked = jnp.take(flat, lists.reshape(-1), axis=0).reshape(col_count, slot_count, row_width)
    alive = jnp.arange(slot_count, dtype=jnp.int32)[None, :] < send_counts[0][:, None]
    picked = jnp.where(alive[:, :, None], picked, jnp.zeros_like(picked))
    received = lax.all_to_all(picked, "blk", 0, 0, tiled=True)

    halves = received.reshape(col_count, slot_count, comps * parts, cores, part_bins)
    halves = jnp.transpose(halves, (3, 0, 1, 2, 4)).reshape(
        cores, col_count * slot_count, comps * parts * part_bins)
    mine = lax.all_to_all(halves, "core", 0, 0, tiled=True)
    mine = mine.reshape(cores * col_count * slot_count, comps * parts * part_bins)
    panel = lax.all_gather(mine, "z", axis=0, tiled=True)

    chip_pairs = lax.all_gather(pair_rows, "core", axis=1, tiled=True)
    chip_counts = lax.all_gather(pair_counts, "core", axis=0, tiled=True)
    cos_rows, sin_rows = lag_part(bin_count, core * part_bins, part_bins)
    partial = pair_sums(chip_counts, chip_pairs[0][:, None], chip_pairs[1][:, None],
                        panel, cos_rows, sin_rows, cores)
    partial = lax.all_to_all(partial, "core", 0, 0, tiled=True)
    total = jnp.sum(partial, axis=0)[:, :LAGS, :] * (1.0 / math.sqrt(bin_count))
    pair_total = pair_rows.shape[1]
    live = jnp.arange(pair_total, dtype=jnp.int32) < pair_counts[0]
    total = jnp.where(live[None, None, :], total, 0.0).astype(jnp.bfloat16)
    return jnp.transpose(total, (1, 0, 2))


def solution(mesh):
    tile_size = mesh.shape["tile"]
    blk_size = mesh.shape["blk"]
    split = Mesh(mesh.devices.reshape(tile_size // 2, 2, blk_size), ("z", "core", "blk"))
    dev = ("z", "core", "blk")
    return jax.shard_map(
        shards,
        mesh=split,
        in_specs=(
            P(dev, None, None, None),
            P(dev, None, None),
            P(dev, None),
            P(None, dev),
            P(dev),
        ),
        out_specs=P(None, None, dev),
        check_vma=False,
    )
```

time: 551 us -> 162 us (0.29)
  the two profiles are of different devices: /device:TPU:1 before, /device:TPU:69 now
where the time goes in v1:
time: 162 us; the launch traced here: 161 us
  waiting for transfers between devices  61.1 us (38%)
  blocking collectives  36.2 us (22%)
  Pallas kernels  29.7 us (18%)
  between operations  14.2 us (9%)
  other arithmetic  10.6 us (7%)
  local copies, waits for them, and re-layouts  9.6 us (6%)
    all_gather x1, waiting for transfers between devices, shards(): panel = lax.all_gather(mine, 'z', axis=0, tiled=True)  61.1 us
    pallas_call x1, Pallas kernels, pair_sums(): pl.pallas_call(kernel, out_shape=jax.ShapeDtypeStruct((owners, 9, LAG_ROW...  29.7 us
    all_to_all x1, blocking collectives, shards(): received = lax.all_to_all(picked, 'blk', 0, 0, tiled=True)  17.4 us
    all_to_all x1, blocking collectives, shards(): partial = lax.all_to_all(partial, 'core', 0, 0, tiled=True)  7.41 us
    all_to_all x1, blocking collectives, shards(): mine = lax.all_to_all(halves, 'core', 0, 0, tiled=True)  7.11 us
  transfers between devices with their start and end apart: 1, of which 1 were waited for; matrix products, arithmetic and copies ran while one was open for 4% of the time, Pallas kernels for 0%

profile of v1, /device:TPU:69, one launch (start us, length us, event | category | flops | bytes accessed | tf_op | source)
XLA Modules:
  0.0 161.3 jit_solution(9478981950522507179)
XLA Ops:
  6.5 0.0 copy-start
  6.5 0.0 all-gather.2.cloned.1.call-start
  6.5 0.8 compare_and_fusion
  7.3 0.8 copy.25
  8.1 0.1 subtract_select_fusion
  8.1 0.1 copy.24
  8.2 0.7 iota_compare_fusion
  8.9 0.1 reshape_squeeze.6
  9.1 1.7 %multiply_reduce_fusion = f32[16,2048]{1,0:T(8,128)S(1)} fusion(f32[16,3,2,2048]{3,2,1,0:T(2,128)} %param.5), kind=kLoop, calls=%fused_computation.12 | loop fusion | flops 360448 | bytes 917504 | tf_op jit(solution)/shard_map/reduce_sum | solution.py:28
  10.8 0.1 reduce_sum.26
  10.9 0.1 reduce_sum.27
  11.0 0.1 broadcast_in_dim.49
  11.1 0.1 mul.64
  11.3 0.0 copy-done
  11.3 0.4 multiply_convert_fusion
  11.7 0.3 reshape.106
  11.9 1.0 gather_fusion
  13.0 0.5 gather.7
  13.5 0.9 broadcast_select_fusion.1
  14.4 17.4 %all_to_all.15 = bf16[16,2,12288]{2,1,0:T(2,128)(2,1)S(1)} all-to-all(bf16[16,2,12288]{2,1,0:T(2,128)(2,1)S(1)} %broadcast_select_fusion.1), channel_id=1, replica_groups=mesh['z'=8,'core'=2,'blk'=16] {'blk'}, dimensions={0} | all-to-all | bytes 1572864 | tf_op jit(solution)/shard_map/all_to_all | solution.py:153
  31.8 0.6 reshape.123
  32.4 0.3 copy.27
  32.6 1.1 reshape.108
  33.7 0.0 copy-start.2
  33.7 0.0 copy-start.1
  33.7 7.1 %all_to_all.16 = bf16[2,32,6144]{2,1,0:T(8,128)(2,1)} all-to-all(bf16[2,32,6144]{2,1,0:T(8,128)(2,1)S(1)} %reshape.108), channel_id=1, replica_groups=mesh['z'=8,'core'=2,'blk'=16] {'core'}, dimensions={0} | all-to-all | bytes 1572864 | tf_op jit(solution)/shard_map/all_to_all | solution.py:158
  40.8 0.0 all-gather.2.cloned.1.call-update
  41.5 0.0 copy-done.2
  41.5 0.6 dynamic-slice
  42.1 0.8 dynamic-update-slice
  42.9 2.4 %all-reduce.2.counts_ref = s32[2]{0:T(128)} all-reduce(s32[2]{0:T(128)S(1)} %dynamic-update-slice), channel_id=1, replica_groups=mesh['z'=8,'core'=2,'blk'=16] {'core'}, use_global_device_ids=true, to_apply=%add.2 | all-reduce | flops 2 | bytes 16
  45.3 0.0 copy-done.1
  45.3 1.8 %all_gather.10 = s32[2,512]{1,0:T(2,128)S(1)} all-gather(s32[2,256]{1,0:T(2,128)S(1)} %copy-done.1), channel_id=1, replica_groups=mesh['z'=8,'core'=2,'blk'=16] {'core'}, dimensions={1}, use_global_device_ids=true | all-gather | bytes 6144 | tf_op jit(solution)/shard_map/all_gather | solution.py:162
  47.1 0.8 copy.29.second_ref
  48.0 0.9 copy.28.first_ref
  48.8 2.3 %negate_convert_fusion = (bf16[129,1024]{1,0:T(8,128)(2,1)S(1)}, bf16[129,1024]{1,0:T(8,128)(2,1)S(1)}) fusion(s32[1024]{0:T(1024)S(1)} %iota_add_fusion, s32[129]{0:T(256)S(1)} %iota_add_fusion.1), kind=kLoop, calls=%fused_computation.17 | loop fusion | flops 2245632 | bytes 532996 | tf_op jit(solution)/shard_map/convert_element_type | solution.py:41
  51.1 0.8 pad.8.sin_ref
  51.9 0.7 pad.7.cos_ref
  52.7 61.1 %all-gather.2.cloned.1.call-done.panel_ref = bf16[512,6144]{1,0:T(8,128)(2,1)} async-done(((bf16[64,6144]{1,0:T(8,128)(2,1)}), bf16[512,6144]{1,0:T(8,128)(2,1)}) %all-gather.2.cloned.1.call-update) | async-done | bytes 6291472 | tf_op jit(solution)/shard_map/all_gather | solution.py:160
  113.8 29.7 %shard_map.55 = f32[2,9,144,256]{3,2,1,0:T(8,128)} custom-call(s32[2]{0:T(128)} %all-reduce.2.counts_ref, s32[512,1]{1,0:T(8,128)} %copy.28.first_ref, s32[512,1]{1,0:T(8,128)} %copy.29.second_ref, bf16[512,6144]{1,0:T(8,128)(2,1)} %all-gather.2.cloned.1.call-done.panel_ref, bf16[144,1024]{1,0:T(8,128)(2,1)} %pad.7.cos_ref, bf16[144,1024]{1,0:T(8,128)(2,1)} %pad.8.sin_ref), custom_call_target="tpu_custom_call" | custom-call | flops 9160359936 | bytes 8945664 | tf_op jit(solution)/shard_map/pallas_call | solution.py:111
  143.4 7.4 %all_to_all.17 = f32[2,9,144,256]{3,2,1,0:T(8,128)S(1)} all-to-all(f32[2,9,144,256]{3,2,1,0:T(8,128)} %shard_map.55), channel_id=1, replica_groups=mesh['z'=8,'core'=2,'blk'=16] {'core'}, dimensions={0} | all-to-all | bytes 5308416 | tf_op jit(solution)/shard_map/all_to_all | solution.py:167
  150.8 1.4 reduce_sum.28
  152.2 2.3 %fusion.2 = bf16[129,9,256]{2,0,1:T(8,128)(2,1)} fusion(f32[9,144,256]{2,1,0:T(8,128)} %reduce_sum.28, pred[256]{0:T(512)(128)(4,1)S(1)} %iota_compare_fusion.1), kind=kLoop, calls=%fused_computation.13 | loop fusion | flops 891648 | bytes 1783552 | tf_op jit(solution)/shard_map/transpose | solution.py:172
  (8 shorter events, 0.0 us)
Async XLA Ops:
  6.5 4.7 %copy-start = (f32[16,3,2,2048]{3,2,1,0:T(2,128)S(1)}, f32[16,3,2,2048]{3,2,1,0:T(2,128)}, u32[]{:S(2)}) copy-start(f32[16,3,2,2048]{3,2,1,0:T(2,128)} %param.5) | copy-start | bytes 2359300
  6.5 107.2 %all-gather.2.cloned.1.call-start = ((), (), s32[]{:S(2)}) async-start(), calls=%async_computation.3 | async-start | bytes 7077888 | tf_op jit(solution)/shard_map/all_gather | solution.py:160
  33.7 7.8 %copy-start.2 = (u32[256]{0:T(256)S(1)}, u32[256]{0:T(256)}, u32[]{:S(2)}) copy-start(u32[256]{0:T(256)} %constant.79) | copy-start | bytes 3076
  33.7 11.6 %copy-start.1 = (s32[2,256]{1,0:T(2,128)S(1)}, s32[2,256]{1,0:T(2,128)}, u32[]{:S(2)}) copy-start(s32[2,256]{1,0:T(2,128)} %param.8) | copy-start | bytes 6148
Sparse Core Ops, SparseCore 0:
  41.0 72.7 all-gather.1

commit v2 on v1

--- a/solution.py
+++ b/solution.py
@@ -14,6 +14,7 @@
 PAIR_BLOCK = 128
 BIN_CHUNK = 256
 GATHER_CHUNK = 512
+CHUNKS = 4
 
 
 def whiten(spectra):
@@ -42,15 +43,19 @@
     return cos_rows, sin_rows
 
 
-def pair_kernel(counts_ref, first_ref, second_ref, panel_ref, cos_ref, sin_ref, out_ref,
-                f_scr, s_scr, *, blocks_per_owner, part_bins):
+def pair_kernel(counts_ref, first_ref, second_ref, panel_ref, cos_ref, sin_ref, *rest,
+                blocks_per_owner, part_bins, accumulate):
+    if accumulate:
+        acc_ref, out_ref, f_scr, s_scr = rest
+    else:
+        out_ref, f_scr, s_scr = rest
     step = pl.program_id(0)
     owner = step // blocks_per_owner
     start = (step % blocks_per_owner) * PAIR_BLOCK
     live = start < counts_ref[owner]
-
-    @pl.when(jnp.logical_not(live))
-    def _():
+    if accumulate:
+        out_ref[...] = acc_ref[...]
+    else:
         out_ref[...] = jnp.zeros_like(out_ref)
 
     @pl.when(live)
@@ -60,30 +65,31 @@
         iota = lax.broadcasted_iota(jnp.int32, (PAIR_BLOCK, rows), 1)
         pick_first = (first_ref[...] == iota).astype(jnp.bfloat16)
         pick_second = (second_ref[...] == iota).astype(jnp.bfloat16)
+        gather_chunk = min(GATHER_CHUNK, width)
 
         def gather(c, carry):
-            off = pl.multiple_of(c * GATHER_CHUNK, GATHER_CHUNK)
-            block = panel_ref[:, pl.ds(off, GATHER_CHUNK)]
-            f_scr[:, pl.ds(off, GATHER_CHUNK)] = jnp.dot(
+            off = pl.multiple_of(c * gather_chunk, gather_chunk)
+            block = panel_ref[:, pl.ds(off, gather_chunk)]
+            f_scr[:, pl.ds(off, gather_chunk)] = jnp.dot(
                 pick_first, block, preferred_element_type=jnp.float32)
-            s_scr[:, pl.ds(off, GATHER_CHUNK)] = jnp.dot(
+            s_scr[:, pl.ds(off, gather_chunk)] = jnp.dot(
                 pick_second, block, preferred_element_type=jnp.float32)
             return carry
 
-        lax.fori_loop(0, width // GATHER_CHUNK, gather, 0)
-        out_ref[...] = jnp.zeros_like(out_ref)
+        lax.fori_loop(0, width // gather_chunk, gather, 0)
         nt = (((1,), (1,)), ((), ()))
+        bin_chunk = min(BIN_CHUNK, part_bins)
 
         def chunk(kc, carry):
-            off = pl.multiple_of(kc * BIN_CHUNK, BIN_CHUNK)
-            cos_blk = cos_ref[:, pl.ds(off, BIN_CHUNK)]
-            sin_blk = sin_ref[:, pl.ds(off, BIN_CHUNK)]
+            off = pl.multiple_of(kc * bin_chunk, bin_chunk)
+            cos_blk = cos_ref[:, pl.ds(off, bin_chunk)]
+            sin_blk = sin_ref[:, pl.ds(off, bin_chunk)]
             for a in range(3):
-                f_re = f_scr[:, pl.ds(2 * a * part_bins + off, BIN_CHUNK)]
-                f_im = f_scr[:, pl.ds((2 * a + 1) * part_bins + off, BIN_CHUNK)]
+                f_re = f_scr[:, pl.ds(2 * a * part_bins + off, bin_chunk)]
+                f_im = f_scr[:, pl.ds((2 * a + 1) * part_bins + off, bin_chunk)]
                 for b in range(3):
-                    s_re = s_scr[:, pl.ds(2 * b * part_bins + off, BIN_CHUNK)]
-                    s_im = s_scr[:, pl.ds((2 * b + 1) * part_bins + off, BIN_CHUNK)]
+                    s_re = s_scr[:, pl.ds(2 * b * part_bins + off, bin_chunk)]
+                    s_im = s_scr[:, pl.ds((2 * b + 1) * part_bins + off, bin_chunk)]
                     real_part = (f_re * s_re + f_im * s_im).astype(jnp.bfloat16)
                     imag_part = (f_im * s_re - f_re * s_im).astype(jnp.bfloat16)
                     acc = lax.dot_general(cos_blk, real_part, nt,
@@ -93,46 +99,57 @@
                     out_ref[0, 3 * a + b] += acc
             return carry
 
-        lax.fori_loop(0, part_bins // BIN_CHUNK, chunk, 0)
-
-
-def pair_sums(counts, first_idx, second_idx, panel, cos_rows, sin_rows, owners):
+        lax.fori_loop(0, part_bins // bin_chunk, chunk, 0)
+
+
+def pair_sums(counts, first_idx, second_idx, panel, cos_rows, sin_rows, owners, chunk_id, acc):
     rows, width = panel.shape
     part_bins = width // 6
     pairs = first_idx.shape[0]
     per_owner = pairs // owners
     blocks_per_owner = per_owner // PAIR_BLOCK
     grid = (pairs // PAIR_BLOCK,)
+    accumulate = acc is not None
     kernel = functools.partial(pair_kernel, blocks_per_owner=blocks_per_owner,
-                               part_bins=part_bins)
+                               part_bins=part_bins, accumulate=accumulate)
     flops = 2 * pairs * rows * width * 2 + 2 * LAG_ROWS * 2 * part_bins * 9 * pairs
+    out_bytes = owners * 9 * LAG_ROWS * per_owner * 4
     cost = pl.CostEstimate(flops=flops, transcendentals=0,
-                           bytes_accessed=rows * width * 2 + owners * 9 * LAG_ROWS * per_owner * 4)
+                           bytes_accessed=rows * width * 2 + out_bytes * (2 if accumulate else 1))
+    out_spec = pl.BlockSpec(
+        (1, 9, LAG_ROWS, PAIR_BLOCK),
+        lambda i, c: (i // blocks_per_owner, 0, 0, i % blocks_per_owner))
+    in_specs = [
+        pl.BlockSpec((PAIR_BLOCK, 1), lambda i, c: (i, 0)),
+        pl.BlockSpec((PAIR_BLOCK, 1), lambda i, c: (i, 0)),
+        pl.BlockSpec((rows, width), lambda i, c: (0, 0)),
+        pl.BlockSpec((LAG_ROWS, part_bins), lambda i, c: (0, chunk_id)),
+        pl.BlockSpec((LAG_ROWS, part_bins), lambda i, c: (0, chunk_id)),
+    ]
+    args = [counts, first_idx, second_idx, panel, cos_rows, sin_rows]
+    aliases = {}
+    if accumulate:
+        in_specs.append(out_spec)
+        args.append(acc)
+        aliases = {len(args) - 1: 0}
     return pl.pallas_call(
         kernel,
         out_shape=jax.ShapeDtypeStruct((owners, 9, LAG_ROWS, per_owner), jnp.float32),
         grid_spec=pltpu.PrefetchScalarGridSpec(
             num_scalar_prefetch=1,
             grid=grid,
-            in_specs=[
-                pl.BlockSpec((PAIR_BLOCK, 1), lambda i, c: (i, 0)),
-                pl.BlockSpec((PAIR_BLOCK, 1), lambda i, c: (i, 0)),
-                pl.BlockSpec((rows, width), lambda i, c: (0, 0)),
-                pl.BlockSpec((LAG_ROWS, part_bins), lambda i, c: (0, 0)),
-                pl.BlockSpec((LAG_ROWS, part_bins), lambda i, c: (0, 0)),
-            ],
-            out_specs=pl.BlockSpec(
-                (1, 9, LAG_ROWS, PAIR_BLOCK),
-                lambda i, c: (i // blocks_per_owner, 0, 0, i % blocks_per_owner)),
+            in_specs=in_specs,
+            out_specs=out_spec,
             scratch_shapes=[
                 pltpu.VMEM((PAIR_BLOCK, width), jnp.float32),
                 pltpu.VMEM((PAIR_BLOCK, width), jnp.float32),
             ],
         ),
+        input_output_aliases=aliases,
         compiler_params=pltpu.CompilerParams(
             dimension_semantics=("arbitrary",), vmem_limit_bytes=60 * 1024 * 1024),
         cost_estimate=cost,
-    )(counts, first_idx, second_idx, panel, cos_rows, sin_rows)
+    )(*args)
 
 
 def shards(spectra, send_rows, send_counts, pair_rows, pair_counts):
@@ -152,18 +169,20 @@
     picked = jnp.where(alive[:, :, None], picked, jnp.zeros_like(picked))
     received = lax.all_to_all(picked, "blk", 0, 0, tiled=True)
 
-    halves = received.reshape(col_count, slot_count, comps * parts, cores, part_bins)
-    halves = jnp.transpose(halves, (3, 0, 1, 2, 4)).reshape(
-        cores, col_count * slot_count, comps * parts * part_bins)
-    mine = lax.all_to_all(halves, "core", 0, 0, tiled=True)
-    mine = mine.reshape(cores * col_count * slot_count, comps * parts * part_bins)
-    panel = lax.all_gather(mine, "z", axis=0, tiled=True)
-
     chip_pairs = lax.all_gather(pair_rows, "core", axis=1, tiled=True)
     chip_counts = lax.all_gather(pair_counts, "core", axis=0, tiled=True)
     cos_rows, sin_rows = lag_part(bin_count, core * part_bins, part_bins)
-    partial = pair_sums(chip_counts, chip_pairs[0][:, None], chip_pairs[1][:, None],
-                        panel, cos_rows, sin_rows, cores)
+    chunk_bins = part_bins // CHUNKS
+    pieces = received.reshape(col_count, slot_count, comps * parts, cores, CHUNKS, chunk_bins)
+    partial = None
+    for chunk_id in range(CHUNKS):
+        piece = jnp.transpose(pieces[:, :, :, :, chunk_id, :], (3, 0, 1, 2, 4)).reshape(
+            cores, col_count * slot_count, comps * parts * chunk_bins)
+        mine = lax.all_to_all(piece, "core", 0, 0, tiled=True)
+        mine = mine.reshape(cores * col_count * slot_count, comps * parts * chunk_bins)
+        panel = lax.all_gather(mine, "z", axis=0, tiled=True)
+        partial = pair_sums(chip_counts, chip_pairs[0][:, None], chip_pairs[1][:, None],
+                            panel, cos_rows, sin_rows, cores, chunk_id, partial)
     partial = lax.all_to_all(partial, "core", 0, 0, tiled=True)
     total = jnp.sum(partial, axis=0)[:, :LAGS, :] * (1.0 / math.sqrt(bin_count))
     pair_total = pair_rows.shape[1]

time: 162 us -> 230 us (1.42)
  the two profiles are of different devices: /device:TPU:69 before, /device:TPU:1 now
where the time goes in v2:
time: 230 us; the launch traced here: 229 us
  waiting for transfers between devices  105 us (46%)
  blocking collectives  56.3 us (24%)
  Pallas kernels  32.9 us (14%)
  between operations  14 us (6%)
  local copies, waits for them, and re-layouts  10.7 us (5%)
  other arithmetic  9.83 us (4%)
    all_gather x4, waiting for transfers between devices, shards(): panel = lax.all_gather(mine, 'z', axis=0, tiled=True)  105 us
    pallas_call x4, Pallas kernels, pair_sums(): pl.pallas_call(kernel, out_shape=jax.ShapeDtypeStruct((owners, 9, LAG_ROW...  32.9 us
    all_to_all x1, blocking collectives, shards(): received = lax.all_to_all(picked, 'blk', 0, 0, tiled=True)  20.9 us
    all_to_all x4, blocking collectives, shards(): mine = lax.all_to_all(piece, 'core', 0, 0, tiled=True)  19.8 us
    all_to_all x1, blocking collectives, shards(): partial = lax.all_to_all(partial, 'core', 0, 0, tiled=True)  11.2 us
  transfers between devices with their start and end apart: 4, of which 4 were waited for; matrix products, arithmetic and copies ran while one was open for 3% of the time, Pallas kernels for 11%

profile of v2, /device:TPU:1, one launch (start us, length us, event | category | flops | bytes accessed | tf_op | source)
XLA Modules:
  0.0 228.8 jit_solution(12102300285613816313)
XLA Ops:
  6.5 0.1 subtract_select_fusion
  6.6 0.8 copy.77
  7.4 0.7 compare_and_fusion
  8.1 1.7 multiply_reduce_fusion
  9.8 0.1 reduce_sum.26
  9.9 0.1 reduce_sum.27
  10.1 0.1 broadcast_in_dim.49
  10.2 0.1 mul.64
  10.3 0.4 multiply_convert_fusion
  10.7 0.3 reshape.124
  11.0 0.1 reshape_squeeze.6
  11.1 1.0 gather_fusion
  12.2 0.5 gather.7
  12.7 0.1 copy.76
  12.8 0.0 copy-done.2
  12.8 0.1 iota_compare_fusion
  12.9 0.9 broadcast_select_fusion.1
  13.7 20.9 %all_to_all.30 = bf16[16,2,12288]{2,1,0:T(2,128)(2,1)S(1)} all-to-all(bf16[16,2,12288]{2,1,0:T(2,128)(2,1)S(1)} %broadcast_select_fusion.1), channel_id=1, replica_groups=mesh['z'=8,'core'=2,'blk'=16] {'blk'}, dimensions={0} | all-to-all | bytes 1572864 | tf_op jit(solution)/shard_map/all_to_all | solution.py:170
  34.6 0.6 reshape.147
  35.2 1.2 fusion.10
  36.5 0.2 reshape.132
  36.7 6.0 %all_to_all.31 = bf16[2,32,1536]{2,1,0:T(8,128)(2,1)} all-to-all(bf16[2,32,1536]{2,1,0:T(8,128)(2,1)S(1)} %reshape.132), channel_id=1, replica_groups=mesh['z'=8,'core'=2,'blk'=16] {'core'}, dimensions={0} | all-to-all | bytes 393216 | tf_op jit(solution)/shard_map/all_to_all | solution.py:181
  42.9 0.2 reshape.130
  43.1 4.6 %all_to_all.32 = bf16[2,32,1536]{2,1,0:T(8,128)(2,1)} all-to-all(bf16[2,32,1536]{2,1,0:T(8,128)(2,1)S(1)} %reshape.130), channel_id=1, replica_groups=mesh['z'=8,'core'=2,'blk'=16] {'core'}, dimensions={0} | all-to-all | bytes 393216 | tf_op jit(solution)/shard_map/all_to_all | solution.py:181
  47.8 0.2 reshape.128
  48.1 4.6 %all_to_all.33 = bf16[2,32,1536]{2,1,0:T(8,128)(2,1)} all-to-all(bf16[2,32,1536]{2,1,0:T(8,128)(2,1)S(1)} %reshape.128), channel_id=1, replica_groups=mesh['z'=8,'core'=2,'blk'=16] {'core'}, dimensions={0} | all-to-all | bytes 393216 | tf_op jit(solution)/shard_map/all_to_all | solution.py:181
  52.8 0.2 reshape.126
  53.1 4.6 %all_to_all.34 = bf16[2,32,1536]{2,1,0:T(8,128)(2,1)} all-to-all(bf16[2,32,1536]{2,1,0:T(8,128)(2,1)S(1)} %reshape.126), channel_id=1, replica_groups=mesh['z'=8,'core'=2,'blk'=16] {'core'}, dimensions={0} | all-to-all | bytes 393216 | tf_op jit(solution)/shard_map/all_to_all | solution.py:181
  58.3 0.6 dynamic-slice
  58.9 0.8 dynamic-update-slice
  59.7 2.4 %all-reduce.2.counts_ref = s32[2]{0:T(128)} all-reduce(s32[2]{0:T(128)S(1)} %dynamic-update-slice), channel_id=1, replica_groups=mesh['z'=8,'core'=2,'blk'=16] {'core'}, use_global_device_ids=true, to_apply=%add.2 | all-reduce | flops 2 | bytes 16
  62.1 2.3 %negate_convert_fusion = (bf16[129,1024]{1,0:T(8,128)(2,1)S(1)}, bf16[129,1024]{1,0:T(8,128)(2,1)S(1)}) fusion(s32[1024]{0:T(1024)S(1)} %iota_add_fusion, s32[129]{0:T(256)S(1)} %iota_add_fusion.1), kind=kLoop, calls=%fused_computation.17 | loop fusion | flops 2245632 | bytes 532996 | tf_op jit(solution)/shard_map/convert_element_type | solution.py:42
  64.4 0.7 pad.7.cos_ref
  65.1 0.8 pad.8.sin_ref
  65.9 2.0 all_gather.19
  67.9 0.9 copy.93.first_ref
  68.8 0.9 copy.94.second_ref
  69.6 8.2 %all-gather.11.cloned.1.call-done.panel_ref = bf16[512,1536]{1,0:T(8,128)(2,1)} async-done(((bf16[64,1536]{1,0:T(8,128)(2,1)}), bf16[512,1536]{1,0:T(8,128)(2,1)}) %all-gather.11.cloned.1.call-update) | async-done | bytes 1572880 | tf_op jit(solution)/shard_map/all_gather | solution.py:183
  77.8 7.6 %shard_map.55.rest_0_ = f32[2,9,144,256]{3,2,1,0:T(8,128)} custom-call(s32[2]{0:T(128)} %all-reduce.2.counts_ref, s32[512,1]{1,0:T(8,128)} %copy.93.first_ref, s32[512,1]{1,0:T(8,128)} %copy.94.second_ref, bf16[512,1536]{1,0:T(8,128)(2,1)} %all-gather.11.cloned.1.call-done.panel_ref, bf16[144,1024]{1,0:T(8,128)(2,1)} %pad.7.cos_ref, ...), custom_call_target="tpu_custom_call" | custom-call | flops 2290089984 | bytes 4227072 | tf_op jit(solution)/shard_map/pallas_call | solution.py:135
  85.4 32.9 %all-gather.9.cloned.1.call-done.panel_ref = bf16[512,1536]{1,0:T(8,128)(2,1)} async-done(((bf16[64,1536]{1,0:T(8,128)(2,1)}), bf16[512,1536]{1,0:T(8,128)(2,1)}) %all-gather.9.cloned.1.call-update) | async-done | bytes 1572880 | tf_op jit(solution)/shard_map/all_gather | solution.py:183
  118.3 8.4 %shard_map.56.rest_0_ = f32[2,9,144,256]{3,2,1,0:T(8,128)} custom-call(s32[2]{0:T(128)} %all-reduce.2.counts_ref, s32[512,1]{1,0:T(8,128)} %copy.93.first_ref, s32[512,1]{1,0:T(8,128)} %copy.94.second_ref, bf16[512,1536]{1,0:T(8,128)(2,1)} %all-gather.9.cloned.1.call-done.panel_ref, bf16[144,1024]{1,0:T(8,128)(2,1)} %pad.7.cos_ref, ...), custom_call_target="tpu_custom_call", output_to_operand_aliasing={{}: (6, {})} | custom-call | flops 2290089984 | bytes 6881280 | tf_op jit(solution)/shard_map/pallas_call | solution.py:135
  126.7 32.0 %all-gather.7.cloned.1.call-done.panel_ref = bf16[512,1536]{1,0:T(8,128)(2,1)} async-done(((bf16[64,1536]{1,0:T(8,128)(2,1)}), bf16[512,1536]{1,0:T(8,128)(2,1)}) %all-gather.7.cloned.1.call-update) | async-done | bytes 1572880 | tf_op jit(solution)/shard_map/all_gather | solution.py:183
  158.7 8.4 %shard_map.57.rest_0_ = f32[2,9,144,256]{3,2,1,0:T(8,128)} custom-call(s32[2]{0:T(128)} %all-reduce.2.counts_ref, s32[512,1]{1,0:T(8,128)} %copy.93.first_ref, s32[512,1]{1,0:T(8,128)} %copy.94.second_ref, bf16[512,1536]{1,0:T(8,128)(2,1)} %all-gather.7.cloned.1.call-done.panel_ref, bf16[144,1024]{1,0:T(8,128)(2,1)} %pad.7.cos_ref, ...), custom_call_target="tpu_custom_call", output_to_operand_aliasing={{}: (6, {})} | custom-call | flops 2290089984 | bytes 6881280 | tf_op jit(solution)/shard_map/pallas_call | solution.py:135
  167.2 31.8 %all-gather.5.cloned.1.call-done.panel_ref = bf16[512,1536]{1,0:T(8,128)(2,1)} async-done(((bf16[64,1536]{1,0:T(8,128)(2,1)}), bf16[512,1536]{1,0:T(8,128)(2,1)}) %all-gather.5.cloned.1.call-update) | async-done | bytes 1572880 | tf_op jit(solution)/shard_map/all_gather | solution.py:183
  199.0 8.4 %shard_map.58 = f32[2,9,144,256]{3,2,1,0:T(8,128)} custom-call(s32[2]{0:T(128)} %all-reduce.2.counts_ref, s32[512,1]{1,0:T(8,128)} %copy.93.first_ref, s32[512,1]{1,0:T(8,128)} %copy.94.second_ref, bf16[512,1536]{1,0:T(8,128)(2,1)} %all-gather.5.cloned.1.call-done.panel_ref, bf16[144,1024]{1,0:T(8,128)(2,1)} %pad.7.cos_ref, ...), custom_call_target="tpu_custom_call", output_to_operand_aliasing={{}: (6, {})} | custom-call | flops 2290089984 | bytes 6881280 | tf_op jit(solution)/shard_map/pallas_call | solution.py:135
  207.4 11.2 %all_to_all.35 = f32[2,9,144,256]{3,2,1,0:T(8,128)S(1)} all-to-all(f32[2,9,144,256]{3,2,1,0:T(8,128)} %shard_map.58), channel_id=1, replica_groups=mesh['z'=8,'core'=2,'blk'=16] {'core'}, dimensions={0} | all-to-all | bytes 5308416 | tf_op jit(solution)/shard_map/all_to_all | solution.py:186
  218.7 1.4 reduce_sum.28
  220.0 2.3 fusion.2
  (27 shorter events, 0.4 us)
Async XLA Ops:
  6.5 3.8 %copy-start = (f32[16,3,2,2048]{3,2,1,0:T(2,128)S(1)}, f32[16,3,2,2048]{3,2,1,0:T(2,128)}, u32[]{:S(2)}) copy-start(f32[16,3,2,2048]{3,2,1,0:T(2,128)} %param.5) | copy-start | bytes 2359300
  6.5 71.3 %all-gather.11.cloned.1.call-start = ((), (), s32[]{:S(2)}) async-start(), calls=%async_computation.9 | async-start | bytes 1769472 | tf_op jit(solution)/shard_map/all_gather | solution.py:183
  12.2 0.7 copy-start.2
  42.8 75.5 %all-gather.9.cloned.1.call-start = ((), (), s32[]{:S(2)}) async-start(), calls=%async_computation.8 | async-start | bytes 1769472 | tf_op jit(solution)/shard_map/all_gather | solution.py:183
  47.7 111.0 %all-gather.7.cloned.1.call-start = ((), (), s32[]{:S(2)}) async-start(), calls=%async_computation.7 | async-start | bytes 1769472 | tf_op jit(solution)/shard_map/all_gather | solution.py:183
  47.8 10.6 %copy-start.3 = (u32[256]{0:T(256)S(1)}, u32[256]{0:T(256)}, u32[]{:S(2)}) copy-start(u32[256]{0:T(256)} %constant.79) | copy-start | bytes 3076
  52.7 146.3 %all-gather.5.cloned.1.call-start = ((), (), s32[]{:S(2)}) async-start(), calls=%async_computation.6 | async-start | bytes 1769472 | tf_op jit(solution)/shard_map/all_gather | solution.py:183
  52.7 13.1 %copy-start.1 = (s32[2,256]{1,0:T(2,128)S(1)}, s32[2,256]{1,0:T(2,128)}, u32[]{:S(2)}) copy-start(s32[2,256]{1,0:T(2,128)} %param.8) | copy-start | bytes 6148
Sparse Core Ops, SparseCore 0:
  42.9 34.8 all-gather.10
  79.6 38.6 all-gather.8
  120.1 38.5 all-gather.6
  160.4 38.5 all-gather.4

commit v3 on v2

--- a/solution.py
+++ b/solution.py
@@ -14,7 +14,6 @@
 PAIR_BLOCK = 128
 BIN_CHUNK = 256
 GATHER_CHUNK = 512
-CHUNKS = 4
 
 
 def whiten(spectra):
@@ -167,22 +166,18 @@
     picked = jnp.take(flat, lists.reshape(-1), axis=0).reshape(col_count, slot_count, row_width)
     alive = jnp.arange(slot_count, dtype=jnp.int32)[None, :] < send_counts[0][:, None]
     picked = jnp.where(alive[:, :, None], picked, jnp.zeros_like(picked))
-    received = lax.all_to_all(picked, "blk", 0, 0, tiled=True)
+    pieces = picked.reshape(col_count, slot_count, comps * parts, cores, part_bins)
+    pieces = jnp.transpose(pieces, (3, 0, 1, 2, 4)).reshape(
+        cores * col_count, slot_count, comps * parts * part_bins)
+    mine = lax.all_to_all(pieces, ("core", "blk"), 0, 0, tiled=True)
+    mine = mine.reshape(cores * col_count * slot_count, comps * parts * part_bins)
+    panel = lax.all_gather(mine, "z", axis=0, tiled=True)
 
     chip_pairs = lax.all_gather(pair_rows, "core", axis=1, tiled=True)
     chip_counts = lax.all_gather(pair_counts, "core", axis=0, tiled=True)
     cos_rows, sin_rows = lag_part(bin_count, core * part_bins, part_bins)
-    chunk_bins = part_bins // CHUNKS
-    pieces = received.reshape(col_count, slot_count, comps * parts, cores, CHUNKS, chunk_bins)
-    partial = None
-    for chunk_id in range(CHUNKS):
-        piece = jnp.transpose(pieces[:, :, :, :, chunk_id, :], (3, 0, 1, 2, 4)).reshape(
-            cores, col_count * slot_count, comps * parts * chunk_bins)
-        mine = lax.all_to_all(piece, "core", 0, 0, tiled=True)
-        mine = mine.reshape(cores * col_count * slot_count, comps * parts * chunk_bins)
-        panel = lax.all_gather(mine, "z", axis=0, tiled=True)
-        partial = pair_sums(chip_counts, chip_pairs[0][:, None], chip_pairs[1][:, None],
-                            panel, cos_rows, sin_rows, cores, chunk_id, partial)
+    partial = pair_sums(chip_counts, chip_pairs[0][:, None], chip_pairs[1][:, None],
+                        panel, cos_rows, sin_rows, cores, 0, None)
     partial = lax.all_to_all(partial, "core", 0, 0, tiled=True)
     total = jnp.sum(partial, axis=0)[:, :LAGS, :] * (1.0 / math.sqrt(bin_count))
     pair_total = pair_rows.shape[1]

time: 230 us -> 155 us (0.67)
  the two profiles are of different devices: /device:TPU:1 before, /device:TPU:159 now
where the time goes in v3:
time: 155 us
  waiting for transfers between devices  60.7 us (39%)
  blocking collectives  30.2 us (19%)
  Pallas kernels  29.7 us (19%)
  between operations  14.2 us (9%)
  local copies, waits for them, and re-layouts  10.8 us (7%)
  other arithmetic  9.2 us (6%)
    all_gather x1, waiting for transfers between devices, shards(): panel = lax.all_gather(mine, 'z', axis=0, tiled=True)  60.6 us
    pallas_call x1, Pallas kernels, pair_sums(): pl.pallas_call(kernel, out_shape=jax.ShapeDtypeStruct((owners, 9, LAG_ROW...  29.7 us
    all_to_all x1, blocking collectives, shards(): mine = lax.all_to_all(pieces, ('core', 'blk'), 0, 0, tiled=True)  18.6 us
    all_to_all x1, blocking collectives, shards(): partial = lax.all_to_all(partial, 'core', 0, 0, tiled=True)  7.37 us
  transfers between devices with their start and end apart: 1, of which 1 were waited for; matrix products, arithmetic and copies ran while one was open for 4% of the time, Pallas kernels for 0%

profile of v3, /device:TPU:159, one launch (start us, length us, event | category | flops | bytes accessed | tf_op | source)
XLA Modules:
  0.0 154.7 jit_solution(3548333273971542014)
XLA Ops:
  6.5 0.0 copy-start
  6.5 0.0 all-gather.2.cloned.1.call-start
  6.5 0.1 subtract_select_fusion
  6.6 0.8 copy.19
  7.4 0.7 compare_and_fusion
  8.1 0.1 reshape_squeeze.6
  8.2 1.7 %multiply_reduce_fusion = f32[16,2048]{1,0:T(8,128)S(1)} fusion(f32[16,3,2,2048]{3,2,1,0:T(2,128)} %param.5), kind=kLoop, calls=%fused_computation.13 | loop fusion | flops 360448 | bytes 917504 | tf_op jit(solution)/shard_map/reduce_sum | solution.py:28
  9.9 0.1 reduce_sum.26
  10.0 0.1 reduce_sum.27
  10.2 0.1 broadcast_in_dim.49
  10.3 0.1 mul.64
  10.4 0.0 copy-done
  10.4 0.4 multiply_convert_fusion
  10.8 0.3 reshape.106
  11.1 1.0 gather_fusion
  12.2 0.6 gather.7
  12.7 0.3 fusion.3
  13.0 1.1 reshape.107
  14.1 0.8 copy.21
  14.9 18.6 %all_to_all.10 = bf16[32,2,6144]{2,1,0:T(2,128)(2,1)S(1)} all-to-all(bf16[32,2,6144]{2,1,0:T(2,128)(2,1)S(1)} %copy.21), channel_id=1, replica_groups=mesh['z'=8,'core'=2,'blk'=16] {'core','blk'}, dimensions={0} | all-to-all | bytes 1572864 | tf_op jit(solution)/shard_map/all_to_all | solution.py:172
  33.5 0.0 copy-start.2
  33.5 0.0 copy-start.1
  33.5 1.2 reshape.108
  34.7 0.0 all-gather.2.cloned.1.call-update
  35.4 0.0 copy-done.2
  35.4 0.6 dynamic-slice
  36.0 0.8 dynamic-update-slice
  36.7 2.4 %all-reduce.2.counts_ref = s32[2]{0:T(128)} all-reduce(s32[2]{0:T(128)S(1)} %dynamic-update-slice), channel_id=1, replica_groups=mesh['z'=8,'core'=2,'blk'=16] {'core'}, use_global_device_ids=true, to_apply=%add.2 | all-reduce | flops 2 | bytes 16
  39.2 0.0 copy-done.1
  39.2 1.8 %all_gather.10 = s32[2,512]{1,0:T(2,128)S(1)} all-gather(s32[2,256]{1,0:T(2,128)S(1)} %copy-done.1), channel_id=1, replica_groups=mesh['z'=8,'core'=2,'blk'=16] {'core'}, dimensions={1}, use_global_device_ids=true | all-gather | bytes 6144 | tf_op jit(solution)/shard_map/all_gather | solution.py:176
  40.9 0.8 copy.23.second_ref
  41.8 0.9 copy.22.first_ref
  42.7 2.3 %negate_convert_fusion = (bf16[129,1024]{1,0:T(8,128)(2,1)S(1)}, bf16[129,1024]{1,0:T(8,128)(2,1)S(1)}) fusion(s32[1024]{0:T(1024)S(1)} %iota_add_fusion, s32[129]{0:T(256)S(1)} %iota_add_fusion.1), kind=kLoop, calls=%fused_computation.18 | loop fusion | flops 2245632 | bytes 532996 | tf_op jit(solution)/shard_map/convert_element_type | solution.py:41
  45.0 0.8 pad.8.sin_ref
  45.7 0.7 pad.7.cos_ref
  46.5 60.6 %all-gather.2.cloned.1.call-done.panel_ref = bf16[512,6144]{1,0:T(8,128)(2,1)} async-done(((bf16[64,6144]{1,0:T(8,128)(2,1)}), bf16[512,6144]{1,0:T(8,128)(2,1)}) %all-gather.2.cloned.1.call-update) | async-done | bytes 6291472 | tf_op jit(solution)/shard_map/all_gather | solution.py:174
  107.1 29.7 %shard_map.55 = f32[2,9,144,256]{3,2,1,0:T(8,128)} custom-call(s32[2]{0:T(128)} %all-reduce.2.counts_ref, s32[512,1]{1,0:T(8,128)} %copy.22.first_ref, s32[512,1]{1,0:T(8,128)} %copy.23.second_ref, bf16[512,6144]{1,0:T(8,128)(2,1)} %all-gather.2.cloned.1.call-done.panel_ref, bf16[144,1024]{1,0:T(8,128)(2,1)} %pad.7.cos_ref, bf16[144,1024]{1,0:T(8,128)(2,1)} %pad.8.sin_ref), custom_call_target="tpu_custom_call" | custom-call | flops 9160359936 | bytes 8945664 | tf_op jit(solution)/shard_map/pallas_call | solution.py:134
  136.8 7.4 %all_to_all.11 = f32[2,9,144,256]{3,2,1,0:T(8,128)S(1)} all-to-all(f32[2,9,144,256]{3,2,1,0:T(8,128)} %shard_map.55), channel_id=1, replica_groups=mesh['z'=8,'core'=2,'blk'=16] {'core'}, dimensions={0} | all-to-all | bytes 5308416 | tf_op jit(solution)/shard_map/all_to_all | solution.py:181
  144.2 1.4 reduce_sum.28
  145.6 2.3 %fusion.4 = bf16[129,9,256]{2,0,1:T(8,128)(2,1)} fusion(f32[9,144,256]{2,1,0:T(8,128)} %reduce_sum.28, pred[256]{0:T(512)(128)(4,1)S(1)} %iota_compare_fusion.1), kind=kLoop, calls=%fused_computation.14 | loop fusion | flops 891648 | bytes 1783552 | tf_op jit(solution)/shard_map/transpose | solution.py:186
  (8 shorter events, 0.0 us)
Async XLA Ops:
  6.5 3.9 %copy-start = (f32[16,3,2,2048]{3,2,1,0:T(2,128)S(1)}, f32[16,3,2,2048]{3,2,1,0:T(2,128)}, u32[]{:S(2)}) copy-start(f32[16,3,2,2048]{3,2,1,0:T(2,128)} %param.5) | copy-start | bytes 2359300
  6.5 100.6 %all-gather.2.cloned.1.call-start = ((), (), s32[]{:S(2)}) async-start(), calls=%async_computation.2 | async-start | bytes 7077888 | tf_op jit(solution)/shard_map/all_gather | solution.py:174
  33.5 1.9 %copy-start.2 = (u32[256]{0:T(256)S(1)}, u32[256]{0:T(256)}, u32[]{:S(2)}) copy-start(u32[256]{0:T(256)} %constant.79) | copy-start | bytes 3076
  33.5 5.6 %copy-start.1 = (s32[2,256]{1,0:T(2,128)S(1)}, s32[2,256]{1,0:T(2,128)}, u32[]{:S(2)}) copy-start(s32[2,256]{1,0:T(2,128)} %param.8) | copy-start | bytes 6148
Sparse Core Ops, SparseCore 0:
  34.9 72.2 all-gather.1

commit v4 on v3

--- a/solution.py
+++ b/solution.py
@@ -151,6 +151,127 @@
     )(*args)
 
 
+MESH_ID = pl.DeviceIdType.MESH
+
+
+def spread_kernel(pieces_ref, panel_ref, send_plane, recv_plane, local_sem, send_right,
+                  send_left, recv_ring, *, ring_size, plane_size, blk_size, slots):
+    me_z = lax.axis_index("z")
+    me_c = lax.axis_index("core")
+    me_b = lax.axis_index("blk")
+    me_q = me_c * blk_size + me_b
+    right = (me_z + 1) % ring_size
+    left = (me_z + ring_size - 1) % ring_size
+
+    def plane_dev(q):
+        return (me_z, q // blk_size, q % blk_size)
+
+    barrier = pltpu.get_barrier_semaphore()
+
+    def greet(i, carry):
+        q = (me_q + i) % plane_size
+        pl.semaphore_signal(barrier, 1, device_id=plane_dev(q), device_id_type=MESH_ID)
+        return carry
+
+    lax.fori_loop(1, plane_size, greet, 0)
+    pl.semaphore_signal(barrier, 1, device_id=(right, me_c, me_b), device_id_type=MESH_ID)
+    pl.semaphore_signal(barrier, 1, device_id=(left, me_c, me_b), device_id_type=MESH_ID)
+    pl.semaphore_wait(barrier, plane_size + 1)
+
+    block_rows = plane_size * slots
+    base = me_z * block_rows
+
+    def rows_of(q):
+        return panel_ref.at[pl.ds(base + q * slots, slots)]
+
+    local = pltpu.make_async_copy(pieces_ref.at[me_q], rows_of(me_q), local_sem)
+    local.start()
+
+    def plane_copy(q, src_q, dst_q):
+        return pltpu.make_async_remote_copy(
+            pieces_ref.at[q], rows_of(dst_q), send_plane.at[q], recv_plane.at[src_q],
+            device_id=plane_dev(q), device_id_type=MESH_ID)
+
+    def send(i, carry):
+        q = (me_q + i) % plane_size
+        plane_copy(q, me_q, me_q).start()
+        return carry
+
+    lax.fori_loop(1, plane_size, send, 0)
+
+    def arrive(i, carry):
+        q = (me_q + plane_size - i) % plane_size
+        plane_copy(q, q, q).wait_recv()
+        return carry
+
+    lax.fori_loop(1, plane_size, arrive, 0)
+    local.wait()
+
+    def sent(i, carry):
+        q = (me_q + i) % plane_size
+        plane_copy(q, me_q, me_q).wait_send()
+        return carry
+
+    lax.fori_loop(1, plane_size, sent, 0)
+
+    def block_of(k):
+        return panel_ref.at[pl.ds(k * block_rows, block_rows)]
+
+    def ring_copy(k, sem, dev):
+        return pltpu.make_async_remote_copy(
+            block_of(k), block_of(k), sem, recv_ring.at[k],
+            device_id=(dev, me_c, me_b), device_id_type=MESH_ID)
+
+    n_right = ring_size // 2
+    n_left = ring_size - 1 - n_right
+    right_sends = []
+    left_sends = []
+    for s in range(max(n_right, n_left)):
+        if s < n_right:
+            k = (me_z + ring_size - s) % ring_size
+            if s > 0:
+                ring_copy(k, send_right.at[s], left).wait_recv()
+            c = ring_copy(k, send_right.at[s], right)
+            c.start()
+            right_sends.append(c)
+        if s < n_left:
+            k = (me_z + s) % ring_size
+            if s > 0:
+                ring_copy(k, send_left.at[s], right).wait_recv()
+            c = ring_copy(k, send_left.at[s], left)
+            c.start()
+            left_sends.append(c)
+    ring_copy((me_z + ring_size - n_right) % ring_size, send_right.at[0], left).wait_recv()
+    if n_left > 0:
+        ring_copy((me_z + n_left) % ring_size, send_left.at[0], right).wait_recv()
+    for c in right_sends + left_sends:
+        c.wait_send()
+
+
+def spread(pieces, ring_size, plane_size, blk_size):
+    _, slots, width = pieces.shape
+    rows = ring_size * plane_size * slots
+    kernel = functools.partial(spread_kernel, ring_size=ring_size, plane_size=plane_size,
+                               blk_size=blk_size, slots=slots)
+    n_right = ring_size // 2
+    n_left = max(ring_size - 1 - n_right, 1)
+    return pl.pallas_call(
+        kernel,
+        out_shape=jax.ShapeDtypeStruct((rows, width), pieces.dtype),
+        in_specs=[pl.BlockSpec(memory_space=pl.ANY)],
+        out_specs=pl.BlockSpec(memory_space=pl.ANY),
+        scratch_shapes=[
+            pltpu.SemaphoreType.DMA((plane_size,)),
+            pltpu.SemaphoreType.DMA((plane_size,)),
+            pltpu.SemaphoreType.DMA(()),
+            pltpu.SemaphoreType.DMA((n_right,)),
+            pltpu.SemaphoreType.DMA((n_left,)),
+            pltpu.SemaphoreType.DMA((ring_size,)),
+        ],
+        compiler_params=pltpu.CompilerParams(collective_id=0, has_side_effects=True),
+    )(pieces)
+
+
 def shards(spectra, send_rows, send_counts, pair_rows, pair_counts):
     whitened = whiten(spectra)
     station_count, comps, parts, bin_count = whitened.shape
@@ -169,9 +290,7 @@
     pieces = picked.reshape(col_count, slot_count, comps * parts, cores, part_bins)
     pieces = jnp.transpose(pieces, (3, 0, 1, 2, 4)).reshape(
         cores * col_count, slot_count, comps * parts * part_bins)
-    mine = lax.all_to_all(pieces, ("core", "blk"), 0, 0, tiled=True)
-    mine = mine.reshape(cores * col_count * slot_count, comps * parts * part_bins)
-    panel = lax.all_gather(mine, "z", axis=0, tiled=True)
+    panel = spread(pieces, lax.axis_size("z"), cores * col_count, col_count)
 
     chip_pairs = lax.all_gather(pair_rows, "core", axis=1, tiled=True)
     chip_counts = lax.all_gather(pair_counts, "core", axis=0, tiled=True)

time: 155 us -> 152 us (0.981)
  the two profiles are of different devices: /device:TPU:159 before, /device:TPU:245 now
where the time goes in v4:
time: 152 us; the launch traced here: 151 us
  Pallas kernels  117 us (77%)
  local copies, waits for them, and re-layouts  11.1 us (7%)
  other arithmetic  9.2 us (6%)
  starting transfers between devices  6 us (4%)
  blocking collectives  4.61 us (3%)
  waiting for transfers between devices  2.89 us (2%)
    pallas_call x1, Pallas kernels, spread(): pl.pallas_call(kernel, out_shape=jax.ShapeDtypeStruct((rows, width), piec...  86.9 us
    pallas_call x1, Pallas kernels, pair_sums(): pl.pallas_call(kernel, out_shape=jax.ShapeDtypeStruct((owners, 9, LAG_ROW...  29.7 us
    all_to_all x1, starting transfers between devices, shards(): partial = lax.all_to_all(partial, 'core', 0, 0, tiled=True)  6 us
  transfers between devices with their start and end apart: 1, of which 1 were waited for; matrix products, arithmetic and copies ran while one was open for 0% of the time, Pallas kernels for 0%

profile of v4, /device:TPU:245, one launch (start us, length us, event | category | flops | bytes accessed | tf_op | source)
XLA Modules:
  0.0 151.2 jit_solution(14476478902616645063)
XLA Ops:
  0.0 0.0 copy-start
  0.0 0.1 subtract_select_fusion
  0.8 1.3 dynamic-slice
  2.1 0.8 dynamic-update-slice
  2.8 2.7 %all-reduce.2.counts_ref = s32[2]{0:T(128)} all-reduce(s32[2]{0:T(128)S(1)} %dynamic-update-slice), channel_id=1, replica_groups=mesh['z'=8,'core'=2,'blk'=16] {'core'}, use_global_device_ids=true, to_apply=%add.2 | all-reduce | flops 2 | bytes 16
  5.5 0.8 copy.14
  6.2 0.7 compare_and_fusion
  6.9 2.0 %all_gather.7 = s32[2,512]{1,0:T(2,128)S(1)} all-gather(s32[2,256]{1,0:T(2,128)} %param.8), channel_id=1, replica_groups=mesh['z'=8,'core'=2,'blk'=16] {'core'}, dimensions={1}, use_global_device_ids=true | all-gather | bytes 6144 | tf_op jit(solution)/shard_map/all_gather | solution.py:295
  8.9 0.1 reshape_squeeze.6
  9.0 1.7 %multiply_reduce_fusion = f32[16,2048]{1,0:T(8,128)S(1)} fusion(f32[16,3,2,2048]{3,2,1,0:T(2,128)} %param.5), kind=kLoop, calls=%fused_computation.13 | loop fusion | flops 360448 | bytes 917504 | tf_op jit(solution)/shard_map/reduce_sum | solution.py:28
  10.7 0.1 reduce_sum.26
  10.8 0.1 reduce_sum.27
  11.0 0.1 broadcast_in_dim.49
  11.1 0.1 mul.64
  11.2 0.0 copy-done
  11.2 0.4 multiply_convert_fusion
  11.6 0.3 reshape.103
  11.9 0.8 copy.18.second_ref
  12.7 0.9 copy.17.first_ref
  13.6 1.0 gather_fusion
  14.7 0.6 gather.7
  15.2 0.3 fusion.3
  15.5 1.1 reshape.104
  16.6 1.7 %copy.16.pieces_ref = bf16[32,2,6144]{2,1,0:T(2,128)(2,1)} copy(bf16[32,2,6144]{2,0,1:T(8,128)(2,1)S(1)} %reshape.104) | data formatting | bytes 1572864 | tf_op jit(solution)/shard_map/reshape | solution.py:291
  18.3 2.3 %negate_convert_fusion = (bf16[129,1024]{1,0:T(8,128)(2,1)S(1)}, bf16[129,1024]{1,0:T(8,128)(2,1)S(1)}) fusion(s32[1024]{0:T(1024)S(1)} %iota_add_fusion, s32[129]{0:T(256)S(1)} %iota_add_fusion.1), kind=kLoop, calls=%fused_computation.18 | loop fusion | flops 2245632 | bytes 532996 | tf_op jit(solution)/shard_map/convert_element_type | solution.py:41
  20.6 0.8 pad.8.sin_ref
  21.3 0.7 pad.7.cos_ref
  22.1 86.9 %shard_map.55.panel_ref = bf16[512,6144]{1,0:T(8,128)(2,1)} custom-call(bf16[32,2,6144]{2,1,0:T(2,128)(2,1)} %copy.16.pieces_ref), custom_call_target="tpu_custom_call" | custom-call | tf_op jit(solution)/shard_map/pallas_call | solution.py:258
  109.0 29.7 %shard_map.56 = f32[2,9,144,256]{3,2,1,0:T(8,128)} custom-call(s32[2]{0:T(128)} %all-reduce.2.counts_ref, s32[512,1]{1,0:T(8,128)} %copy.17.first_ref, s32[512,1]{1,0:T(8,128)} %copy.18.second_ref, bf16[512,6144]{1,0:T(8,128)(2,1)} %shard_map.55.panel_ref, bf16[144,1024]{1,0:T(8,128)(2,1)} %pad.7.cos_ref, bf16[144,1024]{1,0:T(8,128)(2,1)} %pad.8.sin_ref), custom_call_target="tpu_custom_call" | custom-call | flops 9160359936 | bytes 8945664 | tf_op jit(solution)/shard_map/pallas_call | solution.py:134
  138.7 6.0 %all-to-all-start = ((f32[2,9,144,256]{3,2,1,0:T(8,128)}), f32[2,9,144,256]{3,2,1,0:T(8,128)S(1)}, u32[]{:S(2)}, u32[]{:S(2)}) async-start(f32[2,9,144,256]{3,2,1,0:T(8,128)} %shard_map.56), calls=%async_computation | async-start | bytes 5308416 | tf_op jit(solution)/shard_map/all_to_all | solution.py:300
  144.7 2.9 %all-to-all-done = f32[2,9,144,256]{3,2,1,0:T(8,128)S(1)} async-done(((f32[2,9,144,256]{3,2,1,0:T(8,128)}), f32[2,9,144,256]{3,2,1,0:T(8,128)S(1)}, u32[]{:S(2)}, u32[]{:S(2)}) %all-to-all-start) | async-done | bytes 2654240 | tf_op jit(solution)/shard_map/all_to_all | solution.py:300
  147.6 1.4 reduce_sum.28
  148.9 2.3 %fusion.4 = bf16[129,9,256]{2,0,1:T(8,128)(2,1)} fusion(f32[9,144,256]{2,1,0:T(8,128)} %reduce_sum.28, pred[256]{0:T(512)(128)(4,1)S(1)} %iota_compare_fusion.1), kind=kLoop, calls=%fused_computation.14 | loop fusion | flops 891648 | bytes 1783552 | tf_op jit(solution)/shard_map/transpose | solution.py:305
  (8 shorter events, 0.0 us)
Async XLA Ops:
  0.0 11.2 %copy-start = (f32[16,3,2,2048]{3,2,1,0:T(2,128)S(1)}, f32[16,3,2,2048]{3,2,1,0:T(2,128)}, u32[]{:S(2)}) copy-start(f32[16,3,2,2048]{3,2,1,0:T(2,128)} %param.5) | copy-start | bytes 2359300
  138.7 8.9 %all-to-all-start = ((f32[2,9,144,256]{3,2,1,0:T(8,128)}), f32[2,9,144,256]{3,2,1,0:T(8,128)S(1)}, u32[]{:S(2)}, u32[]{:S(2)}) async-start(f32[2,9,144,256]{3,2,1,0:T(8,128)} %shard_map.56), calls=%async_computation | async-start | bytes 5308416 | tf_op jit(solution)/shard_map/all_to_all | solution.py:300

commit v5 on v4

--- a/solution.py
+++ b/solution.py
@@ -2,6 +2,8 @@
 import math
 
 import jax
+import ml_dtypes
+import numpy as np
 import jax.numpy as jnp
 from jax import lax
 from jax.experimental import pallas as pl
@@ -31,15 +33,15 @@
     return (spectra * taper * spread_scale[:, None, None, :]).astype(jnp.bfloat16)
 
 
-def lag_part(bin_count, first_bin, part_bins):
-    lag_index = jnp.arange(LAGS, dtype=jnp.int32) - LAGS // 2
-    bin_index = first_bin + jnp.arange(part_bins, dtype=jnp.int32)
+def lag_tables(bin_count):
+    lag_index = np.arange(LAGS, dtype=np.int32) - LAGS // 2
+    bin_index = np.arange(bin_count, dtype=np.int32)
     phase_steps = lag_index[:, None] * bin_index[None, :] % (2 * bin_count)
-    angle = phase_steps.astype(jnp.float32) * (jnp.pi / bin_count)
+    angle = phase_steps.astype(np.float32) * np.float32(np.pi / bin_count)
     pad = ((0, LAG_ROWS - LAGS), (0, 0))
-    cos_rows = jnp.pad(jnp.cos(angle).astype(jnp.bfloat16), pad)
-    sin_rows = jnp.pad((-jnp.sin(angle)).astype(jnp.bfloat16), pad)
-    return cos_rows, sin_rows
+    cos_rows = np.pad(np.cos(angle).astype(np.float32).astype(ml_dtypes.bfloat16), pad)
+    sin_rows = np.pad((-np.sin(angle)).astype(np.float32).astype(ml_dtypes.bfloat16), pad)
+    return jnp.asarray(cos_rows), jnp.asarray(sin_rows)
 
 
 def pair_kernel(counts_ref, first_ref, second_ref, panel_ref, cos_ref, sin_ref, *rest,
@@ -122,8 +124,8 @@
         pl.BlockSpec((PAIR_BLOCK, 1), lambda i, c: (i, 0)),
         pl.BlockSpec((PAIR_BLOCK, 1), lambda i, c: (i, 0)),
         pl.BlockSpec((rows, width), lambda i, c: (0, 0)),
-        pl.BlockSpec((LAG_ROWS, part_bins), lambda i, c: (0, chunk_id)),
-        pl.BlockSpec((LAG_ROWS, part_bins), lambda i, c: (0, chunk_id)),
+        pl.BlockSpec((LAG_ROWS, part_bins), lambda i, c: (0, c[owners])),
+        pl.BlockSpec((LAG_ROWS, part_bins), lambda i, c: (0, c[owners])),
     ]
     args = [counts, first_idx, second_idx, panel, cos_rows, sin_rows]
     aliases = {}
@@ -222,29 +224,39 @@
             block_of(k), block_of(k), sem, recv_ring.at[k],
             device_id=(dev, me_c, me_b), device_id_type=MESH_ID)
 
-    n_right = ring_size // 2
-    n_left = ring_size - 1 - n_right
-    right_sends = []
-    left_sends = []
-    for s in range(max(n_right, n_left)):
-        if s < n_right:
-            k = (me_z + ring_size - s) % ring_size
-            if s > 0:
-                ring_copy(k, send_right.at[s], left).wait_recv()
-            c = ring_copy(k, send_right.at[s], right)
-            c.start()
-            right_sends.append(c)
-        if s < n_left:
-            k = (me_z + s) % ring_size
-            if s > 0:
-                ring_copy(k, send_left.at[s], right).wait_recv()
-            c = ring_copy(k, send_left.at[s], left)
-            c.start()
-            left_sends.append(c)
-    ring_copy((me_z + ring_size - n_right) % ring_size, send_right.at[0], left).wait_recv()
-    if n_left > 0:
-        ring_copy((me_z + n_left) % ring_size, send_left.at[0], right).wait_recv()
-    for c in right_sends + left_sends:
+    half = ring_size // 2
+    half_rows = block_rows // 2
+
+    def part_of(k, first):
+        start = k * block_rows + (0 if first else half_rows)
+        return panel_ref.at[pl.ds(start, half_rows)]
+
+    def part_copy(k, first, sem, dev):
+        slot = k if first else ring_size
+        return pltpu.make_async_remote_copy(
+            part_of(k, first), part_of(k, first), sem, recv_ring.at[slot],
+            device_id=(dev, me_c, me_b), device_id_type=MESH_ID)
+
+    sends = []
+    for s in range(half):
+        k = (me_z + ring_size - s) % ring_size
+        if s > 0:
+            ring_copy(k, send_right.at[s], left).wait_recv()
+        c = ring_copy(k, send_right.at[s], right) if s < half - 1 else part_copy(
+            k, True, send_right.at[s], right)
+        c.start()
+        sends.append(c)
+        k = (me_z + s) % ring_size
+        if s > 0:
+            ring_copy(k, send_left.at[s], right).wait_recv()
+        c = ring_copy(k, send_left.at[s], left) if s < half - 1 else part_copy(
+            k, False, send_left.at[s], left)
+        c.start()
+        sends.append(c)
+    far = (me_z + half) % ring_size
+    part_copy(far, True, send_right.at[0], left).wait_recv()
+    part_copy(far, False, send_left.at[0], right).wait_recv()
+    for c in sends:
         c.wait_send()
 
 
@@ -253,8 +265,7 @@
     rows = ring_size * plane_size * slots
     kernel = functools.partial(spread_kernel, ring_size=ring_size, plane_size=plane_size,
                                blk_size=blk_size, slots=slots)
-    n_right = ring_size // 2
-    n_left = max(ring_size - 1 - n_right, 1)
+    half = ring_size // 2
     return pl.pallas_call(
         kernel,
         out_shape=jax.ShapeDtypeStruct((rows, width), pieces.dtype),
@@ -264,9 +275,9 @@
             pltpu.SemaphoreType.DMA((plane_size,)),
             pltpu.SemaphoreType.DMA((plane_size,)),
             pltpu.SemaphoreType.DMA(()),
-            pltpu.SemaphoreType.DMA((n_right,)),
-            pltpu.SemaphoreType.DMA((n_left,)),
-            pltpu.SemaphoreType.DMA((ring_size,)),
+            pltpu.SemaphoreType.DMA((half,)),
+            pltpu.SemaphoreType.DMA((half,)),
+            pltpu.SemaphoreType.DMA((ring_size + 1,)),
         ],
         compiler_params=pltpu.CompilerParams(collective_id=0, has_side_effects=True),
     )(pieces)
@@ -294,7 +305,8 @@
 
     chip_pairs = lax.all_gather(pair_rows, "core", axis=1, tiled=True)
     chip_counts = lax.all_gather(pair_counts, "core", axis=0, tiled=True)
-    cos_rows, sin_rows = lag_part(bin_count, core * part_bins, part_bins)
+    cos_rows, sin_rows = lag_tables(bin_count)
+    chip_counts = jnp.concatenate([chip_counts, core.astype(jnp.int32)[None]])
     partial = pair_sums(chip_counts, chip_pairs[0][:, None], chip_pairs[1][:, None],
                         panel, cos_rows, sin_rows, cores, 0, None)
     partial = lax.all_to_all(partial, "core", 0, 0, tiled=True)

time: 152 us -> 146 us (0.961)
  the two profiles are of different devices: /device:TPU:245 before, /device:TPU:59 now
where the time goes in v5:
time: 146 us; the launch traced here: 145 us
  Pallas kernels  114 us (78%)
  local copies, waits for them, and re-layouts  9.6 us (7%)
  other arithmetic  7.49 us (5%)
  starting transfers between devices  5.93 us (4%)
  blocking collectives  4.09 us (3%)
  waiting for transfers between devices  2.89 us (2%)
    pallas_call x1, Pallas kernels, spread(): pl.pallas_call(kernel, out_shape=jax.ShapeDtypeStruct((rows, width), piec...  84.8 us
    pallas_call x1, Pallas kernels, pair_sums(): pl.pallas_call(kernel, out_shape=jax.ShapeDtypeStruct((owners, 9, LAG_ROW...  29.6 us
    all_to_all x1, starting transfers between devices, shards(): partial = lax.all_to_all(partial, 'core', 0, 0, tiled=True)  5.93 us
  transfers between devices with their start and end apart: 1, of which 1 were waited for; matrix products, arithmetic and copies ran while one was open for 0% of the time, Pallas kernels for 0%

profile of v5, /device:TPU:59, one launch (start us, length us, event | category | flops | bytes accessed | tf_op | source)
XLA Modules:
  0.0 145.2 jit_solution(2648579913316468145)
XLA Ops:
  0.0 0.0 copy-start
  0.0 0.1 subtract_select_fusion
  0.8 1.3 dynamic-slice
  2.0 0.8 dynamic-update-slice
  2.8 2.1 %all-reduce = s32[2]{0:T(128)S(1)} all-reduce(s32[2]{0:T(128)S(1)} %dynamic-update-slice), channel_id=1, replica_groups=mesh['z'=8,'core'=2,'blk'=16] {'core'}, use_global_device_ids=true, to_apply=%add | all-reduce | flops 2 | bytes 16
  4.9 0.8 copy.16
  5.7 0.7 compare_and_fusion
  6.4 1.9 %all_gather.7 = s32[2,512]{1,0:T(2,128)S(1)} all-gather(s32[2,256]{1,0:T(2,128)} %param.10), channel_id=1, replica_groups=mesh['z'=8,'core'=2,'blk'=16] {'core'}, dimensions={1}, use_global_device_ids=true | all-gather | bytes 6144 | tf_op jit(solution)/shard_map/all_gather | solution.py:306
  8.3 0.1 reshape_squeeze.6
  8.5 1.7 %multiply_reduce_fusion = f32[16,2048]{1,0:T(8,128)S(1)} fusion(f32[16,3,2,2048]{3,2,1,0:T(2,128)} %param.7), kind=kLoop, calls=%fused_computation.8 | loop fusion | flops 360448 | bytes 917504 | tf_op jit(solution)/shard_map/reduce_sum | solution.py:30
  10.2 0.1 reduce_sum.26
  10.3 0.1 reduce_sum.27
  10.4 0.1 broadcast_in_dim.51
  10.6 0.1 mul.42
  10.7 0.0 copy-done
  10.7 0.4 multiply_convert_fusion
  11.1 0.3 reshape.95
  11.3 0.9 copy.20.second_ref
  12.2 0.9 copy.19.first_ref
  13.1 1.0 gather_fusion
  14.1 0.6 gather.7
  14.7 0.3 fusion.3
  15.0 1.1 reshape.96
  16.1 1.7 %copy.18.pieces_ref = bf16[32,2,6144]{2,1,0:T(2,128)(2,1)} copy(bf16[32,2,6144]{2,0,1:T(8,128)(2,1)S(1)} %reshape.96) | data formatting | bytes 1572864 | tf_op jit(solution)/shard_map/reshape | solution.py:302
  17.8 84.8 %shard_map.73.panel_ref = bf16[512,6144]{1,0:T(8,128)(2,1)} custom-call(bf16[32,2,6144]{2,1,0:T(2,128)(2,1)} %copy.18.pieces_ref), custom_call_target="tpu_custom_call" | custom-call | tf_op jit(solution)/shard_map/pallas_call | solution.py:269
  102.5 0.6 pad_add_fusion.counts_ref
  103.1 29.6 %shard_map.74 = f32[2,9,144,256]{3,2,1,0:T(8,128)} custom-call(s32[3]{0:T(128)} %pad_add_fusion.counts_ref, s32[512,1]{1,0:T(8,128)} %copy.19.first_ref, s32[512,1]{1,0:T(8,128)} %copy.20.second_ref, bf16[512,6144]{1,0:T(8,128)(2,1)} %shard_map.73.panel_ref, bf16[144,2048]{1,0:T(8,128)(2,1)} %constant.50.clone.cos_ref, bf16[144,2048]{1,0:T(8,128)(2,1)} %constant.51.clone.sin_ref), custom_call_target="tpu_custom_call" | custom-call | flops 9160359936 | bytes 8945664 | tf_op jit(solution)/shard_map/pallas_call | solution.py:136
  132.8 5.9 %all-to-all-start = ((f32[2,9,144,256]{3,2,1,0:T(8,128)}), f32[2,9,144,256]{3,2,1,0:T(8,128)S(1)}, u32[]{:S(2)}, u32[]{:S(2)}) async-start(f32[2,9,144,256]{3,2,1,0:T(8,128)} %shard_map.74), calls=%async_computation | async-start | bytes 5308416 | tf_op jit(solution)/shard_map/all_to_all | solution.py:312
  138.7 2.9 %all-to-all-done = f32[2,9,144,256]{3,2,1,0:T(8,128)S(1)} async-done(((f32[2,9,144,256]{3,2,1,0:T(8,128)}), f32[2,9,144,256]{3,2,1,0:T(8,128)S(1)}, u32[]{:S(2)}, u32[]{:S(2)}) %all-to-all-start) | async-done | bytes 2654240 | tf_op jit(solution)/shard_map/all_to_all | solution.py:312
  141.6 1.4 reduce_sum.28
  143.0 2.3 %fusion.4 = bf16[129,9,256]{2,0,1:T(8,128)(2,1)} fusion(f32[9,144,256]{2,1,0:T(8,128)} %reduce_sum.28, pred[256]{0:T(512)(128)(4,1)S(1)} %iota_compare_fusion.1), kind=kLoop, calls=%fused_computation.9 | loop fusion | flops 891648 | bytes 1783552 | tf_op jit(solution)/shard_map/transpose | solution.py:317
  (6 shorter events, 0.0 us)
Async XLA Ops:
  0.0 10.7 %copy-start = (f32[16,3,2,2048]{3,2,1,0:T(2,128)S(1)}, f32[16,3,2,2048]{3,2,1,0:T(2,128)}, u32[]{:S(2)}) copy-start(f32[16,3,2,2048]{3,2,1,0:T(2,128)} %param.7) | copy-start | bytes 2359300
  132.8 8.8 %all-to-all-start = ((f32[2,9,144,256]{3,2,1,0:T(8,128)}), f32[2,9,144,256]{3,2,1,0:T(8,128)S(1)}, u32[]{:S(2)}, u32[]{:S(2)}) async-start(f32[2,9,144,256]{3,2,1,0:T(8,128)} %shard_map.74), calls=%async_computation | async-start | bytes 5308416 | tf_op jit(solution)/shard_map/all_to_all | solution.py:312

commit v6 on v5

--- a/solution.py
+++ b/solution.py
@@ -156,8 +156,9 @@
 MESH_ID = pl.DeviceIdType.MESH
 
 
-def spread_kernel(pieces_ref, panel_ref, send_plane, recv_plane, local_sem, send_right,
-                  send_left, recv_ring, *, ring_size, plane_size, blk_size, slots):
+def spread_kernel(pieces_ref, meta_ref, panel_ref, chip_meta_ref, send_plane, recv_plane,
+                  local_sem, send_right, send_left, recv_ring, meta_sems, *, ring_size,
+                  plane_size, blk_size, slots):
     me_z = lax.axis_index("z")
     me_c = lax.axis_index("core")
     me_b = lax.axis_index("blk")
@@ -179,6 +180,14 @@
     pl.semaphore_signal(barrier, 1, device_id=(right, me_c, me_b), device_id_type=MESH_ID)
     pl.semaphore_signal(barrier, 1, device_id=(left, me_c, me_b), device_id_type=MESH_ID)
     pl.semaphore_wait(barrier, plane_size + 1)
+
+    partner = (me_z, 1 - me_c, me_b)
+    meta_local = pltpu.make_async_copy(meta_ref, chip_meta_ref.at[me_c], meta_sems.at[0])
+    meta_local.start()
+    meta_copy = pltpu.make_async_remote_copy(
+        meta_ref, chip_meta_ref.at[me_c], meta_sems.at[1], meta_sems.at[2],
+        device_id=partner, device_id_type=MESH_ID)
+    meta_copy.start()
 
     block_rows = plane_size * slots
     base = me_z * block_rows
@@ -258,9 +267,14 @@
     part_copy(far, False, send_left.at[0], right).wait_recv()
     for c in sends:
         c.wait_send()
-
-
-def spread(pieces, ring_size, plane_size, blk_size):
+    meta_local.wait()
+    pltpu.make_async_remote_copy(
+        meta_ref, chip_meta_ref.at[1 - me_c], meta_sems.at[1], meta_sems.at[2],
+        device_id=partner, device_id_type=MESH_ID).wait_recv()
+    meta_copy.wait_send()
+
+
+def spread(pieces, meta, ring_size, plane_size, blk_size):
     _, slots, width = pieces.shape
     rows = ring_size * plane_size * slots
     kernel = functools.partial(spread_kernel, ring_size=ring_size, plane_size=plane_size,
@@ -268,9 +282,10 @@
     half = ring_size // 2
     return pl.pallas_call(
         kernel,
-        out_shape=jax.ShapeDtypeStruct((rows, width), pieces.dtype),
-        in_specs=[pl.BlockSpec(memory_space=pl.ANY)],
-        out_specs=pl.BlockSpec(memory_space=pl.ANY),
+        out_shape=(jax.ShapeDtypeStruct((rows, width), pieces.dtype),
+                   jax.ShapeDtypeStruct((2,) + meta.shape, meta.dtype)),
+        in_specs=[pl.BlockSpec(memory_space=pl.ANY), pl.BlockSpec(memory_space=pl.ANY)],
+        out_specs=(pl.BlockSpec(memory_space=pl.ANY), pl.BlockSpec(memory_space=pl.ANY)),
         scratch_shapes=[
             pltpu.SemaphoreType.DMA((plane_size,)),
             pltpu.SemaphoreType.DMA((plane_size,)),
@@ -278,9 +293,10 @@
             pltpu.SemaphoreType.DMA((half,)),
             pltpu.SemaphoreType.DMA((half,)),
             pltpu.SemaphoreType.DMA((ring_size + 1,)),
+            pltpu.SemaphoreType.DMA((3,)),
         ],
         compiler_params=pltpu.CompilerParams(collective_id=0, has_side_effects=True),
-    )(pieces)
+    )(pieces, meta)
 
 
 def shards(spectra, send_rows, send_counts, pair_rows, pair_counts):
@@ -301,17 +317,18 @@
     pieces = picked.reshape(col_count, slot_count, comps * parts, cores, part_bins)
     pieces = jnp.transpose(pieces, (3, 0, 1, 2, 4)).reshape(
         cores * col_count, slot_count, comps * parts * part_bins)
-    panel = spread(pieces, lax.axis_size("z"), cores * col_count, col_count)
-
-    chip_pairs = lax.all_gather(pair_rows, "core", axis=1, tiled=True)
-    chip_counts = lax.all_gather(pair_counts, "core", axis=0, tiled=True)
+    pair_total = pair_rows.shape[1]
+    meta = jnp.concatenate(
+        [pair_rows, jnp.broadcast_to(pair_counts[:, None], (1, pair_total))], axis=0)
+    panel, chip_meta = spread(pieces, meta, lax.axis_size("z"), cores * col_count, col_count)
     cos_rows, sin_rows = lag_tables(bin_count)
-    chip_counts = jnp.concatenate([chip_counts, core.astype(jnp.int32)[None]])
-    partial = pair_sums(chip_counts, chip_pairs[0][:, None], chip_pairs[1][:, None],
+    chip_counts = jnp.concatenate([chip_meta[:, 2, 0], core.astype(jnp.int32)[None]])
+    chip_first = chip_meta[:, 0, :].reshape(cores * pair_total, 1)
+    chip_second = chip_meta[:, 1, :].reshape(cores * pair_total, 1)
+    partial = pair_sums(chip_counts, chip_first, chip_second,
                         panel, cos_rows, sin_rows, cores, 0, None)
     partial = lax.all_to_all(partial, "core", 0, 0, tiled=True)
     total = jnp.sum(partial, axis=0)[:, :LAGS, :] * (1.0 / math.sqrt(bin_count))
-    pair_total = pair_rows.shape[1]
     live = jnp.arange(pair_total, dtype=jnp.int32) < pair_counts[0]
     total = jnp.where(live[None, None, :], total, 0.0).astype(jnp.bfloat16)
     return jnp.transpose(total, (1, 0, 2))

time: 146 us -> 140 us (0.959)
  the two profiles are of different devices: /device:TPU:59 before, /device:TPU:127 now
where the time goes in v6:
time: 140 us; the launch traced here: 139 us
  Pallas kernels  112 us (80%)
  local copies, waits for them, and re-layouts  9.78 us (7%)
  other arithmetic  7.49 us (5%)
  starting transfers between devices  6.31 us (5%)
  waiting for transfers between devices  2.89 us (2%)
    pallas_call x1, Pallas kernels, spread(): pl.pallas_call(kernel, out_shape=(jax.ShapeDtypeStruct((rows, width), pie...  82.4 us
    pallas_call x1, Pallas kernels, pair_sums(): pl.pallas_call(kernel, out_shape=jax.ShapeDtypeStruct((owners, 9, LAG_ROW...  29.6 us
    all_to_all x1, starting transfers between devices, shards(): partial = lax.all_to_all(partial, 'core', 0, 0, tiled=True)  6.31 us
    all_to_all x1, waiting for transfers between devices, shards(): partial = lax.all_to_all(partial, 'core', 0, 0, tiled=True)  2.89 us
  transfers between devices with their start and end apart: 1, of which 1 were waited for; matrix products, arithmetic and copies ran while one was open for 0% of the time, Pallas kernels for 0%

profile of v6, /device:TPU:127, one launch (start us, length us, event | category | flops | bytes accessed | tf_op | source)
XLA Modules:
  0.0 139.3 jit_solution(14010026571238619639)
XLA Ops:
  0.0 0.0 copy-start
  0.0 0.1 subtract_select_fusion
  0.8 0.8 copy.16
  1.5 0.7 compare_and_fusion
  2.2 0.1 reshape_squeeze.12
  2.3 1.7 %multiply_reduce_fusion = f32[16,2048]{1,0:T(8,128)S(1)} fusion(f32[16,3,2,2048]{3,2,1,0:T(2,128)} %param.7), kind=kLoop, calls=%fused_computation.8 | loop fusion | flops 360448 | bytes 917504 | tf_op jit(solution)/shard_map/reduce_sum | solution.py:30
  4.0 0.1 reduce_sum.26
  4.1 0.1 reduce_sum.27
  4.3 0.1 broadcast_in_dim.54
  4.4 0.1 mul.42
  4.6 0.0 copy-done
  4.6 0.4 multiply_convert_fusion
  4.9 0.3 reshape.98
  5.2 1.0 gather_fusion
  6.3 0.6 gather.7
  6.9 0.3 fusion.3
  7.1 0.0 copy-start.1
  7.2 1.1 reshape.99
  8.2 1.7 %copy.18.pieces_ref = bf16[32,2,6144]{2,1,0:T(2,128)(2,1)} copy(bf16[32,2,6144]{2,0,1:T(8,128)(2,1)S(1)} %reshape.99) | data formatting | bytes 1572864 | tf_op jit(solution)/shard_map/reshape | solution.py:318
  9.9 0.0 copy-done.1
  9.9 0.6 concatenate.6.meta_ref
  10.5 82.4 %shard_map.73 = (bf16[512,6144]{1,0:T(8,128)(2,1)}, s32[2,3,256]{2,1,0:T(4,128)}) custom-call(bf16[32,2,6144]{2,1,0:T(2,128)(2,1)} %copy.18.pieces_ref, s32[3,256]{1,0:T(4,128)} %concatenate.6.meta_ref), custom_call_target="tpu_custom_call" | custom-call | tf_op jit(solution)/shard_map/pallas_call | solution.py:283
  92.9 0.8 slice_reduce_fusion
  93.7 0.8 fusion.9
  94.5 0.9 copy.19.first_ref
  95.4 0.9 copy.20.second_ref
  96.3 0.6 pad_add_fusion.counts_ref
  96.8 29.6 %shard_map.74 = f32[2,9,144,256]{3,2,1,0:T(8,128)} custom-call(s32[3]{0:T(128)} %pad_add_fusion.counts_ref, s32[512,1]{1,0:T(8,128)} %copy.19.first_ref, s32[512,1]{1,0:T(8,128)} %copy.20.second_ref, bf16[512,6144]{1,0:T(8,128)(2,1)} %get-tuple-element.8.panel_ref, bf16[144,2048]{1,0:T(8,128)(2,1)} %constant.50.clone.cos_ref, ...), custom_call_target="tpu_custom_call" | custom-call | flops 9160359936 | bytes 8945664 | tf_op jit(solution)/shard_map/pallas_call | solution.py:136
  126.5 6.3 %all-to-all-start = ((f32[2,9,144,256]{3,2,1,0:T(8,128)}), f32[2,9,144,256]{3,2,1,0:T(8,128)S(1)}, u32[]{:S(2)}, u32[]{:S(2)}) async-start(f32[2,9,144,256]{3,2,1,0:T(8,128)} %shard_map.74), calls=%async_computation | async-start | bytes 5308416 | tf_op jit(solution)/shard_map/all_to_all | solution.py:330
  132.8 2.9 %all-to-all-done = f32[2,9,144,256]{3,2,1,0:T(8,128)S(1)} async-done(((f32[2,9,144,256]{3,2,1,0:T(8,128)}), f32[2,9,144,256]{3,2,1,0:T(8,128)S(1)}, u32[]{:S(2)}, u32[]{:S(2)}) %all-to-all-start) | async-done | bytes 2654240 | tf_op jit(solution)/shard_map/all_to_all | solution.py:330
  135.7 1.4 reduce_sum.28
  137.1 2.3 %fusion.4 = bf16[129,9,256]{2,0,1:T(8,128)(2,1)} fusion(f32[9,144,256]{2,1,0:T(8,128)} %reduce_sum.28, pred[256]{0:T(512)(128)(4,1)S(1)} %iota_compare_fusion.1), kind=kLoop, calls=%fused_computation.9 | loop fusion | flops 891648 | bytes 1783552 | tf_op jit(solution)/shard_map/transpose | solution.py:334
  (4 shorter events, 0.0 us)
Async XLA Ops:
  0.0 4.6 %copy-start = (f32[16,3,2,2048]{3,2,1,0:T(2,128)S(1)}, f32[16,3,2,2048]{3,2,1,0:T(2,128)}, u32[]{:S(2)}) copy-start(f32[16,3,2,2048]{3,2,1,0:T(2,128)} %param.7) | copy-start | bytes 2359300
  7.1 2.8 %copy-start.1 = (s32[2,256]{1,0:T(2,128)S(1)}, s32[2,256]{1,0:T(2,128)}, u32[]{:S(2)}) copy-start(s32[2,256]{1,0:T(2,128)} %param.10) | copy-start | bytes 6148
  126.5 9.2 %all-to-all-start = ((f32[2,9,144,256]{3,2,1,0:T(8,128)}), f32[2,9,144,256]{3,2,1,0:T(8,128)S(1)}, u32[]{:S(2)}, u32[]{:S(2)}) async-start(f32[2,9,144,256]{3,2,1,0:T(8,128)} %shard_map.74), calls=%async_computation | async-start | bytes 5308416 | tf_op jit(solution)/shard_map/all_to_all | solution.py:330

commit v7 on v6

--- a/solution.py
+++ b/solution.py
@@ -299,6 +299,37 @@
     )(pieces, meta)
 
 
+def exchange_kernel(part_ref, out_ref, recv_buf, sems, *, scale):
+    me_z = lax.axis_index("z")
+    me_c = lax.axis_index("core")
+    me_b = lax.axis_index("blk")
+    partner = (me_z, 1 - me_c, me_b)
+    barrier = pltpu.get_barrier_semaphore()
+    pl.semaphore_signal(barrier, 1, device_id=partner, device_id_type=MESH_ID)
+    pl.semaphore_wait(barrier, 1)
+    copy = pltpu.make_async_remote_copy(
+        part_ref.at[1 - me_c], recv_buf, sems.at[0], sems.at[1],
+        device_id=partner, device_id_type=MESH_ID)
+    copy.start()
+    copy.wait()
+    out_ref[...] = (part_ref[me_c] + recv_buf[...]) * scale
+
+
+def exchange(partial, scale):
+    shape = partial.shape[1:]
+    return pl.pallas_call(
+        functools.partial(exchange_kernel, scale=scale),
+        out_shape=jax.ShapeDtypeStruct(shape, partial.dtype),
+        in_specs=[pl.BlockSpec(memory_space=pltpu.VMEM)],
+        out_specs=pl.BlockSpec(memory_space=pltpu.VMEM),
+        scratch_shapes=[
+            pltpu.VMEM(shape, partial.dtype),
+            pltpu.SemaphoreType.DMA((2,)),
+        ],
+        compiler_params=pltpu.CompilerParams(collective_id=1, has_side_effects=True),
+    )(partial)
+
+
 def shards(spectra, send_rows, send_counts, pair_rows, pair_counts):
     whitened = whiten(spectra)
     station_count, comps, parts, bin_count = whitened.shape
@@ -327,8 +358,7 @@
     chip_second = chip_meta[:, 1, :].reshape(cores * pair_total, 1)
     partial = pair_sums(chip_counts, chip_first, chip_second,
                         panel, cos_rows, sin_rows, cores, 0, None)
-    partial = lax.all_to_all(partial, "core", 0, 0, tiled=True)
-    total = jnp.sum(partial, axis=0)[:, :LAGS, :] * (1.0 / math.sqrt(bin_count))
+    total = exchange(partial, 1.0 / math.sqrt(bin_count))[:, :LAGS, :]
     live = jnp.arange(pair_total, dtype=jnp.int32) < pair_counts[0]
     total = jnp.where(live[None, None, :], total, 0.0).astype(jnp.bfloat16)
     return jnp.transpose(total, (1, 0, 2))

time: 140 us -> 134 us (0.957)
  the two profiles are of different devices: /device:TPU:127 before, /device:TPU:21 now
where the time goes in v7:
time: 134 us
  Pallas kernels  117 us (87%)
  local copies, waits for them, and re-layouts  10.4 us (8%)
  other arithmetic  6.15 us (5%)
    pallas_call x1, Pallas kernels, spread(): pl.pallas_call(kernel, out_shape=(jax.ShapeDtypeStruct((rows, width), pie...  83.8 us
    pallas_call x1, Pallas kernels, pair_sums(): pl.pallas_call(kernel, out_shape=jax.ShapeDtypeStruct((owners, 9, LAG_ROW...  24.4 us
    pallas_call x1, Pallas kernels, exchange(): pl.pallas_call(functools.partial(exchange_kernel, scale=scale), out_shape...  8.38 us
    reshape x2, local copies, waits for them, and re-layouts, shards(): jnp.transpose(pieces, (3, 0, 1, 2, 4))  2.75 us

profile of v7, /device:TPU:21, one launch (start us, length us, event | category | flops | bytes accessed | tf_op | source)
XLA Modules:
  0.0 134.0 jit_solution(9553904334619502299)
XLA Ops:
  0.0 0.0 copy-start
  0.7 0.7 compare_and_fusion
  1.4 1.3 concatenate.6.meta_ref
  2.7 0.8 copy.16
  3.5 0.1 reshape_squeeze.12
  3.6 0.1 subtract_select_fusion
  3.6 1.7 %multiply_reduce_fusion = f32[16,2048]{1,0:T(8,128)S(1)} fusion(f32[16,3,2,2048]{3,2,1,0:T(2,128)} %param.7), kind=kLoop, calls=%fused_computation.6 | loop fusion | flops 360448 | bytes 917504 | tf_op jit(solution)/shard_map/reduce_sum | solution.py:30
  5.3 0.1 reduce_sum.14
  5.4 0.1 reduce_sum.18
  5.6 0.1 broadcast_in_dim.54
  5.7 0.1 mul.36
  5.9 0.0 copy-done
  5.9 0.4 multiply_convert_fusion
  6.2 0.3 reshape.98
  6.5 1.0 gather_fusion
  7.6 0.6 gather.7
  8.2 0.3 fusion.1
  8.4 1.1 reshape.99
  9.5 1.7 %copy.18.pieces_ref = bf16[32,2,6144]{2,1,0:T(2,128)(2,1)} copy(bf16[32,2,6144]{2,0,1:T(8,128)(2,1)S(1)} %reshape.99) | data formatting | bytes 1572864 | tf_op jit(solution)/shard_map/reshape | solution.py:349
  11.2 83.8 %shard_map.73 = (bf16[512,6144]{1,0:T(8,128)(2,1)}, s32[2,3,256]{2,1,0:T(4,128)}) custom-call(bf16[32,2,6144]{2,1,0:T(2,128)(2,1)} %copy.18.pieces_ref, s32[3,256]{1,0:T(4,128)} %concatenate.6.meta_ref), custom_call_target="tpu_custom_call" | custom-call | tf_op jit(solution)/shard_map/pallas_call | solution.py:283
  95.0 0.8 slice_reduce_fusion
  95.8 0.8 fusion.7
  96.6 0.7 pad_add_fusion.counts_ref
  97.3 0.9 copy.19.first_ref
  98.1 0.9 copy.20.second_ref
  99.0 24.4 %shard_map.74.part_ref = f32[2,9,144,256]{3,2,1,0:T(8,128)} custom-call(s32[3]{0:T(128)} %pad_add_fusion.counts_ref, s32[512,1]{1,0:T(8,128)} %copy.19.first_ref, s32[512,1]{1,0:T(8,128)} %copy.20.second_ref, bf16[512,6144]{1,0:T(8,128)(2,1)} %get-tuple-element.8.panel_ref, bf16[144,2048]{1,0:T(8,128)(2,1)} %constant.48.clone.cos_ref, ...), custom_call_target="tpu_custom_call" | custom-call | flops 9160359936 | bytes 8945664 | tf_op jit(solution)/shard_map/pallas_call | solution.py:136
  123.4 8.4 %shard_map.75 = f32[9,144,256]{2,1,0:T(8,128)} custom-call(f32[2,9,144,256]{3,2,1,0:T(8,128)} %shard_map.74.part_ref), custom_call_target="tpu_custom_call" | custom-call | tf_op jit(solution)/shard_map/pallas_call | solution.py:320
  131.8 2.2 %fusion.2 = bf16[129,9,256]{2,0,1:T(8,128)(2,1)} fusion(f32[9,144,256]{2,1,0:T(8,128)} %shard_map.75, pred[256]{0:T(512)(128)(4,1)S(1)} %iota_compare_fusion.1), kind=kLoop, calls=%fused_computation.7 | loop fusion | flops 297216 | bytes 1189120 | tf_op jit(solution)/shard_map/transpose | solution.py:364
  (4 shorter events, 0.0 us)
Async XLA Ops:
  0.0 5.9 %copy-start = (f32[16,3,2,2048]{3,2,1,0:T(2,128)S(1)}, f32[16,3,2,2048]{3,2,1,0:T(2,128)}, u32[]{:S(2)}) copy-start(f32[16,3,2,2048]{3,2,1,0:T(2,128)} %param.7) | copy-start | bytes 2359300

commit v8 on v7

--- a/solution.py
+++ b/solution.py
@@ -16,6 +16,7 @@
 PAIR_BLOCK = 128
 BIN_CHUNK = 256
 GATHER_CHUNK = 512
+SUBS = 2
 
 
 def whiten(spectra):
@@ -79,28 +80,31 @@
 
         lax.fori_loop(0, width // gather_chunk, gather, 0)
         nt = (((1,), (1,)), ((), ()))
-        bin_chunk = min(BIN_CHUNK, part_bins)
-
-        def chunk(kc, carry):
-            off = pl.multiple_of(kc * bin_chunk, bin_chunk)
-            cos_blk = cos_ref[:, pl.ds(off, bin_chunk)]
-            sin_blk = sin_ref[:, pl.ds(off, bin_chunk)]
-            for a in range(3):
-                f_re = f_scr[:, pl.ds(2 * a * part_bins + off, bin_chunk)]
-                f_im = f_scr[:, pl.ds((2 * a + 1) * part_bins + off, bin_chunk)]
-                for b in range(3):
-                    s_re = s_scr[:, pl.ds(2 * b * part_bins + off, bin_chunk)]
-                    s_im = s_scr[:, pl.ds((2 * b + 1) * part_bins + off, bin_chunk)]
-                    real_part = (f_re * s_re + f_im * s_im).astype(jnp.bfloat16)
-                    imag_part = (f_im * s_re - f_re * s_im).astype(jnp.bfloat16)
-                    acc = lax.dot_general(cos_blk, real_part, nt,
-                                          preferred_element_type=jnp.float32)
-                    acc = acc + lax.dot_general(sin_blk, imag_part, nt,
-                                                preferred_element_type=jnp.float32)
-                    out_ref[0, 3 * a + b] += acc
-            return carry
-
-        lax.fori_loop(0, part_bins // bin_chunk, chunk, 0)
+        sub_bins = part_bins // SUBS
+        bin_chunk = min(BIN_CHUNK, sub_bins)
+        for sub in range(SUBS):
+            col0 = sub * 6 * sub_bins
+
+            def chunk(kc, carry):
+                off = pl.multiple_of(kc * bin_chunk, bin_chunk)
+                cos_blk = cos_ref[:, pl.ds(sub * sub_bins + off, bin_chunk)]
+                sin_blk = sin_ref[:, pl.ds(sub * sub_bins + off, bin_chunk)]
+                for a in range(3):
+                    f_re = f_scr[:, pl.ds(col0 + 2 * a * sub_bins + off, bin_chunk)]
+                    f_im = f_scr[:, pl.ds(col0 + (2 * a + 1) * sub_bins + off, bin_chunk)]
+                    for b in range(3):
+                        s_re = s_scr[:, pl.ds(col0 + 2 * b * sub_bins + off, bin_chunk)]
+                        s_im = s_scr[:, pl.ds(col0 + (2 * b + 1) * sub_bins + off, bin_chunk)]
+                        real_part = (f_re * s_re + f_im * s_im).astype(jnp.bfloat16)
+                        imag_part = (f_im * s_re - f_re * s_im).astype(jnp.bfloat16)
+                        acc = lax.dot_general(cos_blk, real_part, nt,
+                                              preferred_element_type=jnp.float32)
+                        acc = acc + lax.dot_general(sin_blk, imag_part, nt,
+                                                    preferred_element_type=jnp.float32)
+                        out_ref[0, 3 * a + b] += acc
+                return carry
+
+            lax.fori_loop(0, sub_bins // bin_chunk, chunk, 0)
 
 
 def pair_sums(counts, first_idx, second_idx, panel, cos_rows, sin_rows, owners, chunk_id, acc):
@@ -158,7 +162,7 @@
 
 def spread_kernel(pieces_ref, meta_ref, panel_ref, chip_meta_ref, send_plane, recv_plane,
                   local_sem, send_right, send_left, recv_ring, meta_sems, *, ring_size,
-                  plane_size, blk_size, slots):
+                  plane_size, blk_size, slots, subs):
     me_z = lax.axis_index("z")
     me_c = lax.axis_index("core")
     me_b = lax.axis_index("blk")
@@ -189,82 +193,100 @@
         device_id=partner, device_id_type=MESH_ID)
     meta_copy.start()
 
+    sub_width = panel_ref.shape[1] // subs
     block_rows = plane_size * slots
+    half_rows = block_rows // 2
     base = me_z * block_rows
-
-    def rows_of(q):
-        return panel_ref.at[pl.ds(base + q * slots, slots)]
-
-    local = pltpu.make_async_copy(pieces_ref.at[me_q], rows_of(me_q), local_sem)
-    local.start()
-
-    def plane_copy(q, src_q, dst_q):
+    half = ring_size // 2
+
+    def cols(sub):
+        return pl.ds(sub * sub_width, sub_width)
+
+    def rows_of(q, sub):
+        return panel_ref.at[pl.ds(base + q * slots, slots), cols(sub)]
+
+    def local_copy(sub):
+        return pltpu.make_async_copy(
+            pieces_ref.at[me_q, :, cols(sub)], rows_of(me_q, sub), local_sem.at[sub])
+
+    def plane_copy(q, src_q, sub):
         return pltpu.make_async_remote_copy(
-            pieces_ref.at[q], rows_of(dst_q), send_plane.at[q], recv_plane.at[src_q],
-            device_id=plane_dev(q), device_id_type=MESH_ID)
-
-    def send(i, carry):
-        q = (me_q + i) % plane_size
-        plane_copy(q, me_q, me_q).start()
-        return carry
-
-    lax.fori_loop(1, plane_size, send, 0)
-
-    def arrive(i, carry):
-        q = (me_q + plane_size - i) % plane_size
-        plane_copy(q, q, q).wait_recv()
-        return carry
-
-    lax.fori_loop(1, plane_size, arrive, 0)
-    local.wait()
-
-    def sent(i, carry):
-        q = (me_q + i) % plane_size
-        plane_copy(q, me_q, me_q).wait_send()
-        return carry
-
-    lax.fori_loop(1, plane_size, sent, 0)
-
-    def block_of(k):
-        return panel_ref.at[pl.ds(k * block_rows, block_rows)]
-
-    def ring_copy(k, sem, dev):
+            pieces_ref.at[q, :, cols(sub)], rows_of(src_q, sub), send_plane.at[sub, q],
+            recv_plane.at[sub, src_q], device_id=plane_dev(q), device_id_type=MESH_ID)
+
+    def scatter(sub):
+        local_copy(sub).start()
+
+        def send(i, carry):
+            q = (me_q + i) % plane_size
+            plane_copy(q, me_q, sub).start()
+            return carry
+
+        lax.fori_loop(1, plane_size, send, 0)
+
+    def gathered(sub):
+        def arrive(i, carry):
+            q = (me_q + plane_size - i) % plane_size
+            plane_copy(q, q, sub).wait_recv()
+            return carry
+
+        lax.fori_loop(1, plane_size, arrive, 0)
+        local_copy(sub).wait()
+
+    def block_of(k, sub):
+        return panel_ref.at[pl.ds(k * block_rows, block_rows), cols(sub)]
+
+    def part_of(k, first, sub):
+        start = k * block_rows + (0 if first else half_rows)
+        return panel_ref.at[pl.ds(start, half_rows), cols(sub)]
+
+    def ring_copy(k, sem, dev, sub):
         return pltpu.make_async_remote_copy(
-            block_of(k), block_of(k), sem, recv_ring.at[k],
+            block_of(k, sub), block_of(k, sub), sem, recv_ring.at[sub, k],
             device_id=(dev, me_c, me_b), device_id_type=MESH_ID)
 
-    half = ring_size // 2
-    half_rows = block_rows // 2
-
-    def part_of(k, first):
-        start = k * block_rows + (0 if first else half_rows)
-        return panel_ref.at[pl.ds(start, half_rows)]
-
-    def part_copy(k, first, sem, dev):
+    def part_copy(k, first, sem, dev, sub):
         slot = k if first else ring_size
         return pltpu.make_async_remote_copy(
-            part_of(k, first), part_of(k, first), sem, recv_ring.at[slot],
+            part_of(k, first, sub), part_of(k, first, sub), sem, recv_ring.at[sub, slot],
             device_id=(dev, me_c, me_b), device_id_type=MESH_ID)
 
     sends = []
-    for s in range(half):
+
+    def ring_step(s, sub):
         k = (me_z + ring_size - s) % ring_size
         if s > 0:
-            ring_copy(k, send_right.at[s], left).wait_recv()
-        c = ring_copy(k, send_right.at[s], right) if s < half - 1 else part_copy(
-            k, True, send_right.at[s], right)
+            ring_copy(k, send_right.at[sub, s], left, sub).wait_recv()
+        c = ring_copy(k, send_right.at[sub, s], right, sub) if s < half - 1 else part_copy(
+            k, True, send_right.at[sub, s], right, sub)
         c.start()
         sends.append(c)
         k = (me_z + s) % ring_size
         if s > 0:
-            ring_copy(k, send_left.at[s], right).wait_recv()
-        c = ring_copy(k, send_left.at[s], left) if s < half - 1 else part_copy(
-            k, False, send_left.at[s], left)
+            ring_copy(k, send_left.at[sub, s], right, sub).wait_recv()
+        c = ring_copy(k, send_left.at[sub, s], left, sub) if s < half - 1 else part_copy(
+            k, False, send_left.at[sub, s], left, sub)
         c.start()
         sends.append(c)
+
+    for sub in range(subs):
+        scatter(sub)
+        gathered(sub)
+        ring_step(0, sub)
+    for s in range(1, half):
+        for sub in range(subs):
+            ring_step(s, sub)
     far = (me_z + half) % ring_size
-    part_copy(far, True, send_right.at[0], left).wait_recv()
-    part_copy(far, False, send_left.at[0], right).wait_recv()
+    for sub in range(subs):
+        part_copy(far, True, send_right.at[sub, 0], left, sub).wait_recv()
+        part_copy(far, False, send_left.at[sub, 0], right, sub).wait_recv()
+    for sub in range(subs):
+        def sent(i, carry):
+            q = (me_q + i) % plane_size
+            plane_copy(q, me_q, sub).wait_send()
+            return carry
+
+        lax.fori_loop(1, plane_size, sent, 0)
     for c in sends:
         c.wait_send()
     meta_local.wait()
@@ -278,7 +300,7 @@
     _, slots, width = pieces.shape
     rows = ring_size * plane_size * slots
     kernel = functools.partial(spread_kernel, ring_size=ring_size, plane_size=plane_size,
-                               blk_size=blk_size, slots=slots)
+                               blk_size=blk_size, slots=slots, subs=SUBS)
     half = ring_size // 2
     return pl.pallas_call(
         kernel,
@@ -287,12 +309,12 @@
         in_specs=[pl.BlockSpec(memory_space=pl.ANY), pl.BlockSpec(memory_space=pl.ANY)],
         out_specs=(pl.BlockSpec(memory_space=pl.ANY), pl.BlockSpec(memory_space=pl.ANY)),
         scratch_shapes=[
-            pltpu.SemaphoreType.DMA((plane_size,)),
-            pltpu.SemaphoreType.DMA((plane_size,)),
-            pltpu.SemaphoreType.DMA(()),
-            pltpu.SemaphoreType.DMA((half,)),
-            pltpu.SemaphoreType.DMA((half,)),
-            pltpu.SemaphoreType.DMA((ring_size + 1,)),
+            pltpu.SemaphoreType.DMA((SUBS, plane_size)),
+            pltpu.SemaphoreType.DMA((SUBS, plane_size)),
+            pltpu.SemaphoreType.DMA((SUBS,)),
+            pltpu.SemaphoreType.DMA((SUBS, half)),
+            pltpu.SemaphoreType.DMA((SUBS, half)),
+            pltpu.SemaphoreType.DMA((SUBS, ring_size + 1)),
             pltpu.SemaphoreType.DMA((3,)),
         ],
         compiler_params=pltpu.CompilerParams(collective_id=0, has_side_effects=True),
@@ -345,8 +367,9 @@
     picked = jnp.take(flat, lists.reshape(-1), axis=0).reshape(col_count, slot_count, row_width)
     alive = jnp.arange(slot_count, dtype=jnp.int32)[None, :] < send_counts[0][:, None]
     picked = jnp.where(alive[:, :, None], picked, jnp.zeros_like(picked))
-    pieces = picked.reshape(col_count, slot_count, comps * parts, cores, part_bins)
-    pieces = jnp.transpose(pieces, (3, 0, 1, 2, 4)).reshape(
+    pieces = picked.reshape(col_count, slot_count, comps * parts, cores, SUBS,
+                            part_bins // SUBS)
+    pieces = jnp.transpose(pieces, (3, 0, 1, 4, 2, 5)).reshape(
         cores * col_count, slot_count, comps * parts * part_bins)
     pair_total = pair_rows.shape[1]
     meta = jnp.concatenate(

time: 134 us -> 130 us (0.970)
  the two profiles are of different devices: /device:TPU:21 before, /device:TPU:119 now
where the time goes in v8:
time: 130 us
  Pallas kernels  112 us (86%)
  local copies, waits for them, and re-layouts  10.3 us (8%)
  other arithmetic  6.15 us (5%)
    pallas_call x1, Pallas kernels, spread(): pl.pallas_call(kernel, out_shape=(jax.ShapeDtypeStruct((rows, width), pie...  76.4 us
    pallas_call x1, Pallas kernels, pair_sums(): pl.pallas_call(kernel, out_shape=jax.ShapeDtypeStruct((owners, 9, LAG_ROW...  29.7 us
    pallas_call x1, Pallas kernels, exchange(): pl.pallas_call(functools.partial(exchange_kernel, scale=scale), out_shape...  6.37 us
    reshape x2, local copies, waits for them, and re-layouts, shards(): jnp.transpose(pieces, (3, 0, 1, 4, 2, 5))  2.63 us

profile of v8, /device:TPU:119, one launch (start us, length us, event | category | flops | bytes accessed | tf_op | source)
XLA Modules:
  0.0 129.8 jit_solution(13104093049862555177)
XLA Ops:
  0.0 0.0 copy-start
  0.7 0.7 compare_and_fusion
  1.4 1.3 concatenate.6.meta_ref
  2.7 0.8 copy.16
  3.5 0.1 reshape_squeeze.12
  3.6 0.1 subtract_select_fusion
  3.6 1.7 %multiply_reduce_fusion = f32[16,2048]{1,0:T(8,128)S(1)} fusion(f32[16,3,2,2048]{3,2,1,0:T(2,128)} %param.7), kind=kLoop, calls=%fused_computation.6 | loop fusion | flops 360448 | bytes 917504 | tf_op jit(solution)/shard_map/reduce_sum | solution.py:31
  5.3 0.1 reduce_sum.14
  5.4 0.1 reduce_sum.18
  5.6 0.1 broadcast_in_dim.54
  5.7 0.1 mul.36
  5.9 0.0 copy-done
  5.9 0.4 multiply_convert_fusion
  6.2 0.3 reshape.98
  6.5 1.0 gather_fusion
  7.6 0.6 gather.7
  8.2 0.3 fusion.1
  8.4 0.9 reshape.99
  9.4 1.7 %copy.18.pieces_ref = bf16[32,2,6144]{2,1,0:T(2,128)(2,1)} copy(bf16[32,2,6144]{2,0,1:T(8,128)(2,1)S(1)} %reshape.99) | data formatting | bytes 1572864 | tf_op jit(solution)/shard_map/reshape | solution.py:372
  11.1 76.4 %shard_map.73 = (bf16[512,6144]{1,0:T(8,128)(2,1)}, s32[2,3,256]{2,1,0:T(4,128)}) custom-call(bf16[32,2,6144]{2,1,0:T(2,128)(2,1)} %copy.18.pieces_ref, s32[3,256]{1,0:T(4,128)} %concatenate.6.meta_ref), custom_call_target="tpu_custom_call" | custom-call | tf_op jit(solution)/shard_map/pallas_call | solution.py:305
  87.5 0.8 slice_reduce_fusion
  88.3 0.8 fusion.7
  89.1 0.7 pad_add_fusion.counts_ref
  89.8 0.9 copy.19.first_ref
  90.6 0.9 copy.20.second_ref
  91.5 29.7 %shard_map.74.part_ref = f32[2,9,144,256]{3,2,1,0:T(8,128)} custom-call(s32[3]{0:T(128)} %pad_add_fusion.counts_ref, s32[512,1]{1,0:T(8,128)} %copy.19.first_ref, s32[512,1]{1,0:T(8,128)} %copy.20.second_ref, bf16[512,6144]{1,0:T(8,128)(2,1)} %get-tuple-element.8.panel_ref, bf16[144,2048]{1,0:T(8,128)(2,1)} %constant.48.clone.cos_ref, ...), custom_call_target="tpu_custom_call" | custom-call | flops 9160359936 | bytes 8945664 | tf_op jit(solution)/shard_map/pallas_call | solution.py:140
  121.2 6.4 %shard_map.75 = f32[9,144,256]{2,1,0:T(8,128)} custom-call(f32[2,9,144,256]{3,2,1,0:T(8,128)} %shard_map.74.part_ref), custom_call_target="tpu_custom_call" | custom-call | tf_op jit(solution)/shard_map/pallas_call | solution.py:342
  127.5 2.2 %fusion.2 = bf16[129,9,256]{2,0,1:T(8,128)(2,1)} fusion(f32[9,144,256]{2,1,0:T(8,128)} %shard_map.75, pred[256]{0:T(512)(128)(4,1)S(1)} %iota_compare_fusion.1), kind=kLoop, calls=%fused_computation.7 | loop fusion | flops 297216 | bytes 1189120 | tf_op jit(solution)/shard_map/transpose | solution.py:387
  (4 shorter events, 0.0 us)
Async XLA Ops:
  0.0 5.9 %copy-start = (f32[16,3,2,2048]{3,2,1,0:T(2,128)S(1)}, f32[16,3,2,2048]{3,2,1,0:T(2,128)}, u32[]{:S(2)}) copy-start(f32[16,3,2,2048]{3,2,1,0:T(2,128)} %param.7) | copy-start | bytes 2359300

commit v9 on v8

--- a/solution.py
+++ b/solution.py
@@ -16,7 +16,7 @@
 PAIR_BLOCK = 128
 BIN_CHUNK = 256
 GATHER_CHUNK = 512
-SUBS = 2
+SUBS = 4
 
 
 def whiten(spectra):

time: 130 us -> 135 us (1.038)
  the two profiles are of different devices: /device:TPU:119 before, /device:TPU:65 now
where the time goes in v9:
time: 135 us; the launch traced here: 134 us
  Pallas kernels  117 us (87%)
  local copies, waits for them, and re-layouts  10.2 us (8%)
  other arithmetic  6.15 us (5%)
    pallas_call x1, Pallas kernels, spread(): pl.pallas_call(kernel, out_shape=(jax.ShapeDtypeStruct((rows, width), pie...  81.3 us
    pallas_call x1, Pallas kernels, pair_sums(): pl.pallas_call(kernel, out_shape=jax.ShapeDtypeStruct((owners, 9, LAG_ROW...  28.1 us
    pallas_call x1, Pallas kernels, exchange(): pl.pallas_call(functools.partial(exchange_kernel, scale=scale), out_shape...  7.69 us

profile of v9, /device:TPU:65, one launch (start us, length us, event | category | flops | bytes accessed | tf_op | source)
XLA Modules:
  0.0 134.3 jit_solution(18116483961941064980)
XLA Ops:
  0.0 0.0 copy-start
  0.7 0.7 compare_and_fusion
  1.4 1.3 concatenate.6.meta_ref
  2.7 0.8 copy.16
  3.5 0.1 reshape_squeeze.12
  3.6 0.1 subtract_select_fusion
  3.6 1.7 %multiply_reduce_fusion = f32[16,2048]{1,0:T(8,128)S(1)} fusion(f32[16,3,2,2048]{3,2,1,0:T(2,128)} %param.7), kind=kLoop, calls=%fused_computation.6 | loop fusion | flops 360448 | bytes 917504 | tf_op jit(solution)/shard_map/reduce_sum | solution.py:31
  5.3 0.1 reduce_sum.14
  5.4 0.1 reduce_sum.18
  5.6 0.1 broadcast_in_dim.54
  5.7 0.1 mul.36
  5.9 0.0 copy-done
  5.9 0.4 multiply_convert_fusion
  6.2 0.3 reshape.98
  6.5 1.0 gather_fusion
  7.6 0.6 gather.7
  8.2 0.3 fusion.1
  8.4 0.8 reshape.99
  9.3 1.7 %copy.18.pieces_ref = bf16[32,2,6144]{2,1,0:T(2,128)(2,1)} copy(bf16[32,2,6144]{2,0,1:T(8,128)(2,1)S(1)} %reshape.99) | data formatting | bytes 1572864 | tf_op jit(solution)/shard_map/reshape | solution.py:372
  11.0 81.3 %shard_map.73 = (bf16[512,6144]{1,0:T(8,128)(2,1)}, s32[2,3,256]{2,1,0:T(4,128)}) custom-call(bf16[32,2,6144]{2,1,0:T(2,128)(2,1)} %copy.18.pieces_ref, s32[3,256]{1,0:T(4,128)} %concatenate.6.meta_ref), custom_call_target="tpu_custom_call" | custom-call | tf_op jit(solution)/shard_map/pallas_call | solution.py:305
  92.3 0.8 slice_reduce_fusion
  93.1 0.8 fusion.7
  93.9 0.7 pad_add_fusion.counts_ref
  94.6 0.9 copy.19.first_ref
  95.4 0.9 copy.20.second_ref
  96.3 28.1 %shard_map.74.part_ref = f32[2,9,144,256]{3,2,1,0:T(8,128)} custom-call(s32[3]{0:T(128)} %pad_add_fusion.counts_ref, s32[512,1]{1,0:T(8,128)} %copy.19.first_ref, s32[512,1]{1,0:T(8,128)} %copy.20.second_ref, bf16[512,6144]{1,0:T(8,128)(2,1)} %get-tuple-element.8.panel_ref, bf16[144,2048]{1,0:T(8,128)(2,1)} %constant.48.clone.cos_ref, ...), custom_call_target="tpu_custom_call" | custom-call | flops 9160359936 | bytes 8945664 | tf_op jit(solution)/shard_map/pallas_call | solution.py:140
  124.4 7.7 %shard_map.75 = f32[9,144,256]{2,1,0:T(8,128)} custom-call(f32[2,9,144,256]{3,2,1,0:T(8,128)} %shard_map.74.part_ref), custom_call_target="tpu_custom_call" | custom-call | tf_op jit(solution)/shard_map/pallas_call | solution.py:342
  132.1 2.2 %fusion.2 = bf16[129,9,256]{2,0,1:T(8,128)(2,1)} fusion(f32[9,144,256]{2,1,0:T(8,128)} %shard_map.75, pred[256]{0:T(512)(128)(4,1)S(1)} %iota_compare_fusion.1), kind=kLoop, calls=%fused_computation.7 | loop fusion | flops 297216 | bytes 1189120 | tf_op jit(solution)/shard_map/transpose | solution.py:387
  (4 shorter events, 0.0 us)
Async XLA Ops:
  0.0 5.9 %copy-start = (f32[16,3,2,2048]{3,2,1,0:T(2,128)S(1)}, f32[16,3,2,2048]{3,2,1,0:T(2,128)}, u32[]{:S(2)}) copy-start(f32[16,3,2,2048]{3,2,1,0:T(2,128)} %param.7) | copy-start | bytes 2359300

commit v10 on v8

--- a/solution.py
+++ b/solution.py
@@ -45,7 +45,7 @@
     return jnp.asarray(cos_rows), jnp.asarray(sin_rows)
 
 
-def pair_kernel(counts_ref, first_ref, second_ref, panel_ref, cos_ref, sin_ref, *rest,
+def pair_kernel(counts_ref, core_ref, pairs_ref, panel_ref, cos_ref, sin_ref, *rest,
                 blocks_per_owner, part_bins, accumulate):
     if accumulate:
         acc_ref, out_ref, f_scr, s_scr = rest
@@ -54,7 +54,7 @@
     step = pl.program_id(0)
     owner = step // blocks_per_owner
     start = (step % blocks_per_owner) * PAIR_BLOCK
-    live = start < counts_ref[owner]
+    live = start < counts_ref[owner, 0]
     if accumulate:
         out_ref[...] = acc_ref[...]
     else:
@@ -64,9 +64,10 @@
     def _():
         rows = panel_ref.shape[0]
         width = panel_ref.shape[1]
-        iota = lax.broadcasted_iota(jnp.int32, (PAIR_BLOCK, rows), 1)
-        pick_first = (first_ref[...] == iota).astype(jnp.bfloat16)
-        pick_second = (second_ref[...] == iota).astype(jnp.bfloat16)
+        iota = lax.broadcasted_iota(jnp.int32, (rows, PAIR_BLOCK), 0)
+        idx = pairs_ref[0]
+        pick_first = jnp.where(idx[0:1, :] == iota, 1.0, 0.0).T.astype(jnp.bfloat16)
+        pick_second = jnp.where(idx[1:2, :] == iota, 1.0, 0.0).T.astype(jnp.bfloat16)
         gather_chunk = min(GATHER_CHUNK, width)
 
         def gather(c, carry):
@@ -107,10 +108,10 @@
             lax.fori_loop(0, sub_bins // bin_chunk, chunk, 0)
 
 
-def pair_sums(counts, first_idx, second_idx, panel, cos_rows, sin_rows, owners, chunk_id, acc):
+def pair_sums(counts, core_arr, chip_pairs, panel, cos_rows, sin_rows, owners, chunk_id, acc):
     rows, width = panel.shape
     part_bins = width // 6
-    pairs = first_idx.shape[0]
+    pairs = chip_pairs.shape[0] * chip_pairs.shape[2]
     per_owner = pairs // owners
     blocks_per_owner = per_owner // PAIR_BLOCK
     grid = (pairs // PAIR_BLOCK,)
@@ -123,15 +124,15 @@
                            bytes_accessed=rows * width * 2 + out_bytes * (2 if accumulate else 1))
     out_spec = pl.BlockSpec(
         (1, 9, LAG_ROWS, PAIR_BLOCK),
-        lambda i, c: (i // blocks_per_owner, 0, 0, i % blocks_per_owner))
+        lambda i, c, k: (i // blocks_per_owner, 0, 0, i % blocks_per_owner))
     in_specs = [
-        pl.BlockSpec((PAIR_BLOCK, 1), lambda i, c: (i, 0)),
-        pl.BlockSpec((PAIR_BLOCK, 1), lambda i, c: (i, 0)),
-        pl.BlockSpec((rows, width), lambda i, c: (0, 0)),
-        pl.BlockSpec((LAG_ROWS, part_bins), lambda i, c: (0, c[owners])),
-        pl.BlockSpec((LAG_ROWS, part_bins), lambda i, c: (0, c[owners])),
+        pl.BlockSpec((1, 2, PAIR_BLOCK),
+                     lambda i, c, k: (i // blocks_per_owner, 0, i % blocks_per_owner)),
+        pl.BlockSpec((rows, width), lambda i, c, k: (0, 0)),
+        pl.BlockSpec((LAG_ROWS, part_bins), lambda i, c, k: (0, k[0])),
+        pl.BlockSpec((LAG_ROWS, part_bins), lambda i, c, k: (0, k[0])),
     ]
-    args = [counts, first_idx, second_idx, panel, cos_rows, sin_rows]
+    args = [counts, core_arr, chip_pairs, panel, cos_rows, sin_rows]
     aliases = {}
     if accumulate:
         in_specs.append(out_spec)
@@ -141,7 +142,7 @@
         kernel,
         out_shape=jax.ShapeDtypeStruct((owners, 9, LAG_ROWS, per_owner), jnp.float32),
         grid_spec=pltpu.PrefetchScalarGridSpec(
-            num_scalar_prefetch=1,
+            num_scalar_prefetch=2,
             grid=grid,
             in_specs=in_specs,
             out_specs=out_spec,
@@ -160,7 +161,8 @@
 MESH_ID = pl.DeviceIdType.MESH
 
 
-def spread_kernel(pieces_ref, meta_ref, panel_ref, chip_meta_ref, send_plane, recv_plane,
+def spread_kernel(pieces_ref, rows_ref, count_ref, panel_ref, chip_rows_ref, chip_count_ref,
+                  send_plane, recv_plane,
                   local_sem, send_right, send_left, recv_ring, meta_sems, *, ring_size,
                   plane_size, blk_size, slots, subs):
     me_z = lax.axis_index("z")
@@ -186,12 +188,18 @@
     pl.semaphore_wait(barrier, plane_size + 1)
 
     partner = (me_z, 1 - me_c, me_b)
-    meta_local = pltpu.make_async_copy(meta_ref, chip_meta_ref.at[me_c], meta_sems.at[0])
-    meta_local.start()
-    meta_copy = pltpu.make_async_remote_copy(
-        meta_ref, chip_meta_ref.at[me_c], meta_sems.at[1], meta_sems.at[2],
-        device_id=partner, device_id_type=MESH_ID)
-    meta_copy.start()
+    meta_copies = []
+    for idx, (src, dst) in enumerate(((rows_ref, chip_rows_ref), (count_ref, chip_count_ref))):
+        local = pltpu.make_async_copy(src, dst.at[me_c], meta_sems.at[3 * idx])
+        local.start()
+        remote = pltpu.make_async_remote_copy(
+            src, dst.at[me_c], meta_sems.at[3 * idx + 1], meta_sems.at[3 * idx + 2],
+            device_id=partner, device_id_type=MESH_ID)
+        remote.start()
+        arrival = pltpu.make_async_remote_copy(
+            src, dst.at[1 - me_c], meta_sems.at[3 * idx + 1], meta_sems.at[3 * idx + 2],
+            device_id=partner, device_id_type=MESH_ID)
+        meta_copies.append((local, remote, arrival))
 
     sub_width = panel_ref.shape[1] // subs
     block_rows = plane_size * slots
@@ -289,14 +297,13 @@
         lax.fori_loop(1, plane_size, sent, 0)
     for c in sends:
         c.wait_send()
-    meta_local.wait()
-    pltpu.make_async_remote_copy(
-        meta_ref, chip_meta_ref.at[1 - me_c], meta_sems.at[1], meta_sems.at[2],
-        device_id=partner, device_id_type=MESH_ID).wait_recv()
-    meta_copy.wait_send()
-
-
-def spread(pieces, meta, ring_size, plane_size, blk_size):
+    for local, remote, arrival in meta_copies:
+        local.wait()
+        arrival.wait_recv()
+        remote.wait_send()
+
+
+def spread(pieces, pair_rows, pair_counts, ring_size, plane_size, blk_size):
     _, slots, width = pieces.shape
     rows = ring_size * plane_size * slots
     kernel = functools.partial(spread_kernel, ring_size=ring_size, plane_size=plane_size,
@@ -305,9 +312,10 @@
     return pl.pallas_call(
         kernel,
         out_shape=(jax.ShapeDtypeStruct((rows, width), pieces.dtype),
-                   jax.ShapeDtypeStruct((2,) + meta.shape, meta.dtype)),
-        in_specs=[pl.BlockSpec(memory_space=pl.ANY), pl.BlockSpec(memory_space=pl.ANY)],
-        out_specs=(pl.BlockSpec(memory_space=pl.ANY), pl.BlockSpec(memory_space=pl.ANY)),
+                   jax.ShapeDtypeStruct((2,) + pair_rows.shape, pair_rows.dtype),
+                   jax.ShapeDtypeStruct((2,) + pair_counts.shape, pair_counts.dtype)),
+        in_specs=[pl.BlockSpec(memory_space=pl.ANY)] * 3,
+        out_specs=(pl.BlockSpec(memory_space=pl.ANY),) * 3,
         scratch_shapes=[
             pltpu.SemaphoreType.DMA((SUBS, plane_size)),
             pltpu.SemaphoreType.DMA((SUBS, plane_size)),
@@ -315,10 +323,10 @@
             pltpu.SemaphoreType.DMA((SUBS, half)),
             pltpu.SemaphoreType.DMA((SUBS, half)),
             pltpu.SemaphoreType.DMA((SUBS, ring_size + 1)),
-            pltpu.SemaphoreType.DMA((3,)),
+            pltpu.SemaphoreType.DMA((6,)),
         ],
         compiler_params=pltpu.CompilerParams(collective_id=0, has_side_effects=True),
-    )(pieces, meta)
+    )(pieces, pair_rows, pair_counts)
 
 
 def exchange_kernel(part_ref, out_ref, recv_buf, sems, *, scale):
@@ -372,15 +380,12 @@
     pieces = jnp.transpose(pieces, (3, 0, 1, 4, 2, 5)).reshape(
         cores * col_count, slot_count, comps * parts * part_bins)
     pair_total = pair_rows.shape[1]
-    meta = jnp.concatenate(
-        [pair_rows, jnp.broadcast_to(pair_counts[:, None], (1, pair_total))], axis=0)
-    panel, chip_meta = spread(pieces, meta, lax.axis_size("z"), cores * col_count, col_count)
+    panel, chip_pairs, chip_counts = spread(pieces, pair_rows, pair_counts, lax.axis_size("z"),
+                                            cores * col_count, col_count)
     cos_rows, sin_rows = lag_tables(bin_count)
-    chip_counts = jnp.concatenate([chip_meta[:, 2, 0], core.astype(jnp.int32)[None]])
-    chip_first = chip_meta[:, 0, :].reshape(cores * pair_total, 1)
-    chip_second = chip_meta[:, 1, :].reshape(cores * pair_total, 1)
-    partial = pair_sums(chip_counts, chip_first, chip_second,
-                        panel, cos_rows, sin_rows, cores, 0, None)
+    core_arr = core.astype(jnp.int32)[None]
+    partial = pair_sums(chip_counts, core_arr, chip_pairs, panel, cos_rows, sin_rows, cores, 0,
+                        None)
     total = exchange(partial, 1.0 / math.sqrt(bin_count))[:, :LAGS, :]
     live = jnp.arange(pair_total, dtype=jnp.int32) < pair_counts[0]
     total = jnp.where(live[None, None, :], total, 0.0).astype(jnp.bfloat16)

time: 130 us -> 119 us (0.915)
  the two profiles are of different devices: /device:TPU:119 before, /device:TPU:1 now
where the time goes in v10:
time: 119 us; the launch traced here: 118 us
  Pallas kernels  106 us (89%)
  local copies, waits for them, and re-layouts  5.73 us (5%)
  other arithmetic  5.49 us (5%)
    pallas_call x1, Pallas kernels, spread(): pl.pallas_call(kernel, out_shape=(jax.ShapeDtypeStruct((rows, width), pie...  79.8 us
    pallas_call x1, Pallas kernels, pair_sums(): pl.pallas_call(kernel, out_shape=jax.ShapeDtypeStruct((owners, 9, LAG_ROW...  18.2 us
    pallas_call x1, Pallas kernels, exchange(): pl.pallas_call(functools.partial(exchange_kernel, scale=scale), out_shape...  7.67 us
    reshape x2, local copies, waits for them, and re-layouts, shards(): jnp.transpose(pieces, (3, 0, 1, 4, 2, 5))  2.63 us

profile of v10, /device:TPU:1, one launch (start us, length us, event | category | flops | bytes accessed | tf_op | source)
XLA Modules:
  0.0 117.7 jit_solution(1763394829118238965)
XLA Ops:
  0.0 0.0 copy-start
  0.7 0.7 compare_and_fusion
  1.4 0.8 copy.14
  2.2 0.1 reshape_squeeze.6
  2.3 0.1 subtract_select_fusion
  2.4 1.7 %multiply_reduce_fusion = f32[16,2048]{1,0:T(8,128)S(1)} fusion(f32[16,3,2,2048]{3,2,1,0:T(2,128)} %param.7), kind=kLoop, calls=%fused_computation.6 | loop fusion | flops 360448 | bytes 917504 | tf_op jit(solution)/shard_map/reduce_sum | solution.py:31
  4.1 0.1 reduce_sum.14
  4.2 0.1 reduce_sum.18
  4.3 0.1 broadcast_in_dim.50
  4.5 0.1 mul.36
  4.6 0.0 copy-done
  4.6 0.4 multiply_convert_fusion
  5.0 0.3 reshape.95
  5.3 1.0 gather_fusion
  6.3 0.6 gather.7
  6.9 0.3 fusion.1
  7.2 0.9 reshape.96
  8.1 1.7 %copy.16.pieces_ref = bf16[32,2,6144]{2,1,0:T(2,128)(2,1)} copy(bf16[32,2,6144]{2,0,1:T(8,128)(2,1)S(1)} %reshape.96) | data formatting | bytes 1572864 | tf_op jit(solution)/shard_map/reshape | solution.py:380
  9.8 79.8 %shard_map.73 = (bf16[512,6144]{1,0:T(8,128)(2,1)}, s32[2,2,256]{2,1,0:T(2,128)}, s32[2,1]{1,0:T(2,128)}) custom-call(bf16[32,2,6144]{2,1,0:T(2,128)(2,1)} %copy.16.pieces_ref, s32[2,256]{1,0:T(2,128)} %rows_ref.1, s32[1]{0:T(128)} %copy.22.count_ref), custom_call_target="tpu_custom_call" | custom-call | tf_op jit(solution)/shard_map/pallas_call | solution.py:312
  89.6 18.2 %shard_map.74.part_ref = f32[2,9,144,256]{3,2,1,0:T(8,128)} custom-call(s32[2,1]{1,0:T(2,128)} %get-tuple-element.8.counts_ref, s32[1]{0:T(128)} %bitcast.5.core_ref, s32[2,2,256]{2,1,0:T(2,128)} %get-tuple-element.9.pairs_ref, bf16[512,6144]{1,0:T(8,128)(2,1)} %get-tuple-element.10.panel_ref, bf16[144,2048]{1,0:T(8,128)(2,1)} %constant.48.clone.cos_ref, ...), custom_call_target="tpu_custom_call" | custom-call | flops 9160359936 | bytes 8945664 | tf_op jit(solution)/shard_map/pallas_call | solution.py:141
  107.8 7.7 %shard_map.75 = f32[9,144,256]{2,1,0:T(8,128)} custom-call(f32[2,9,144,256]{3,2,1,0:T(8,128)} %shard_map.74.part_ref), custom_call_target="tpu_custom_call" | custom-call | tf_op jit(solution)/shard_map/pallas_call | solution.py:350
  115.5 2.2 %fusion.2 = bf16[129,9,256]{2,0,1:T(8,128)(2,1)} fusion(f32[9,144,256]{2,1,0:T(8,128)} %shard_map.75, pred[256]{0:T(512)(128)(4,1)S(1)} %iota_compare_fusion.1), kind=kLoop, calls=%fused_computation.7 | loop fusion | flops 297216 | bytes 1189120 | tf_op jit(solution)/shard_map/transpose | solution.py:392
  (4 shorter events, 0.0 us)
Async XLA Ops:
  0.0 4.6 %copy-start = (f32[16,3,2,2048]{3,2,1,0:T(2,128)S(1)}, f32[16,3,2,2048]{3,2,1,0:T(2,128)}, u32[]{:S(2)}) copy-start(f32[16,3,2,2048]{3,2,1,0:T(2,128)} %param.7) | copy-start | bytes 2359300

commit v11 on v10

--- a/solution.py
+++ b/solution.py
@@ -363,22 +363,23 @@
 def shards(spectra, send_rows, send_counts, pair_rows, pair_counts):
     whitened = whiten(spectra)
     station_count, comps, parts, bin_count = whitened.shape
-    row_width = comps * parts * bin_count
     slot_count = send_rows.shape[2]
     cores = lax.axis_size("core")
     part_bins = bin_count // cores
     core = lax.axis_index("core")
 
-    flat = whitened.reshape(station_count, row_width)
+    sub_bins = part_bins // SUBS
+    ordered = jnp.transpose(
+        whitened.reshape(station_count, comps * parts, cores, SUBS, sub_bins), (0, 2, 3, 1, 4))
+    flat = ordered.reshape(station_count * cores, comps * parts * part_bins)
     lists = send_rows[0]
     col_count = lists.shape[0]
-    picked = jnp.take(flat, lists.reshape(-1), axis=0).reshape(col_count, slot_count, row_width)
+    rows = lists[None, :, :] * cores + jnp.arange(cores, dtype=jnp.int32)[:, None, None]
+    pieces = jnp.take(flat, rows.reshape(-1), axis=0).reshape(
+        cores * col_count, slot_count, comps * parts * part_bins)
     alive = jnp.arange(slot_count, dtype=jnp.int32)[None, :] < send_counts[0][:, None]
-    picked = jnp.where(alive[:, :, None], picked, jnp.zeros_like(picked))
-    pieces = picked.reshape(col_count, slot_count, comps * parts, cores, SUBS,
-                            part_bins // SUBS)
-    pieces = jnp.transpose(pieces, (3, 0, 1, 4, 2, 5)).reshape(
-        cores * col_count, slot_count, comps * parts * part_bins)
+    alive = jnp.tile(alive, (cores, 1))
+    pieces = jnp.where(alive[:, :, None], pieces, jnp.zeros_like(pieces))
     pair_total = pair_rows.shape[1]
     panel, chip_pairs, chip_counts = spread(pieces, pair_rows, pair_counts, lax.axis_size("z"),
                                             cores * col_count, col_count)

time: 119 us -> 124 us (1.042)
  Pallas kernels: 106 us -> 112 us
  local copies, waits for them, and re-layouts: 5.73 us -> 3.17 us
  other arithmetic: 5.49 us -> 7.63 us
    pallas_call x1, Pallas kernels: 18.2 us -> 24.2 us  [pair_sums(): pl.pallas_call(kernel, out_shape=jax.ShapeDtypeStruct((owners, 9, LAG_ROW...]
    reshape x3, local copies, waits for them, and re-layouts: 2.92 us -> 0.83 us  [the longest x1 0.48 us: shards(): flat = ordered.reshape(station_count * cores, comps * parts * part_bins)]
    select_n x1 -> x2, other arithmetic: 0.01 us -> 1.76 us  [the longest x1 1.76 us: shards(): pieces = jnp.where(alive[:, :, None], pieces, jnp.zeros_like(pieces))]
where the time goes in v11:
time: 124 us; the launch traced here: 123 us
  Pallas kernels  112 us (90%)
  other arithmetic  7.63 us (6%)
  local copies, waits for them, and re-layouts  3.17 us (3%)
    pallas_call x1, Pallas kernels, spread(): pl.pallas_call(kernel, out_shape=(jax.ShapeDtypeStruct((rows, width), pie...  79.8 us
    pallas_call x1, Pallas kernels, pair_sums(): pl.pallas_call(kernel, out_shape=jax.ShapeDtypeStruct((owners, 9, LAG_ROW...  24.2 us
    pallas_call x1, Pallas kernels, exchange(): pl.pallas_call(functools.partial(exchange_kernel, scale=scale), out_shape...  7.68 us

profile of v11, /device:TPU:1, one launch (start us, length us, event | category | flops | bytes accessed | tf_op | source)
XLA Modules:
  0.0 123.3 jit_solution(16088353118700612100)
XLA Ops:
  0.0 0.0 copy-start
  0.7 0.7 iota_compare_fusion
  1.4 0.7 multiply_bitcast_fusion
  2.1 0.1 copy.25
  2.2 0.1 copy.19
  2.3 0.1 add.77
  2.4 0.1 copy.24
  2.5 0.1 copy.21
  2.6 0.1 subtract_select_fusion
  2.7 1.7 %multiply_reduce_fusion = f32[16,2048]{1,0:T(8,128)S(1)} fusion(f32[16,3,2,2048]{3,2,1,0:T(2,128)} %param.7), kind=kLoop, calls=%fused_computation.5 | loop fusion | flops 360448 | bytes 917504 | tf_op jit(solution)/shard_map/reduce_sum | solution.py:31
  4.4 0.1 reduce_sum.14
  4.5 0.1 reduce_sum.18
  4.6 0.1 broadcast_in_dim.50
  4.8 0.1 mul.44
  4.9 0.0 copy-done
  4.9 0.4 multiply_convert_fusion
  5.3 0.3 reshape.99
  5.5 0.1 copy.27
  5.6 0.5 reshape.100
  6.1 1.0 gather_fusion
  7.1 0.5 gather.7
  7.6 1.8 %broadcast_select_fusion.1.pieces_ref = bf16[32,2,6144]{2,1,0:T(2,128)(2,1)} fusion(pred[32,2]{1,0:T(8,128)(4,1)S(1)} %bitcast.17, bf16[32,2,6144]{2,1,0:T(2,128)(2,1)S(1)} %gather.7, pred[32,2]{1,0:T(8,128)(4,1)S(1)} %copy.21), kind=kLoop, calls=%fused_computation.2 | loop fusion | flops 786432 | bytes 1572992 | tf_op jit(solution)/shard_map/jit(_where)/select_n | solution.py:382
  9.4 79.8 %shard_map.73 = (bf16[512,6144]{1,0:T(8,128)(2,1)}, s32[2,2,256]{2,1,0:T(2,128)}, s32[2,1]{1,0:T(2,128)}) custom-call(bf16[32,2,6144]{2,1,0:T(2,128)(2,1)} %broadcast_select_fusion.1.pieces_ref, s32[2,256]{1,0:T(2,128)} %rows_ref.1, s32[1]{0:T(128)} %copy.28.count_ref), custom_call_target="tpu_custom_call" | custom-call | tf_op jit(solution)/shard_map/pallas_call | solution.py:312
  89.2 24.2 %shard_map.74.part_ref = f32[2,9,144,256]{3,2,1,0:T(8,128)} custom-call(s32[2,1]{1,0:T(2,128)} %get-tuple-element.8.counts_ref, s32[1]{0:T(128)} %bitcast.7.core_ref, s32[2,2,256]{2,1,0:T(2,128)} %get-tuple-element.9.pairs_ref, bf16[512,6144]{1,0:T(8,128)(2,1)} %get-tuple-element.10.panel_ref, bf16[144,2048]{1,0:T(8,128)(2,1)} %constant.50.clone.cos_ref, ...), custom_call_target="tpu_custom_call" | custom-call | flops 9160359936 | bytes 8945664 | tf_op jit(solution)/shard_map/pallas_call | solution.py:141
  113.4 7.7 %shard_map.75 = f32[9,144,256]{2,1,0:T(8,128)} custom-call(f32[2,9,144,256]{3,2,1,0:T(8,128)} %shard_map.74.part_ref), custom_call_target="tpu_custom_call" | custom-call | tf_op jit(solution)/shard_map/pallas_call | solution.py:350
  121.1 2.2 %fusion = bf16[129,9,256]{2,0,1:T(8,128)(2,1)} fusion(f32[9,144,256]{2,1,0:T(8,128)} %shard_map.75, pred[256]{0:T(512)(128)(4,1)S(1)} %iota_compare_fusion.1), kind=kLoop, calls=%fused_computation.6 | loop fusion | flops 297216 | bytes 1189120 | tf_op jit(solution)/shard_map/transpose | solution.py:393
  (7 shorter events, 0.0 us)
Async XLA Ops:
  0.0 4.9 %copy-start = (f32[16,3,2,2048]{3,2,1,0:T(2,128)S(1)}, f32[16,3,2,2048]{3,2,1,0:T(2,128)}, u32[]{:S(2)}) copy-start(f32[16,3,2,2048]{3,2,1,0:T(2,128)} %param.7) | copy-start | bytes 2359300

commit v12 on v10

--- a/solution.py
+++ b/solution.py
@@ -74,9 +74,9 @@
             off = pl.multiple_of(c * gather_chunk, gather_chunk)
             block = panel_ref[:, pl.ds(off, gather_chunk)]
             f_scr[:, pl.ds(off, gather_chunk)] = jnp.dot(
-                pick_first, block, preferred_element_type=jnp.float32)
+                pick_first, block, preferred_element_type=jnp.float32).astype(jnp.bfloat16)
             s_scr[:, pl.ds(off, gather_chunk)] = jnp.dot(
-                pick_second, block, preferred_element_type=jnp.float32)
+                pick_second, block, preferred_element_type=jnp.float32).astype(jnp.bfloat16)
             return carry
 
         lax.fori_loop(0, width // gather_chunk, gather, 0)
@@ -96,8 +96,8 @@
                     for b in range(3):
                         s_re = s_scr[:, pl.ds(col0 + 2 * b * sub_bins + off, bin_chunk)]
                         s_im = s_scr[:, pl.ds(col0 + (2 * b + 1) * sub_bins + off, bin_chunk)]
-                        real_part = (f_re * s_re + f_im * s_im).astype(jnp.bfloat16)
-                        imag_part = (f_im * s_re - f_re * s_im).astype(jnp.bfloat16)
+                        real_part = f_re * s_re + f_im * s_im
+                        imag_part = f_im * s_re - f_re * s_im
                         acc = lax.dot_general(cos_blk, real_part, nt,
                                               preferred_element_type=jnp.float32)
                         acc = acc + lax.dot_general(sin_blk, imag_part, nt,
@@ -147,8 +147,8 @@
             in_specs=in_specs,
             out_specs=out_spec,
             scratch_shapes=[
-                pltpu.VMEM((PAIR_BLOCK, width), jnp.float32),
-                pltpu.VMEM((PAIR_BLOCK, width), jnp.float32),
+                pltpu.VMEM((PAIR_BLOCK, width), jnp.bfloat16),
+                pltpu.VMEM((PAIR_BLOCK, width), jnp.bfloat16),
             ],
         ),
         input_output_aliases=aliases,

time: 119 us -> 122 us (1.025)
  the two profiles are of different devices: /device:TPU:1 before, /device:TPU:3 now
where the time goes in v12:
time: 122 us; the launch traced here: 121 us
  Pallas kernels  109 us (89%)
  local copies, waits for them, and re-layouts  5.73 us (5%)
  other arithmetic  5.49 us (4%)
    pallas_call x1, Pallas kernels, spread(): pl.pallas_call(kernel, out_shape=(jax.ShapeDtypeStruct((rows, width), pie...  78.2 us
    pallas_call x1, Pallas kernels, pair_sums(): pl.pallas_call(kernel, out_shape=jax.ShapeDtypeStruct((owners, 9, LAG_ROW...  23.8 us
    pallas_call x1, Pallas kernels, exchange(): pl.pallas_call(functools.partial(exchange_kernel, scale=scale), out_shape...  7.45 us
    reshape x2, local copies, waits for them, and re-layouts, shards(): jnp.transpose(pieces, (3, 0, 1, 4, 2, 5))  2.63 us

profile of v12, /device:TPU:3, one launch (start us, length us, event | category | flops | bytes accessed | tf_op | source)
XLA Modules:
  0.0 121.5 jit_solution(6459303701972106307)
XLA Ops:
  0.0 0.0 copy-start
  0.7 0.7 compare_and_fusion
  1.4 0.8 copy.14
  2.2 0.1 reshape_squeeze.6
  2.3 0.1 subtract_select_fusion
  2.4 1.7 %multiply_reduce_fusion = f32[16,2048]{1,0:T(8,128)S(1)} fusion(f32[16,3,2,2048]{3,2,1,0:T(2,128)} %param.7), kind=kLoop, calls=%fused_computation.6 | loop fusion | flops 360448 | bytes 917504 | tf_op jit(solution)/shard_map/reduce_sum | solution.py:31
  4.1 0.1 reduce_sum.14
  4.2 0.1 reduce_sum.18
  4.3 0.1 broadcast_in_dim.50
  4.5 0.1 mul.36
  4.6 0.0 copy-done
  4.6 0.4 multiply_convert_fusion
  5.0 0.3 reshape.95
  5.3 1.0 gather_fusion
  6.3 0.6 gather.7
  6.9 0.3 fusion.1
  7.2 0.9 reshape.96
  8.1 1.7 %copy.16.pieces_ref = bf16[32,2,6144]{2,1,0:T(2,128)(2,1)} copy(bf16[32,2,6144]{2,0,1:T(8,128)(2,1)S(1)} %reshape.96) | data formatting | bytes 1572864 | tf_op jit(solution)/shard_map/reshape | solution.py:380
  9.8 78.2 %shard_map.73 = (bf16[512,6144]{1,0:T(8,128)(2,1)}, s32[2,2,256]{2,1,0:T(2,128)}, s32[2,1]{1,0:T(2,128)}) custom-call(bf16[32,2,6144]{2,1,0:T(2,128)(2,1)} %copy.16.pieces_ref, s32[2,256]{1,0:T(2,128)} %rows_ref.1, s32[1]{0:T(128)} %copy.22.count_ref), custom_call_target="tpu_custom_call" | custom-call | tf_op jit(solution)/shard_map/pallas_call | solution.py:312
  88.0 23.8 %shard_map.74.part_ref = f32[2,9,144,256]{3,2,1,0:T(8,128)} custom-call(s32[2,1]{1,0:T(2,128)} %get-tuple-element.8.counts_ref, s32[1]{0:T(128)} %bitcast.5.core_ref, s32[2,2,256]{2,1,0:T(2,128)} %get-tuple-element.9.pairs_ref, bf16[512,6144]{1,0:T(8,128)(2,1)} %get-tuple-element.10.panel_ref, bf16[144,2048]{1,0:T(8,128)(2,1)} %constant.48.clone.cos_ref, ...), custom_call_target="tpu_custom_call" | custom-call | flops 9160359936 | bytes 8945664 | tf_op jit(solution)/shard_map/pallas_call | solution.py:141
  111.8 7.4 %shard_map.75 = f32[9,144,256]{2,1,0:T(8,128)} custom-call(f32[2,9,144,256]{3,2,1,0:T(8,128)} %shard_map.74.part_ref), custom_call_target="tpu_custom_call" | custom-call | tf_op jit(solution)/shard_map/pallas_call | solution.py:350
  119.3 2.2 %fusion.2 = bf16[129,9,256]{2,0,1:T(8,128)(2,1)} fusion(f32[9,144,256]{2,1,0:T(8,128)} %shard_map.75, pred[256]{0:T(512)(128)(4,1)S(1)} %iota_compare_fusion.1), kind=kLoop, calls=%fused_computation.7 | loop fusion | flops 297216 | bytes 1189120 | tf_op jit(solution)/shard_map/transpose | solution.py:392
  (4 shorter events, 0.0 us)
Async XLA Ops:
  0.0 4.6 %copy-start = (f32[16,3,2,2048]{3,2,1,0:T(2,128)S(1)}, f32[16,3,2,2048]{3,2,1,0:T(2,128)}, u32[]{:S(2)}) copy-start(f32[16,3,2,2048]{3,2,1,0:T(2,128)} %param.7) | copy-start | bytes 2359300

commit v13 on v10

--- a/solution.py
+++ b/solution.py
@@ -106,6 +106,8 @@
                 return carry
 
             lax.fori_loop(0, sub_bins // bin_chunk, chunk, 0)
+        column = start + lax.broadcasted_iota(jnp.int32, out_ref.shape, 3)
+        out_ref[...] = jnp.where(column < counts_ref[owner, 0], out_ref[...], 0.0)
 
 
 def pair_sums(counts, core_arr, chip_pairs, panel, cos_rows, sin_rows, owners, chunk_id, acc):
@@ -342,14 +344,14 @@
         device_id=partner, device_id_type=MESH_ID)
     copy.start()
     copy.wait()
-    out_ref[...] = (part_ref[me_c] + recv_buf[...]) * scale
+    out_ref[...] = ((part_ref[me_c] + recv_buf[...]) * scale).astype(out_ref.dtype)
 
 
 def exchange(partial, scale):
     shape = partial.shape[1:]
     return pl.pallas_call(
         functools.partial(exchange_kernel, scale=scale),
-        out_shape=jax.ShapeDtypeStruct(shape, partial.dtype),
+        out_shape=jax.ShapeDtypeStruct(shape, jnp.bfloat16),
         in_specs=[pl.BlockSpec(memory_space=pltpu.VMEM)],
         out_specs=pl.BlockSpec(memory_space=pltpu.VMEM),
         scratch_shapes=[
@@ -387,8 +389,6 @@
     partial = pair_sums(chip_counts, core_arr, chip_pairs, panel, cos_rows, sin_rows, cores, 0,
                         None)
     total = exchange(partial, 1.0 / math.sqrt(bin_count))[:, :LAGS, :]
-    live = jnp.arange(pair_total, dtype=jnp.int32) < pair_counts[0]
-    total = jnp.where(live[None, None, :], total, 0.0).astype(jnp.bfloat16)
     return jnp.transpose(total, (1, 0, 2))
 
 

time: 119 us -> 124 us (1.042)
  the two profiles are of different devices: /device:TPU:1 before, /device:TPU:9 now
where the time goes in v13:
time: 124 us; the launch traced here: 123 us
  Pallas kernels  110 us (89%)
  local copies, waits for them, and re-layouts  7.67 us (6%)
  other arithmetic  4.39 us (4%)
    pallas_call x1, Pallas kernels, spread(): pl.pallas_call(kernel, out_shape=(jax.ShapeDtypeStruct((rows, width), pie...  79.5 us
    pallas_call x1, Pallas kernels, pair_sums(): pl.pallas_call(kernel, out_shape=jax.ShapeDtypeStruct((owners, 9, LAG_ROW...  24.3 us
    pallas_call x1, Pallas kernels, exchange(): pl.pallas_call(functools.partial(exchange_kernel, scale=scale), out_shape...  6.57 us
    reshape x2, local copies, waits for them, and re-layouts, shards(): jnp.transpose(pieces, (3, 0, 1, 4, 2, 5))  2.63 us

profile of v13, /device:TPU:9, one launch (start us, length us, event | category | flops | bytes accessed | tf_op | source)
XLA Modules:
  0.0 123.3 jit_solution(6377004150654149754)
XLA Ops:
  0.7 0.7 compare_and_fusion
  1.3 0.8 copy.14
  2.1 0.1 reshape_squeeze.6
  2.2 0.1 subtract_select_fusion
  2.3 1.7 %multiply_reduce_fusion = f32[16,2048]{1,0:T(8,128)S(1)} fusion(f32[16,3,2,2048]{3,2,1,0:T(2,128)} %param.7), kind=kLoop, calls=%fused_computation.5 | loop fusion | flops 360448 | bytes 917504 | tf_op jit(solution)/shard_map/reduce_sum | solution.py:31
  4.0 0.1 reduce_sum.14
  4.1 0.1 reduce_sum.18
  4.2 0.1 broadcast_in_dim.36
  4.4 0.1 mul.36
  4.5 1.5 %multiply_convert_fusion = bf16[16,3,2,2048]{3,2,1,0:T(2,128)(2,1)S(1)} fusion(f32[16,3,2,2048]{3,2,1,0:T(2,128)} %param.7, f32[16,2048]{1,0:T(8,128)S(1)} %mul.36, f32[2048]{0:T(1024)S(1)} %subtract_select_fusion), kind=kLoop, calls=%fused_computation.4 | loop fusion | flops 589824 | bytes 1318912 | tf_op jit(solution)/shard_map/convert_element_type | solution.py:34
  6.0 0.3 reshape.91
  6.3 1.0 gather_fusion
  7.3 0.6 gather.7
  7.9 0.3 fusion.1
  8.2 0.9 reshape.92
  9.1 1.7 %copy.16.pieces_ref = bf16[32,2,6144]{2,1,0:T(2,128)(2,1)} copy(bf16[32,2,6144]{2,0,1:T(8,128)(2,1)S(1)} %reshape.92) | data formatting | bytes 1572864 | tf_op jit(solution)/shard_map/reshape | solution.py:382
  10.8 79.5 %shard_map.73 = (bf16[512,6144]{1,0:T(8,128)(2,1)}, s32[2,2,256]{2,1,0:T(2,128)}, s32[2,1]{1,0:T(2,128)}) custom-call(bf16[32,2,6144]{2,1,0:T(2,128)(2,1)} %copy.16.pieces_ref, s32[2,256]{1,0:T(2,128)} %rows_ref.1, s32[1]{0:T(128)S(6)} %copy.22.count_ref), custom_call_target="tpu_custom_call" | custom-call | tf_op jit(solution)/shard_map/pallas_call | solution.py:314
  90.4 24.3 %shard_map.74.part_ref = f32[2,9,144,256]{3,2,1,0:T(8,128)} custom-call(s32[2,1]{1,0:T(2,128)} %get-tuple-element.8.counts_ref, s32[1]{0:T(128)} %bitcast.4.core_ref, s32[2,2,256]{2,1,0:T(2,128)} %get-tuple-element.9.pairs_ref, bf16[512,6144]{1,0:T(8,128)(2,1)} %get-tuple-element.10.panel_ref, bf16[144,2048]{1,0:T(8,128)(2,1)} %constant.48.clone.cos_ref, ...), custom_call_target="tpu_custom_call" | custom-call | flops 9160359936 | bytes 8945664 | tf_op jit(solution)/shard_map/pallas_call | solution.py:143
  114.7 6.6 %shard_map.75 = bf16[9,144,256]{2,1,0:T(8,128)(2,1)} custom-call(f32[2,9,144,256]{3,2,1,0:T(8,128)} %shard_map.74.part_ref), custom_call_target="tpu_custom_call" | custom-call | tf_op jit(solution)/shard_map/pallas_call | solution.py:352
  121.3 1.9 %slice_bitcast_fusion = bf16[129,9,256]{2,0,1:T(8,128)(2,1)} fusion(bf16[9,144,256]{2,1,0:T(8,128)(2,1)} %shard_map.75), kind=kLoop, calls=%fused_computation.6 | loop fusion | bytes 1188864 | tf_op jit(solution)/shard_map/transpose | solution.py:392
  (3 shorter events, 0.0 us)

commit v14 on v13

--- a/solution.py
+++ b/solution.py
@@ -42,10 +42,13 @@
     pad = ((0, LAG_ROWS - LAGS), (0, 0))
     cos_rows = np.pad(np.cos(angle).astype(np.float32).astype(ml_dtypes.bfloat16), pad)
     sin_rows = np.pad((-np.sin(angle)).astype(np.float32).astype(ml_dtypes.bfloat16), pad)
-    return jnp.asarray(cos_rows), jnp.asarray(sin_rows)
-
-
-def pair_kernel(counts_ref, core_ref, pairs_ref, panel_ref, cos_ref, sin_ref, *rest,
+    chunks = bin_count // BIN_CHUNK
+    both = np.stack([cos_rows.reshape(LAG_ROWS, chunks, BIN_CHUNK),
+                     sin_rows.reshape(LAG_ROWS, chunks, BIN_CHUNK)], axis=2)
+    return jnp.asarray(both.reshape(LAG_ROWS, 2 * bin_count))
+
+
+def pair_kernel(counts_ref, core_ref, pairs_ref, panel_ref, lag_ref, *rest,
                 blocks_per_owner, part_bins, accumulate):
     if accumulate:
         acc_ref, out_ref, f_scr, s_scr = rest
@@ -88,8 +91,7 @@
 
             def chunk(kc, carry):
                 off = pl.multiple_of(kc * bin_chunk, bin_chunk)
-                cos_blk = cos_ref[:, pl.ds(sub * sub_bins + off, bin_chunk)]
-                sin_blk = sin_ref[:, pl.ds(sub * sub_bins + off, bin_chunk)]
+                lag_blk = lag_ref[:, pl.ds(2 * (sub * sub_bins + off), 2 * bin_chunk)]
                 for a in range(3):
                     f_re = f_scr[:, pl.ds(col0 + 2 * a * sub_bins + off, bin_chunk)]
                     f_im = f_scr[:, pl.ds(col0 + (2 * a + 1) * sub_bins + off, bin_chunk)]
@@ -98,10 +100,9 @@
                         s_im = s_scr[:, pl.ds(col0 + (2 * b + 1) * sub_bins + off, bin_chunk)]
                         real_part = (f_re * s_re + f_im * s_im).astype(jnp.bfloat16)
                         imag_part = (f_im * s_re - f_re * s_im).astype(jnp.bfloat16)
-                        acc = lax.dot_general(cos_blk, real_part, nt,
+                        both = jnp.concatenate([real_part, imag_part], axis=1)
+                        acc = lax.dot_general(lag_blk, both, nt,
                                               preferred_element_type=jnp.float32)
-                        acc = acc + lax.dot_general(sin_blk, imag_part, nt,
-                                                    preferred_element_type=jnp.float32)
                         out_ref[0, 3 * a + b] += acc
                 return carry
 
@@ -110,7 +111,7 @@
         out_ref[...] = jnp.where(column < counts_ref[owner, 0], out_ref[...], 0.0)
 
 
-def pair_sums(counts, core_arr, chip_pairs, panel, cos_rows, sin_rows, owners, chunk_id, acc):
+def pair_sums(counts, core_arr, chip_pairs, panel, lag_rows, owners, chunk_id, acc):
     rows, width = panel.shape
     part_bins = width // 6
     pairs = chip_pairs.shape[0] * chip_pairs.shape[2]
@@ -131,10 +132,9 @@
         pl.BlockSpec((1, 2, PAIR_BLOCK),
                      lambda i, c, k: (i // blocks_per_owner, 0, i % blocks_per_owner)),
         pl.BlockSpec((rows, width), lambda i, c, k: (0, 0)),
-        pl.BlockSpec((LAG_ROWS, part_bins), lambda i, c, k: (0, k[0])),
-        pl.BlockSpec((LAG_ROWS, part_bins), lambda i, c, k: (0, k[0])),
+        pl.BlockSpec((LAG_ROWS, 2 * part_bins), lambda i, c, k: (0, k[0])),
     ]
-    args = [counts, core_arr, chip_pairs, panel, cos_rows, sin_rows]
+    args = [counts, core_arr, chip_pairs, panel, lag_rows]
     aliases = {}
     if accumulate:
         in_specs.append(out_spec)
@@ -384,10 +384,9 @@
     pair_total = pair_rows.shape[1]
     panel, chip_pairs, chip_counts = spread(pieces, pair_rows, pair_counts, lax.axis_size("z"),
                                             cores * col_count, col_count)
-    cos_rows, sin_rows = lag_tables(bin_count)
+    lag_rows = lag_tables(bin_count)
     core_arr = core.astype(jnp.int32)[None]
-    partial = pair_sums(chip_counts, core_arr, chip_pairs, panel, cos_rows, sin_rows, cores, 0,
-                        None)
+    partial = pair_sums(chip_counts, core_arr, chip_pairs, panel, lag_rows, cores, 0, None)
     total = exchange(partial, 1.0 / math.sqrt(bin_count))[:, :LAGS, :]
     return jnp.transpose(total, (1, 0, 2))
 

time: 124 us -> 127 us (1.024)
  the two profiles are of different devices: /device:TPU:9 before, /device:TPU:23 now
where the time goes in v14:
time: 127 us
  Pallas kernels  115 us (91%)
  local copies, waits for them, and re-layouts  7.67 us (6%)
  other arithmetic  3.25 us (3%)
    pallas_call x1, Pallas kernels, spread(): pl.pallas_call(kernel, out_shape=(jax.ShapeDtypeStruct((rows, width), pie...  79.1 us
    pallas_call x1, Pallas kernels, pair_sums(): pl.pallas_call(kernel, out_shape=jax.ShapeDtypeStruct((owners, 9, LAG_ROW...  29.7 us
    pallas_call x1, Pallas kernels, exchange(): pl.pallas_call(functools.partial(exchange_kernel, scale=scale), out_shape...  6.18 us
    reshape x2, local copies, waits for them, and re-layouts, shards(): jnp.transpose(pieces, (3, 0, 1, 4, 2, 5))  2.63 us

profile of v14, /device:TPU:23, one launch (start us, length us, event | category | flops | bytes accessed | tf_op | source)
XLA Modules:
  0.0 126.7 jit_solution(14807046354525085728)
XLA Ops:
  0.0 0.0 copy-start
  0.7 0.7 compare_and_fusion
  1.4 0.8 copy.13
  2.2 0.1 reshape_squeeze.6
  2.3 0.1 subtract_select_fusion
  2.3 1.7 %multiply_reduce_fusion = f32[16,2048]{1,0:T(8,128)S(1)} fusion(f32[16,3,2,2048]{3,2,1,0:T(2,128)} %param.6), kind=kLoop, calls=%fused_computation.5 | loop fusion | flops 360448 | bytes 917504 | tf_op jit(solution)/shard_map/reduce_sum | solution.py:31
  4.0 0.1 reduce_sum.14
  4.2 0.1 reduce_sum.18
  4.3 0.1 broadcast_in_dim.36
  4.4 0.1 mul.36
  4.6 0.0 copy-done
  4.6 0.4 multiply_convert_fusion
  4.9 0.3 reshape.91
  5.2 1.0 gather_fusion
  6.3 0.6 gather.7
  6.9 0.3 fusion.1
  7.2 0.9 reshape.92
  8.1 1.7 %copy.15.pieces_ref = bf16[32,2,6144]{2,1,0:T(2,128)(2,1)} copy(bf16[32,2,6144]{2,0,1:T(8,128)(2,1)S(1)} %reshape.92) | data formatting | bytes 1572864 | tf_op jit(solution)/shard_map/reshape | solution.py:382
  9.8 79.1 %shard_map.64 = (bf16[512,6144]{1,0:T(8,128)(2,1)}, s32[2,2,256]{2,1,0:T(2,128)}, s32[2,1]{1,0:T(2,128)}) custom-call(bf16[32,2,6144]{2,1,0:T(2,128)(2,1)} %copy.15.pieces_ref, s32[2,256]{1,0:T(2,128)} %rows_ref.1, s32[1]{0:T(128)S(6)} %copy.21.count_ref), custom_call_target="tpu_custom_call" | custom-call | tf_op jit(solution)/shard_map/pallas_call | solution.py:314
  88.9 29.7 %shard_map.65.part_ref = f32[2,9,144,256]{3,2,1,0:T(8,128)} custom-call(s32[2,1]{1,0:T(2,128)} %get-tuple-element.8.counts_ref, s32[1]{0:T(128)} %bitcast.4.core_ref, s32[2,2,256]{2,1,0:T(2,128)} %get-tuple-element.9.pairs_ref, bf16[512,6144]{1,0:T(8,128)(2,1)} %get-tuple-element.10.panel_ref, bf16[144,4096]{1,0:T(8,128)(2,1)} %constant.46.clone.lag_ref), custom_call_target="tpu_custom_call" | custom-call | flops 9160359936 | bytes 8945664 | tf_op jit(solution)/shard_map/pallas_call | solution.py:143
  118.6 6.2 %shard_map.66 = bf16[9,144,256]{2,1,0:T(8,128)(2,1)} custom-call(f32[2,9,144,256]{3,2,1,0:T(8,128)} %shard_map.65.part_ref), custom_call_target="tpu_custom_call" | custom-call | tf_op jit(solution)/shard_map/pallas_call | solution.py:352
  124.8 1.9 %slice_bitcast_fusion = bf16[129,9,256]{2,0,1:T(8,128)(2,1)} fusion(bf16[9,144,256]{2,1,0:T(8,128)(2,1)} %shard_map.66), kind=kLoop, calls=%fused_computation.6 | loop fusion | bytes 1188864 | tf_op jit(solution)/shard_map/transpose | solution.py:391
  (3 shorter events, 0.0 us)
Async XLA Ops:
  0.0 4.6 %copy-start = (f32[16,3,2,2048]{3,2,1,0:T(2,128)S(1)}, f32[16,3,2,2048]{3,2,1,0:T(2,128)}, u32[]{:S(2)}) copy-start(f32[16,3,2,2048]{3,2,1,0:T(2,128)} %param.6) | copy-start | bytes 2359300

commit v15 on v14

--- a/solution.py
+++ b/solution.py
@@ -71,15 +71,15 @@
         idx = pairs_ref[0]
         pick_first = jnp.where(idx[0:1, :] == iota, 1.0, 0.0).T.astype(jnp.bfloat16)
         pick_second = jnp.where(idx[1:2, :] == iota, 1.0, 0.0).T.astype(jnp.bfloat16)
+        pick = jnp.concatenate([pick_first, pick_second], axis=0)
         gather_chunk = min(GATHER_CHUNK, width)
 
         def gather(c, carry):
             off = pl.multiple_of(c * gather_chunk, gather_chunk)
             block = panel_ref[:, pl.ds(off, gather_chunk)]
-            f_scr[:, pl.ds(off, gather_chunk)] = jnp.dot(
-                pick_first, block, preferred_element_type=jnp.float32)
-            s_scr[:, pl.ds(off, gather_chunk)] = jnp.dot(
-                pick_second, block, preferred_element_type=jnp.float32)
+            both = jnp.dot(pick, block, preferred_element_type=jnp.float32)
+            f_scr[:, pl.ds(off, gather_chunk)] = both[:PAIR_BLOCK]
+            s_scr[:, pl.ds(off, gather_chunk)] = both[PAIR_BLOCK:]
             return carry
 
         lax.fori_loop(0, width // gather_chunk, gather, 0)

time: 127 us -> 124 us (0.976)
  the two profiles are of different devices: /device:TPU:23 before, /device:TPU:119 now
where the time goes in v15:
time: 124 us
  Pallas kernels  112 us (90%)
  local copies, waits for them, and re-layouts  7.68 us (6%)
  other arithmetic  3.25 us (3%)
    pallas_call x1, Pallas kernels, spread(): pl.pallas_call(kernel, out_shape=(jax.ShapeDtypeStruct((rows, width), pie...  76.4 us
    pallas_call x1, Pallas kernels, pair_sums(): pl.pallas_call(kernel, out_shape=jax.ShapeDtypeStruct((owners, 9, LAG_ROW...  29.3 us
    pallas_call x1, Pallas kernels, exchange(): pl.pallas_call(functools.partial(exchange_kernel, scale=scale), out_shape...  6.16 us
    reshape x2, local copies, waits for them, and re-layouts, shards(): jnp.transpose(pieces, (3, 0, 1, 4, 2, 5))  2.63 us

profile of v15, /device:TPU:119, one launch (start us, length us, event | category | flops | bytes accessed | tf_op | source)
XLA Modules:
  0.0 123.7 jit_solution(723937969798619450)
XLA Ops:
  0.0 0.0 copy-start
  0.7 0.7 compare_and_fusion
  1.4 0.8 copy.13
  2.2 0.1 reshape_squeeze.6
  2.3 0.1 subtract_select_fusion
  2.3 1.7 %multiply_reduce_fusion = f32[16,2048]{1,0:T(8,128)S(1)} fusion(f32[16,3,2,2048]{3,2,1,0:T(2,128)} %param.6), kind=kLoop, calls=%fused_computation.5 | loop fusion | flops 360448 | bytes 917504 | tf_op jit(solution)/shard_map/reduce_sum | solution.py:31
  4.0 0.1 reduce_sum.14
  4.2 0.1 reduce_sum.18
  4.3 0.1 broadcast_in_dim.36
  4.4 0.1 mul.36
  4.6 0.0 copy-done
  4.6 0.4 multiply_convert_fusion
  4.9 0.3 reshape.91
  5.2 1.0 gather_fusion
  6.3 0.6 gather.7
  6.9 0.3 fusion.1
  7.2 0.9 reshape.92
  8.1 1.7 %copy.15.pieces_ref = bf16[32,2,6144]{2,1,0:T(2,128)(2,1)} copy(bf16[32,2,6144]{2,0,1:T(8,128)(2,1)S(1)} %reshape.92) | data formatting | bytes 1572864 | tf_op jit(solution)/shard_map/reshape | solution.py:382
  9.8 76.4 %shard_map.64 = (bf16[512,6144]{1,0:T(8,128)(2,1)}, s32[2,2,256]{2,1,0:T(2,128)}, s32[2,1]{1,0:T(2,128)}) custom-call(bf16[32,2,6144]{2,1,0:T(2,128)(2,1)} %copy.15.pieces_ref, s32[2,256]{1,0:T(2,128)} %rows_ref.1, s32[1]{0:T(128)S(6)} %copy.21.count_ref), custom_call_target="tpu_custom_call" | custom-call | tf_op jit(solution)/shard_map/pallas_call | solution.py:314
  86.2 29.3 %shard_map.65.part_ref = f32[2,9,144,256]{3,2,1,0:T(8,128)} custom-call(s32[2,1]{1,0:T(2,128)} %get-tuple-element.8.counts_ref, s32[1]{0:T(128)} %bitcast.4.core_ref, s32[2,2,256]{2,1,0:T(2,128)} %get-tuple-element.9.pairs_ref, bf16[512,6144]{1,0:T(8,128)(2,1)} %get-tuple-element.10.panel_ref, bf16[144,4096]{1,0:T(8,128)(2,1)} %constant.46.clone.lag_ref), custom_call_target="tpu_custom_call" | custom-call | flops 9160359936 | bytes 8945664 | tf_op jit(solution)/shard_map/pallas_call | solution.py:143
  115.5 6.2 %shard_map.66 = bf16[9,144,256]{2,1,0:T(8,128)(2,1)} custom-call(f32[2,9,144,256]{3,2,1,0:T(8,128)} %shard_map.65.part_ref), custom_call_target="tpu_custom_call" | custom-call | tf_op jit(solution)/shard_map/pallas_call | solution.py:352
  121.7 1.9 %slice_bitcast_fusion = bf16[129,9,256]{2,0,1:T(8,128)(2,1)} fusion(bf16[9,144,256]{2,1,0:T(8,128)(2,1)} %shard_map.66), kind=kLoop, calls=%fused_computation.6 | loop fusion | bytes 1188864 | tf_op jit(solution)/shard_map/transpose | solution.py:391
  (3 shorter events, 0.0 us)
Async XLA Ops:
  0.0 4.6 %copy-start = (f32[16,3,2,2048]{3,2,1,0:T(2,128)S(1)}, f32[16,3,2,2048]{3,2,1,0:T(2,128)}, u32[]{:S(2)}) copy-start(f32[16,3,2,2048]{3,2,1,0:T(2,128)} %param.6) | copy-start | bytes 2359300

commit v16 on v15

--- a/solution.py
+++ b/solution.py
@@ -92,6 +92,7 @@
             def chunk(kc, carry):
                 off = pl.multiple_of(kc * bin_chunk, bin_chunk)
                 lag_blk = lag_ref[:, pl.ds(2 * (sub * sub_bins + off), 2 * bin_chunk)]
+                crosses = []
                 for a in range(3):
                     f_re = f_scr[:, pl.ds(col0 + 2 * a * sub_bins + off, bin_chunk)]
                     f_im = f_scr[:, pl.ds(col0 + (2 * a + 1) * sub_bins + off, bin_chunk)]
@@ -100,15 +101,15 @@
                         s_im = s_scr[:, pl.ds(col0 + (2 * b + 1) * sub_bins + off, bin_chunk)]
                         real_part = (f_re * s_re + f_im * s_im).astype(jnp.bfloat16)
                         imag_part = (f_im * s_re - f_re * s_im).astype(jnp.bfloat16)
-                        both = jnp.concatenate([real_part, imag_part], axis=1)
-                        acc = lax.dot_general(lag_blk, both, nt,
-                                              preferred_element_type=jnp.float32)
-                        out_ref[0, 3 * a + b] += acc
+                        crosses.append(jnp.concatenate([real_part, imag_part], axis=1))
+                stacked = jnp.concatenate(crosses, axis=0)
+                acc = lax.dot_general(stacked, lag_blk, nt, preferred_element_type=jnp.float32)
+                out_ref[0] += acc.reshape(9, PAIR_BLOCK, LAG_ROWS)
                 return carry
 
             lax.fori_loop(0, sub_bins // bin_chunk, chunk, 0)
-        column = start + lax.broadcasted_iota(jnp.int32, out_ref.shape, 3)
-        out_ref[...] = jnp.where(column < counts_ref[owner, 0], out_ref[...], 0.0)
+        row = start + lax.broadcasted_iota(jnp.int32, out_ref.shape, 2)
+        out_ref[...] = jnp.where(row < counts_ref[owner, 0], out_ref[...], 0.0)
 
 
 def pair_sums(counts, core_arr, chip_pairs, panel, lag_rows, owners, chunk_id, acc):
@@ -126,8 +127,8 @@
     cost = pl.CostEstimate(flops=flops, transcendentals=0,
                            bytes_accessed=rows * width * 2 + out_bytes * (2 if accumulate else 1))
     out_spec = pl.BlockSpec(
-        (1, 9, LAG_ROWS, PAIR_BLOCK),
-        lambda i, c, k: (i // blocks_per_owner, 0, 0, i % blocks_per_owner))
+        (1, 9, PAIR_BLOCK, LAG_ROWS),
+        lambda i, c, k: (i // blocks_per_owner, 0, i % blocks_per_owner, 0))
     in_specs = [
         pl.BlockSpec((1, 2, PAIR_BLOCK),
                      lambda i, c, k: (i // blocks_per_owner, 0, i % blocks_per_owner)),
@@ -142,7 +143,7 @@
         aliases = {len(args) - 1: 0}
     return pl.pallas_call(
         kernel,
-        out_shape=jax.ShapeDtypeStruct((owners, 9, LAG_ROWS, per_owner), jnp.float32),
+        out_shape=jax.ShapeDtypeStruct((owners, 9, per_owner, LAG_ROWS), jnp.float32),
         grid_spec=pltpu.PrefetchScalarGridSpec(
             num_scalar_prefetch=2,
             grid=grid,
@@ -387,8 +388,8 @@
     lag_rows = lag_tables(bin_count)
     core_arr = core.astype(jnp.int32)[None]
     partial = pair_sums(chip_counts, core_arr, chip_pairs, panel, lag_rows, cores, 0, None)
-    total = exchange(partial, 1.0 / math.sqrt(bin_count))[:, :LAGS, :]
-    return jnp.transpose(total, (1, 0, 2))
+    total = exchange(partial, 1.0 / math.sqrt(bin_count))[:, :, :LAGS]
+    return jnp.transpose(total, (2, 0, 1))
 
 
 def solution(mesh):

time: 124 us -> 128 us (1.032)
  the two profiles are of different devices: /device:TPU:119 before, /device:TPU:103 now
where the time goes in v16:
time: 128 us; the launch traced here: 127 us
  Pallas kernels  115 us (90%)
  local copies, waits for them, and re-layouts  8.38 us (7%)
  other arithmetic  3.25 us (3%)
    pallas_call x1, Pallas kernels, spread(): pl.pallas_call(kernel, out_shape=(jax.ShapeDtypeStruct((rows, width), pie...  75.8 us
    pallas_call x1, Pallas kernels, pair_sums(): pl.pallas_call(kernel, out_shape=jax.ShapeDtypeStruct((owners, 9, per_own...  29.9 us
    pallas_call x1, Pallas kernels, exchange(): pl.pallas_call(functools.partial(exchange_kernel, scale=scale), out_shape...  9.21 us
    transpose x2, local copies, waits for them, and re-layouts, shards(): return jnp.transpose(total, (2, 0, 1))  2.65 us
    reshape x2, local copies, waits for them, and re-layouts, shards(): jnp.transpose(pieces, (3, 0, 1, 4, 2, 5))  2.63 us

profile of v16, /device:TPU:103, one launch (start us, length us, event | category | flops | bytes accessed | tf_op | source)
XLA Modules:
  0.0 127.4 jit_solution(5478353462820377802)
XLA Ops:
  0.0 0.0 copy-start
  0.7 0.7 compare_and_fusion
  1.4 0.8 copy.15
  2.2 0.1 reshape_squeeze.6
  2.3 0.1 subtract_select_fusion
  2.3 1.7 %multiply_reduce_fusion = f32[16,2048]{1,0:T(8,128)S(1)} fusion(f32[16,3,2,2048]{3,2,1,0:T(2,128)} %param.6), kind=kLoop, calls=%fused_computation.6 | loop fusion | flops 360448 | bytes 917504 | tf_op jit(solution)/shard_map/reduce_sum | solution.py:31
  4.0 0.1 reduce_sum.14
  4.2 0.1 reduce_sum.18
  4.3 0.1 broadcast_in_dim.36
  4.4 0.1 mul.36
  4.6 0.0 copy-done
  4.6 0.4 multiply_convert_fusion
  4.9 0.3 reshape.91
  5.2 1.0 gather_fusion
  6.3 0.6 gather.7
  6.9 0.3 fusion.1
  7.2 0.9 reshape.92
  8.1 1.7 %copy.17.pieces_ref = bf16[32,2,6144]{2,1,0:T(2,128)(2,1)} copy(bf16[32,2,6144]{2,0,1:T(8,128)(2,1)S(1)} %reshape.92) | data formatting | bytes 1572864 | tf_op jit(solution)/shard_map/reshape | solution.py:383
  9.8 75.8 %shard_map.64 = (bf16[512,6144]{1,0:T(8,128)(2,1)}, s32[2,2,256]{2,1,0:T(2,128)}, s32[2,1]{1,0:T(2,128)}) custom-call(bf16[32,2,6144]{2,1,0:T(2,128)(2,1)} %copy.17.pieces_ref, s32[2,256]{1,0:T(2,128)} %rows_ref.1, s32[1]{0:T(128)S(6)} %copy.24.count_ref), custom_call_target="tpu_custom_call" | custom-call | tf_op jit(solution)/shard_map/pallas_call | solution.py:315
  85.6 29.9 %shard_map.65.part_ref = f32[2,9,256,144]{3,2,1,0:T(8,128)} custom-call(s32[2,1]{1,0:T(2,128)} %get-tuple-element.8.counts_ref, s32[1]{0:T(128)} %bitcast.4.core_ref, s32[2,2,256]{2,1,0:T(2,128)} %get-tuple-element.9.pairs_ref, bf16[512,6144]{1,0:T(8,128)(2,1)} %get-tuple-element.10.panel_ref, bf16[144,4096]{1,0:T(8,128)(2,1)} %constant.46.clone.lag_ref), custom_call_target="tpu_custom_call" | custom-call | flops 9160359936 | bytes 8945664 | tf_op jit(solution)/shard_map/pallas_call | solution.py:144
  115.5 9.2 %shard_map.66 = bf16[9,256,144]{2,1,0:T(8,128)(2,1)} custom-call(f32[2,9,256,144]{3,2,1,0:T(8,128)} %shard_map.65.part_ref), custom_call_target="tpu_custom_call" | custom-call | tf_op jit(solution)/shard_map/pallas_call | solution.py:353
  124.7 1.3 %slice_bitcast_fusion = bf16[129,9,256]{0,2,1:T(8,128)(2,1)S(1)} fusion(bf16[9,256,144]{2,1,0:T(8,128)(2,1)} %shard_map.66), kind=kLoop, calls=%fused_computation.1 | loop fusion | bytes 1188864 | tf_op jit(solution)/shard_map/transpose | solution.py:392
  126.1 1.3 %copy.18 = bf16[129,9,256]{2,0,1:T(8,128)(2,1)} copy(bf16[129,9,256]{0,2,1:T(8,128)(2,1)S(1)} %slice_bitcast_fusion) | data formatting | bytes 1188864 | tf_op jit(solution)/shard_map/transpose | solution.py:392
  (3 shorter events, 0.0 us)
Async XLA Ops:
  0.0 4.6 %copy-start = (f32[16,3,2,2048]{3,2,1,0:T(2,128)S(1)}, f32[16,3,2,2048]{3,2,1,0:T(2,128)}, u32[]{:S(2)}) copy-start(f32[16,3,2,2048]{3,2,1,0:T(2,128)} %param.6) | copy-start | bytes 2359300

commit v17 on v15

--- a/solution.py
+++ b/solution.py
@@ -331,11 +331,13 @@
     )(pieces, pair_rows, pair_counts)
 
 
-def exchange_kernel(part_ref, out_ref, recv_buf, sems, *, scale):
+def exchange_kernel(part_ref, out_ref, mine_buf, recv_buf, sems, *, scale):
     me_z = lax.axis_index("z")
     me_c = lax.axis_index("core")
     me_b = lax.axis_index("blk")
     partner = (me_z, 1 - me_c, me_b)
+    local = pltpu.make_async_copy(part_ref.at[me_c], mine_buf, sems.at[2])
+    local.start()
     barrier = pltpu.get_barrier_semaphore()
     pl.semaphore_signal(barrier, 1, device_id=partner, device_id_type=MESH_ID)
     pl.semaphore_wait(barrier, 1)
@@ -343,8 +345,9 @@
         part_ref.at[1 - me_c], recv_buf, sems.at[0], sems.at[1],
         device_id=partner, device_id_type=MESH_ID)
     copy.start()
+    local.wait()
     copy.wait()
-    out_ref[...] = ((part_ref[me_c] + recv_buf[...]) * scale).astype(out_ref.dtype)
+    out_ref[...] = ((mine_buf[...] + recv_buf[...]) * scale).astype(out_ref.dtype)
 
 
 def exchange(partial, scale):
@@ -352,11 +355,12 @@
     return pl.pallas_call(
         functools.partial(exchange_kernel, scale=scale),
         out_shape=jax.ShapeDtypeStruct(shape, jnp.bfloat16),
-        in_specs=[pl.BlockSpec(memory_space=pltpu.VMEM)],
+        in_specs=[pl.BlockSpec(memory_space=pl.ANY)],
         out_specs=pl.BlockSpec(memory_space=pltpu.VMEM),
         scratch_shapes=[
             pltpu.VMEM(shape, partial.dtype),
-            pltpu.SemaphoreType.DMA((2,)),
+            pltpu.VMEM(shape, partial.dtype),
+            pltpu.SemaphoreType.DMA((3,)),
         ],
         compiler_params=pltpu.CompilerParams(collective_id=1, has_side_effects=True),
     )(partial)

time: 124 us -> 123 us (level)
  the two profiles are of different devices: /device:TPU:119 before, /device:TPU:105 now
where the time goes in v17:
time: 123 us
  Pallas kernels  111 us (90%)
  local copies, waits for them, and re-layouts  7.68 us (6%)
  other arithmetic  3.25 us (3%)
    pallas_call x1, Pallas kernels, spread(): pl.pallas_call(kernel, out_shape=(jax.ShapeDtypeStruct((rows, width), pie...  76.8 us
    pallas_call x1, Pallas kernels, pair_sums(): pl.pallas_call(kernel, out_shape=jax.ShapeDtypeStruct((owners, 9, LAG_ROW...  29.3 us
    pallas_call x1, Pallas kernels, exchange(): pl.pallas_call(functools.partial(exchange_kernel, scale=scale), out_shape...  5.04 us
    reshape x2, local copies, waits for them, and re-layouts, shards(): jnp.transpose(pieces, (3, 0, 1, 4, 2, 5))  2.63 us

profile of v17, /device:TPU:105, one launch (start us, length us, event | category | flops | bytes accessed | tf_op | source)
XLA Modules:
  0.0 123.0 jit_solution(1605527735109811894)
XLA Ops:
  0.0 0.0 copy-start
  0.7 0.7 compare_and_fusion
  1.4 0.8 copy.13
  2.2 0.1 reshape_squeeze.6
  2.3 0.1 subtract_select_fusion
  2.3 1.7 %multiply_reduce_fusion = f32[16,2048]{1,0:T(8,128)S(1)} fusion(f32[16,3,2,2048]{3,2,1,0:T(2,128)} %param.6), kind=kLoop, calls=%fused_computation.5 | loop fusion | flops 360448 | bytes 917504 | tf_op jit(solution)/shard_map/reduce_sum | solution.py:31
  4.0 0.1 reduce_sum.14
  4.2 0.1 reduce_sum.18
  4.3 0.1 broadcast_in_dim.36
  4.4 0.1 mul.36
  4.6 0.0 copy-done
  4.6 0.4 multiply_convert_fusion
  4.9 0.3 reshape.91
  5.2 1.0 gather_fusion
  6.3 0.6 gather.7
  6.9 0.3 fusion.1
  7.2 0.9 reshape.92
  8.1 1.7 %copy.15.pieces_ref = bf16[32,2,6144]{2,1,0:T(2,128)(2,1)} copy(bf16[32,2,6144]{2,0,1:T(8,128)(2,1)S(1)} %reshape.92) | data formatting | bytes 1572864 | tf_op jit(solution)/shard_map/reshape | solution.py:386
  9.8 76.8 %shard_map.64 = (bf16[512,6144]{1,0:T(8,128)(2,1)}, s32[2,2,256]{2,1,0:T(2,128)}, s32[2,1]{1,0:T(2,128)}) custom-call(bf16[32,2,6144]{2,1,0:T(2,128)(2,1)} %copy.15.pieces_ref, s32[2,256]{1,0:T(2,128)} %rows_ref.1, s32[1]{0:T(128)S(6)} %copy.21.count_ref), custom_call_target="tpu_custom_call" | custom-call | tf_op jit(solution)/shard_map/pallas_call | solution.py:314
  86.6 29.3 %shard_map.65.part_ref = f32[2,9,144,256]{3,2,1,0:T(8,128)} custom-call(s32[2,1]{1,0:T(2,128)} %get-tuple-element.8.counts_ref, s32[1]{0:T(128)} %bitcast.4.core_ref, s32[2,2,256]{2,1,0:T(2,128)} %get-tuple-element.9.pairs_ref, bf16[512,6144]{1,0:T(8,128)(2,1)} %get-tuple-element.10.panel_ref, bf16[144,4096]{1,0:T(8,128)(2,1)} %constant.46.clone.lag_ref), custom_call_target="tpu_custom_call" | custom-call | flops 9160359936 | bytes 8945664 | tf_op jit(solution)/shard_map/pallas_call | solution.py:143
  116.0 5.0 %shard_map.66 = bf16[9,144,256]{2,1,0:T(8,128)(2,1)} custom-call(f32[2,9,144,256]{3,2,1,0:T(8,128)} %shard_map.65.part_ref), custom_call_target="tpu_custom_call" | custom-call | tf_op jit(solution)/shard_map/pallas_call | solution.py:355
  121.0 1.9 %slice_bitcast_fusion = bf16[129,9,256]{2,0,1:T(8,128)(2,1)} fusion(bf16[9,144,256]{2,1,0:T(8,128)(2,1)} %shard_map.66), kind=kLoop, calls=%fused_computation.6 | loop fusion | bytes 1188864 | tf_op jit(solution)/shard_map/transpose | solution.py:395
  (3 shorter events, 0.0 us)
Async XLA Ops:
  0.0 4.6 %copy-start = (f32[16,3,2,2048]{3,2,1,0:T(2,128)S(1)}, f32[16,3,2,2048]{3,2,1,0:T(2,128)}, u32[]{:S(2)}) copy-start(f32[16,3,2,2048]{3,2,1,0:T(2,128)} %param.6) | copy-start | bytes 2359300

commit v18 on v17

--- a/solution.py
+++ b/solution.py
@@ -48,20 +48,38 @@
     return jnp.asarray(both.reshape(LAG_ROWS, 2 * bin_count))
 
 
-def pair_kernel(counts_ref, core_ref, pairs_ref, panel_ref, lag_ref, *rest,
+def pair_kernel(counts_ref, core_ref, pairs_ref, panel_hbm, lag_ref, *rest,
                 blocks_per_owner, part_bins, accumulate):
     if accumulate:
-        acc_ref, out_ref, f_scr, s_scr = rest
+        acc_ref, out_ref, f_scr, s_scr, panel_ref, panel_sems = rest
     else:
-        out_ref, f_scr, s_scr = rest
+        out_ref, f_scr, s_scr, panel_ref, panel_sems = rest
     step = pl.program_id(0)
     owner = step // blocks_per_owner
     start = (step % blocks_per_owner) * PAIR_BLOCK
     live = start < counts_ref[owner, 0]
+    load_chunk = min(GATHER_CHUNK, panel_ref.shape[1])
+    load_count = panel_ref.shape[1] // load_chunk
+
+    def panel_copy(c):
+        cols = pl.ds(c * load_chunk, load_chunk)
+        return pltpu.make_async_copy(panel_hbm.at[:, cols], panel_ref.at[:, cols],
+                                     panel_sems.at[c])
+
+    @pl.when(step == 0)
+    def _():
+        for c in range(load_count):
+            panel_copy(c).start()
+
     if accumulate:
         out_ref[...] = acc_ref[...]
     else:
         out_ref[...] = jnp.zeros_like(out_ref)
+
+    @pl.when(jnp.logical_and(step == 0, jnp.logical_not(live)))
+    def _():
+        for c in range(load_count):
+            panel_copy(c).wait()
 
     @pl.when(live)
     def _():
@@ -75,6 +93,10 @@
         gather_chunk = min(GATHER_CHUNK, width)
 
         def gather(c, carry):
+            @pl.when(step == 0)
+            def _():
+                panel_copy(c).wait()
+
             off = pl.multiple_of(c * gather_chunk, gather_chunk)
             block = panel_ref[:, pl.ds(off, gather_chunk)]
             both = jnp.dot(pick, block, preferred_element_type=jnp.float32)
@@ -131,7 +153,7 @@
     in_specs = [
         pl.BlockSpec((1, 2, PAIR_BLOCK),
                      lambda i, c, k: (i // blocks_per_owner, 0, i % blocks_per_owner)),
-        pl.BlockSpec((rows, width), lambda i, c, k: (0, 0)),
+        pl.BlockSpec(memory_space=pl.ANY),
         pl.BlockSpec((LAG_ROWS, 2 * part_bins), lambda i, c, k: (0, k[0])),
     ]
     args = [counts, core_arr, chip_pairs, panel, lag_rows]
@@ -151,6 +173,8 @@
             scratch_shapes=[
                 pltpu.VMEM((PAIR_BLOCK, width), jnp.float32),
                 pltpu.VMEM((PAIR_BLOCK, width), jnp.float32),
+                pltpu.VMEM((rows, width), panel.dtype),
+                pltpu.SemaphoreType.DMA((width // min(GATHER_CHUNK, width),)),
             ],
         ),
         input_output_aliases=aliases,

time: 123 us -> 119 us (0.967)
  the two profiles are of different devices: /device:TPU:105 before, /device:TPU:9 now
where the time goes in v18:
time: 119 us
  Pallas kernels  107 us (90%)
  local copies, waits for them, and re-layouts  7.68 us (6%)
  other arithmetic  3.25 us (3%)
    pallas_call x1, Pallas kernels, spread(): pl.pallas_call(kernel, out_shape=(jax.ShapeDtypeStruct((rows, width), pie...  79.5 us
    pallas_call x1, Pallas kernels, pair_sums(): pl.pallas_call(kernel, out_shape=jax.ShapeDtypeStruct((owners, 9, LAG_ROW...  22.7 us
    pallas_call x1, Pallas kernels, exchange(): pl.pallas_call(functools.partial(exchange_kernel, scale=scale), out_shape...  5.19 us
    reshape x2, local copies, waits for them, and re-layouts, shards(): jnp.transpose(pieces, (3, 0, 1, 4, 2, 5))  2.63 us

profile of v18, /device:TPU:9, one launch (start us, length us, event | category | flops | bytes accessed | tf_op | source)
XLA Modules:
  0.0 119.2 jit_solution(2622798730454173557)
XLA Ops:
  0.0 0.0 copy-start
  0.7 0.7 compare_and_fusion
  1.4 0.8 copy.13
  2.2 0.1 reshape_squeeze.6
  2.3 0.1 subtract_select_fusion
  2.3 1.7 %multiply_reduce_fusion = f32[16,2048]{1,0:T(8,128)S(1)} fusion(f32[16,3,2,2048]{3,2,1,0:T(2,128)} %param.6), kind=kLoop, calls=%fused_computation.5 | loop fusion | flops 360448 | bytes 917504 | tf_op jit(solution)/shard_map/reduce_sum | solution.py:31
  4.0 0.1 reduce_sum.14
  4.2 0.1 reduce_sum.18
  4.3 0.1 broadcast_in_dim.36
  4.4 0.1 mul.36
  4.6 0.0 copy-done
  4.6 0.4 multiply_convert_fusion
  4.9 0.3 reshape.91
  5.2 1.0 gather_fusion
  6.3 0.6 gather.7
  6.9 0.3 fusion.1
  7.2 0.9 reshape.92
  8.1 1.7 %copy.15.pieces_ref = bf16[32,2,6144]{2,1,0:T(2,128)(2,1)} copy(bf16[32,2,6144]{2,0,1:T(8,128)(2,1)S(1)} %reshape.92) | data formatting | bytes 1572864 | tf_op jit(solution)/shard_map/reshape | solution.py:410
  9.8 79.5 %shard_map.64 = (bf16[512,6144]{1,0:T(8,128)(2,1)}, s32[2,2,256]{2,1,0:T(2,128)}, s32[2,1]{1,0:T(2,128)}) custom-call(bf16[32,2,6144]{2,1,0:T(2,128)(2,1)} %copy.15.pieces_ref, s32[2,256]{1,0:T(2,128)} %rows_ref.1, s32[1]{0:T(128)S(6)} %copy.21.count_ref), custom_call_target="tpu_custom_call" | custom-call | tf_op jit(solution)/shard_map/pallas_call | solution.py:338
  89.3 22.7 %shard_map.65.part_ref = f32[2,9,144,256]{3,2,1,0:T(8,128)} custom-call(s32[2,1]{1,0:T(2,128)} %get-tuple-element.8.counts_ref, s32[1]{0:T(128)} %bitcast.4.core_ref, s32[2,2,256]{2,1,0:T(2,128)} %get-tuple-element.9.pairs_ref, bf16[512,6144]{1,0:T(8,128)(2,1)} %get-tuple-element.10.panel_hbm, bf16[144,4096]{1,0:T(8,128)(2,1)} %constant.46.clone.lag_ref), custom_call_target="tpu_custom_call" | custom-call | flops 9160359936 | bytes 8945664 | tf_op jit(solution)/shard_map/pallas_call | solution.py:165
  112.0 5.2 %shard_map.66 = bf16[9,144,256]{2,1,0:T(8,128)(2,1)} custom-call(f32[2,9,144,256]{3,2,1,0:T(8,128)} %shard_map.65.part_ref), custom_call_target="tpu_custom_call" | custom-call | tf_op jit(solution)/shard_map/pallas_call | solution.py:379
  117.2 1.9 %slice_bitcast_fusion = bf16[129,9,256]{2,0,1:T(8,128)(2,1)} fusion(bf16[9,144,256]{2,1,0:T(8,128)(2,1)} %shard_map.66), kind=kLoop, calls=%fused_computation.6 | loop fusion | bytes 1188864 | tf_op jit(solution)/shard_map/transpose | solution.py:419
  (3 shorter events, 0.0 us)
Async XLA Ops:
  0.0 4.6 %copy-start = (f32[16,3,2,2048]{3,2,1,0:T(2,128)S(1)}, f32[16,3,2,2048]{3,2,1,0:T(2,128)}, u32[]{:S(2)}) copy-start(f32[16,3,2,2048]{3,2,1,0:T(2,128)} %param.6) | copy-start | bytes 2359300

commit v19 on v17

--- a/solution.py
+++ b/solution.py
@@ -12,7 +12,7 @@
 from jax.sharding import PartitionSpec as P
 
 LAGS = 129
-LAG_ROWS = 144
+LAG_ROWS = 136
 PAIR_BLOCK = 128
 BIN_CHUNK = 256
 GATHER_CHUNK = 512

time: 123 us -> 119 us (0.967)
  the two profiles are of different devices: /device:TPU:105 before, /device:TPU:15 now
where the time goes in v19:
time: 119 us
  Pallas kernels  107 us (90%)
  local copies, waits for them, and re-layouts  7.67 us (6%)
  other arithmetic  3.25 us (3%)
    pallas_call x1, Pallas kernels, spread(): pl.pallas_call(kernel, out_shape=(jax.ShapeDtypeStruct((rows, width), pie...  79 us
    pallas_call x1, Pallas kernels, pair_sums(): pl.pallas_call(kernel, out_shape=jax.ShapeDtypeStruct((owners, 9, LAG_ROW...  23.4 us
    pallas_call x1, Pallas kernels, exchange(): pl.pallas_call(functools.partial(exchange_kernel, scale=scale), out_shape...  4.77 us
    reshape x2, local copies, waits for them, and re-layouts, shards(): jnp.transpose(pieces, (3, 0, 1, 4, 2, 5))  2.63 us

profile of v19, /device:TPU:15, one launch (start us, length us, event | category | flops | bytes accessed | tf_op | source)
XLA Modules:
  0.0 118.9 jit_solution(13072092132156766627)
XLA Ops:
  0.0 0.0 copy-start
  0.7 0.7 compare_and_fusion
  1.4 0.8 copy.13
  2.2 0.1 reshape_squeeze.6
  2.3 0.1 subtract_select_fusion
  2.3 1.7 %multiply_reduce_fusion = f32[16,2048]{1,0:T(8,128)S(1)} fusion(f32[16,3,2,2048]{3,2,1,0:T(2,128)} %param.6), kind=kLoop, calls=%fused_computation.5 | loop fusion | flops 360448 | bytes 917504 | tf_op jit(solution)/shard_map/reduce_sum | solution.py:31
  4.0 0.1 reduce_sum.14
  4.2 0.1 reduce_sum.18
  4.3 0.1 broadcast_in_dim.36
  4.4 0.1 mul.36
  4.6 0.0 copy-done
  4.6 0.4 multiply_convert_fusion
  4.9 0.3 reshape.91
  5.2 1.0 gather_fusion
  6.3 0.6 gather.7
  6.9 0.3 fusion.1
  7.2 0.9 reshape.92
  8.1 1.7 %copy.15.pieces_ref = bf16[32,2,6144]{2,1,0:T(2,128)(2,1)} copy(bf16[32,2,6144]{2,0,1:T(8,128)(2,1)S(1)} %reshape.92) | data formatting | bytes 1572864 | tf_op jit(solution)/shard_map/reshape | solution.py:386
  9.8 79.0 %shard_map.64 = (bf16[512,6144]{1,0:T(8,128)(2,1)}, s32[2,2,256]{2,1,0:T(2,128)}, s32[2,1]{1,0:T(2,128)}) custom-call(bf16[32,2,6144]{2,1,0:T(2,128)(2,1)} %copy.15.pieces_ref, s32[2,256]{1,0:T(2,128)} %rows_ref.1, s32[1]{0:T(128)S(6)} %copy.21.count_ref), custom_call_target="tpu_custom_call" | custom-call | tf_op jit(solution)/shard_map/pallas_call | solution.py:314
  88.8 23.4 %shard_map.65.part_ref = f32[2,9,136,256]{3,2,1,0:T(8,128)} custom-call(s32[2,1]{1,0:T(2,128)} %get-tuple-element.8.counts_ref, s32[1]{0:T(128)} %bitcast.4.core_ref, s32[2,2,256]{2,1,0:T(2,128)} %get-tuple-element.9.pairs_ref, bf16[512,6144]{1,0:T(8,128)(2,1)} %get-tuple-element.10.panel_ref, bf16[136,4096]{1,0:T(8,128)(2,1)} %constant.46.clone.lag_ref), custom_call_target="tpu_custom_call" | custom-call | flops 9009364992 | bytes 8798208 | tf_op jit(solution)/shard_map/pallas_call | solution.py:143
  112.2 4.8 %shard_map.66 = bf16[9,136,256]{2,1,0:T(8,128)(2,1)} custom-call(f32[2,9,136,256]{3,2,1,0:T(8,128)} %shard_map.65.part_ref), custom_call_target="tpu_custom_call" | custom-call | tf_op jit(solution)/shard_map/pallas_call | solution.py:355
  116.9 1.9 %slice_bitcast_fusion = bf16[129,9,256]{2,0,1:T(8,128)(2,1)} fusion(bf16[9,136,256]{2,1,0:T(8,128)(2,1)} %shard_map.66), kind=kLoop, calls=%fused_computation.6 | loop fusion | bytes 1188864 | tf_op jit(solution)/shard_map/transpose | solution.py:395
  (3 shorter events, 0.0 us)
Async XLA Ops:
  0.0 4.6 %copy-start = (f32[16,3,2,2048]{3,2,1,0:T(2,128)S(1)}, f32[16,3,2,2048]{3,2,1,0:T(2,128)}, u32[]{:S(2)}) copy-start(f32[16,3,2,2048]{3,2,1,0:T(2,128)} %param.6) | copy-start | bytes 2359300

commit v20 on v17

--- a/solution.py
+++ b/solution.py
@@ -281,6 +281,7 @@
 
     for sub in range(subs):
         scatter(sub)
+    for sub in range(subs):
         gathered(sub)
         ring_step(0, sub)
     for s in range(1, half):

time: 123 us -> 120 us (0.976)
  the two profiles are of different devices: /device:TPU:105 before, /device:TPU:3 now
where the time goes in v20:
time: 120 us
  Pallas kernels  108 us (90%)
  local copies, waits for them, and re-layouts  7.68 us (6%)
  other arithmetic  3.25 us (3%)
    pallas_call x1, Pallas kernels, spread(): pl.pallas_call(kernel, out_shape=(jax.ShapeDtypeStruct((rows, width), pie...  76.8 us
    pallas_call x1, Pallas kernels, pair_sums(): pl.pallas_call(kernel, out_shape=jax.ShapeDtypeStruct((owners, 9, LAG_ROW...  24 us
    pallas_call x1, Pallas kernels, exchange(): pl.pallas_call(functools.partial(exchange_kernel, scale=scale), out_shape...  7.16 us
    reshape x2, local copies, waits for them, and re-layouts, shards(): jnp.transpose(pieces, (3, 0, 1, 4, 2, 5))  2.63 us

profile of v20, /device:TPU:3, one launch (start us, length us, event | category | flops | bytes accessed | tf_op | source)
XLA Modules:
  0.0 119.7 jit_solution(15453859455402318931)
XLA Ops:
  0.0 0.0 copy-start
  0.7 0.7 compare_and_fusion
  1.4 0.8 copy.13
  2.2 0.1 reshape_squeeze.6
  2.3 0.1 subtract_select_fusion
  2.3 1.7 %multiply_reduce_fusion = f32[16,2048]{1,0:T(8,128)S(1)} fusion(f32[16,3,2,2048]{3,2,1,0:T(2,128)} %param.6), kind=kLoop, calls=%fused_computation.5 | loop fusion | flops 360448 | bytes 917504 | tf_op jit(solution)/shard_map/reduce_sum | solution.py:31
  4.0 0.1 reduce_sum.14
  4.2 0.1 reduce_sum.18
  4.3 0.1 broadcast_in_dim.36
  4.4 0.1 mul.36
  4.6 0.0 copy-done
  4.6 0.4 multiply_convert_fusion
  4.9 0.3 reshape.91
  5.2 1.0 gather_fusion
  6.3 0.6 gather.7
  6.9 0.3 fusion.1
  7.2 0.9 reshape.92
  8.1 1.7 %copy.15.pieces_ref = bf16[32,2,6144]{2,1,0:T(2,128)(2,1)} copy(bf16[32,2,6144]{2,0,1:T(8,128)(2,1)S(1)} %reshape.92) | data formatting | bytes 1572864 | tf_op jit(solution)/shard_map/reshape | solution.py:387
  9.8 76.8 %shard_map.64 = (bf16[512,6144]{1,0:T(8,128)(2,1)}, s32[2,2,256]{2,1,0:T(2,128)}, s32[2,1]{1,0:T(2,128)}) custom-call(bf16[32,2,6144]{2,1,0:T(2,128)(2,1)} %copy.15.pieces_ref, s32[2,256]{1,0:T(2,128)} %rows_ref.1, s32[1]{0:T(128)S(6)} %copy.21.count_ref), custom_call_target="tpu_custom_call" | custom-call | tf_op jit(solution)/shard_map/pallas_call | solution.py:315
  86.6 24.0 %shard_map.65.part_ref = f32[2,9,144,256]{3,2,1,0:T(8,128)} custom-call(s32[2,1]{1,0:T(2,128)} %get-tuple-element.8.counts_ref, s32[1]{0:T(128)} %bitcast.4.core_ref, s32[2,2,256]{2,1,0:T(2,128)} %get-tuple-element.9.pairs_ref, bf16[512,6144]{1,0:T(8,128)(2,1)} %get-tuple-element.10.panel_ref, bf16[144,4096]{1,0:T(8,128)(2,1)} %constant.46.clone.lag_ref), custom_call_target="tpu_custom_call" | custom-call | flops 9160359936 | bytes 8945664 | tf_op jit(solution)/shard_map/pallas_call | solution.py:143
  110.6 7.2 %shard_map.66 = bf16[9,144,256]{2,1,0:T(8,128)(2,1)} custom-call(f32[2,9,144,256]{3,2,1,0:T(8,128)} %shard_map.65.part_ref), custom_call_target="tpu_custom_call" | custom-call | tf_op jit(solution)/shard_map/pallas_call | solution.py:356
  117.7 1.9 %slice_bitcast_fusion = bf16[129,9,256]{2,0,1:T(8,128)(2,1)} fusion(bf16[9,144,256]{2,1,0:T(8,128)(2,1)} %shard_map.66), kind=kLoop, calls=%fused_computation.6 | loop fusion | bytes 1188864 | tf_op jit(solution)/shard_map/transpose | solution.py:396
  (3 shorter events, 0.0 us)
Async XLA Ops:
  0.0 4.6 %copy-start = (f32[16,3,2,2048]{3,2,1,0:T(2,128)S(1)}, f32[16,3,2,2048]{3,2,1,0:T(2,128)}, u32[]{:S(2)}) copy-start(f32[16,3,2,2048]{3,2,1,0:T(2,128)} %param.6) | copy-start | bytes 2359300

commit v21 on v17

--- a/solution.py
+++ b/solution.py
@@ -15,7 +15,7 @@
 LAG_ROWS = 144
 PAIR_BLOCK = 128
 BIN_CHUNK = 256
-GATHER_CHUNK = 512
+GATHER_CHUNK = 1024
 SUBS = 2
 
 

time: 123 us -> 118 us (0.959)
  the two profiles are of different devices: /device:TPU:105 before, /device:TPU:1 now
where the time goes in v21:
time: 118 us
  Pallas kernels  106 us (90%)
  local copies, waits for them, and re-layouts  7.68 us (7%)
  other arithmetic  3.25 us (3%)
    pallas_call x1, Pallas kernels, spread(): pl.pallas_call(kernel, out_shape=(jax.ShapeDtypeStruct((rows, width), pie...  79.8 us
    pallas_call x1, Pallas kernels, pair_sums(): pl.pallas_call(kernel, out_shape=jax.ShapeDtypeStruct((owners, 9, LAG_ROW...  20.4 us
    pallas_call x1, Pallas kernels, exchange(): pl.pallas_call(functools.partial(exchange_kernel, scale=scale), out_shape...  5.88 us
    reshape x2, local copies, waits for them, and re-layouts, shards(): jnp.transpose(pieces, (3, 0, 1, 4, 2, 5))  2.63 us

profile of v21, /device:TPU:1, one launch (start us, length us, event | category | flops | bytes accessed | tf_op | source)
XLA Modules:
  0.0 117.8 jit_solution(14353480818148729085)
XLA Ops:
  0.0 0.0 copy-start
  0.7 0.7 compare_and_fusion
  1.4 0.8 copy.13
  2.2 0.1 reshape_squeeze.6
  2.3 0.1 subtract_select_fusion
  2.3 1.7 %multiply_reduce_fusion = f32[16,2048]{1,0:T(8,128)S(1)} fusion(f32[16,3,2,2048]{3,2,1,0:T(2,128)} %param.6), kind=kLoop, calls=%fused_computation.5 | loop fusion | flops 360448 | bytes 917504 | tf_op jit(solution)/shard_map/reduce_sum | solution.py:31
  4.0 0.1 reduce_sum.14
  4.2 0.1 reduce_sum.18
  4.3 0.1 broadcast_in_dim.36
  4.4 0.1 mul.36
  4.6 0.0 copy-done
  4.6 0.4 multiply_convert_fusion
  4.9 0.3 reshape.91
  5.2 1.0 gather_fusion
  6.3 0.6 gather.7
  6.9 0.3 fusion.1
  7.2 0.9 reshape.92
  8.1 1.7 %copy.15.pieces_ref = bf16[32,2,6144]{2,1,0:T(2,128)(2,1)} copy(bf16[32,2,6144]{2,0,1:T(8,128)(2,1)S(1)} %reshape.92) | data formatting | bytes 1572864 | tf_op jit(solution)/shard_map/reshape | solution.py:386
  9.8 79.8 %shard_map.64 = (bf16[512,6144]{1,0:T(8,128)(2,1)}, s32[2,2,256]{2,1,0:T(2,128)}, s32[2,1]{1,0:T(2,128)}) custom-call(bf16[32,2,6144]{2,1,0:T(2,128)(2,1)} %copy.15.pieces_ref, s32[2,256]{1,0:T(2,128)} %rows_ref.1, s32[1]{0:T(128)S(6)} %copy.21.count_ref), custom_call_target="tpu_custom_call" | custom-call | tf_op jit(solution)/shard_map/pallas_call | solution.py:314
  89.6 20.4 %shard_map.65.part_ref = f32[2,9,144,256]{3,2,1,0:T(8,128)} custom-call(s32[2,1]{1,0:T(2,128)} %get-tuple-element.8.counts_ref, s32[1]{0:T(128)} %bitcast.4.core_ref, s32[2,2,256]{2,1,0:T(2,128)} %get-tuple-element.9.pairs_ref, bf16[512,6144]{1,0:T(8,128)(2,1)} %get-tuple-element.10.panel_ref, bf16[144,4096]{1,0:T(8,128)(2,1)} %constant.46.clone.lag_ref), custom_call_target="tpu_custom_call" | custom-call | flops 9160359936 | bytes 8945664 | tf_op jit(solution)/shard_map/pallas_call | solution.py:143
  110.0 5.9 %shard_map.66 = bf16[9,144,256]{2,1,0:T(8,128)(2,1)} custom-call(f32[2,9,144,256]{3,2,1,0:T(8,128)} %shard_map.65.part_ref), custom_call_target="tpu_custom_call" | custom-call | tf_op jit(solution)/shard_map/pallas_call | solution.py:355
  115.9 1.9 %slice_bitcast_fusion = bf16[129,9,256]{2,0,1:T(8,128)(2,1)} fusion(bf16[9,144,256]{2,1,0:T(8,128)(2,1)} %shard_map.66), kind=kLoop, calls=%fused_computation.6 | loop fusion | bytes 1188864 | tf_op jit(solution)/shard_map/transpose | solution.py:395
  (3 shorter events, 0.0 us)
Async XLA Ops:
  0.0 4.6 %copy-start = (f32[16,3,2,2048]{3,2,1,0:T(2,128)S(1)}, f32[16,3,2,2048]{3,2,1,0:T(2,128)}, u32[]{:S(2)}) copy-start(f32[16,3,2,2048]{3,2,1,0:T(2,128)} %param.6) | copy-start | bytes 2359300
